TPU v7x, 512 devices: a whole 4x4x16 slice. The times are simulated.
512 devices in a mesh: tile: 32 (over y, x, core), fsdp: 16 (over z).
Axes of the slice: x: 4, y: 4, z: 16, core: 2. Of those that a mesh axis runs over, the one named last changes fastest.
Arguments:
- images: bfloat16 [16, 32, 8, 128, 320], P('fsdp', 'tile'), may hold values from -80 to 80
- tile_rows: int32 [16, 32], P('fsdp', 'tile'), may hold values from 1 to 8, 160 in all within a row
- cotangent: bfloat16 [16, 32, 8, 128, 320], P('fsdp', 'tile'), may hold values from -6 to 6
- master_weight: float32 [2880, 320], P('fsdp'), may hold values from -0.109375 to 0.109375
- norm_gain: float32 [320], replicated, may hold values from 0.5 to 1.5
- norm_bias: float32 [320], replicated, may hold values from -3 to 3
- first_moment: float32 [2880, 320], P('fsdp'), may hold values from -6 to 6
- second_moment: float32 [2880, 320], P('fsdp'), may hold values from 0.5 to 4
Outputs:
- activation: bfloat16 [16, 32, 8, 128, 320], P('fsdp', 'tile')
- image_grad: bfloat16 [16, 32, 8, 128, 320], P('fsdp', 'tile')
- weight_grad: float32 [2880, 320], P('fsdp')
- new_weight: float32 [2880, 320], P('fsdp')
- new_first: float32 [2880, 320], P('fsdp')
- new_second: float32 [2880, 320], P('fsdp')
- gain_grad: float32 [320], replicated
- bias_grad: float32 [320], replicated
Inputs may be any that keep to these rules, and one draw needn't show every extreme that they name: `tile_rows`: in each frame the 32 counts sum to 160 and the largest is exactly 8.
All inputs are finite; a program needn't handle non-finite values. No bound on the sum of `tile_rows` on one device may be relied on, other than what follows from the above.
Results may differ from a plain program's by a relative error of at most 0.027.
Values may be sent and summed in bfloat16 or wider, within the bound.
No kernel may reach another device: no remote copies, remote signals or barrier semaphores. Data moves between devices by JAX's collectives and lax.ppermute only.
A program may use at most 64 MiB of HBM per device.

v0:
```python
import jax
import jax.numpy as jnp
from jax import lax
from jax.sharding import PartitionSpec as P

GROUPS = 32
ROWS_MEAN = 5


def extended(cells, sides, width):
    for axis, dim in sides:
        count = lax.axis_size(axis)
        ends = count - 1
        head = lax.slice_in_dim(cells, 0, width, axis=dim)
        tail = lax.slice_in_dim(cells, cells.shape[dim] - width, cells.shape[dim], axis=dim)
        cells = jnp.concatenate(
            [
                lax.ppermute(tail, axis, [(i, (i + 1) % count) for i in range(ends)]),
                cells,
                lax.ppermute(head, axis, [((i + 1) % count, i) for i in range(ends)]),
            ],
            axis=dim,
        )
    return cells


def edge_pair(source, live_count):
    first_row = source[0:1]
    last_row = lax.dynamic_slice_in_dim(source, live_count - 1, 1, 0)
    return jnp.concatenate([first_row, last_row], axis=0)


def framed(source, beside_all, live_count):
    slot_count = source.shape[0]
    zero_row = jnp.zeros_like(source[0:1])
    stacked = jnp.concatenate([beside_all[0:1], source, zero_row], axis=0)
    marker = (jnp.arange(slot_count + 2) == live_count + 1)[:, None, None]
    stacked = jnp.where(marker, beside_all[3:4], stacked)
    return jnp.pad(stacked, ((0, 0), (1, 1), (0, 0)))


def patches_of(padded, slot_count, cell_cols):
    pieces = [
        padded[row_step : row_step + slot_count, col_step : col_step + cell_cols, :]
        for row_step in range(3)
        for col_step in range(3)
    ]
    return jnp.concatenate(pieces, axis=-1).reshape(slot_count * cell_cols, -1)


def local(
    images, tile_rows, cotangent, master_weight, norm_gain, norm_bias, first_moment, second_moment
):
    slot_count, cell_cols, channels = (images.shape[2], images.shape[3], images.shape[4])
    per_group = channels // GROUPS
    tile_count = lax.axis_size("tile")
    shards = lax.axis_size("fsdp")
    population = jnp.float32(ROWS_MEAN * tile_count * cell_cols * per_group)
    live_count = tile_rows[0, 0]
    live_rows = jnp.arange(slot_count) < live_count
    cell_mask = jnp.repeat(live_rows, cell_cols).astype(jnp.float32)[:, None]

    def grouped(values):
        return jnp.sum(values.reshape(-1, GROUPS, per_group), axis=(0, 2))

    def spread(stat):
        return jnp.repeat(stat, per_group)

    source = jnp.where(live_rows[:, None, None], images[0, 0], jnp.zeros((), jnp.bfloat16))
    beside_all = extended(edge_pair(source, live_count), (("tile", 0),), 1)
    columns = patches_of(framed(source, beside_all, live_count), slot_count, cell_cols)
    gathered = lax.all_gather(master_weight.astype(jnp.bfloat16), "fsdp", axis=0, tiled=True)
    mixed = jnp.dot(columns, gathered, preferred_element_type=jnp.float32)
    group_mean = lax.psum(grouped(mixed * cell_mask), "tile") / population
    centered = (mixed - spread(group_mean)) * cell_mask
    variance = lax.psum(grouped(centered * centered), "tile") / population
    inverse = lax.rsqrt(variance + 1e-05)
    normed = (mixed - spread(group_mean)) * spread(inverse)
    shifted = normed * norm_gain + norm_bias
    gate_value = jax.nn.sigmoid(shifted)
    activation = (shifted * gate_value * cell_mask).astype(jnp.bfloat16).reshape(images.shape)
    upstream = cotangent[0, 0].reshape(-1, channels).astype(jnp.float32) * cell_mask
    dshift = upstream * gate_value * (1.0 + shifted * (1.0 - gate_value))
    scaled = dshift * norm_gain
    delta_sum, cross_sum = lax.psum((grouped(scaled), grouped(scaled * normed)), "tile")
    gain_total, bias_total = lax.psum(
        (jnp.sum(dshift * normed, axis=0), jnp.sum(dshift, axis=0)), ("tile", "fsdp")
    )
    norm_scale = jnp.float32(shards * ROWS_MEAN * tile_count * cell_cols) ** (-0.5)
    pre_grad = spread(inverse) * (
        scaled - spread(delta_sum / population) - normed * spread(cross_sum / population)
    )
    pre_grad = (pre_grad * cell_mask).astype(jnp.bfloat16)
    grad_field = pre_grad.reshape(slot_count, cell_cols, channels)
    grad_around = extended(edge_pair(grad_field, live_count), (("tile", 0),), 1)
    grad_columns = patches_of(framed(grad_field, grad_around, live_count), slot_count, cell_cols)
    flipped = (
        gathered.reshape(9, channels, channels)[::-1]
        .transpose(0, 2, 1)
        .reshape(9 * channels, channels)
    )
    image_grad = (
        (jnp.dot(grad_columns, flipped, preferred_element_type=jnp.float32) * cell_mask)
        .astype(jnp.bfloat16)
        .reshape(images.shape)
    )
    full_grad = lax.psum(
        lax.dot_general(
            columns, pre_grad, (((0,), (0,)), ((), ())), preferred_element_type=jnp.float32
        ).astype(jnp.bfloat16),
        "tile",
    )
    grad_shard = lax.psum_scatter(full_grad, "fsdp", scatter_dimension=0, tiled=True).astype(
        jnp.float32
    )
    weight_grad = grad_shard * norm_scale
    new_first = 0.9 * first_moment + 0.1 * weight_grad
    new_second = 0.999 * second_moment + 0.001 * weight_grad * weight_grad
    first_fix = new_first / (1.0 - 0.9**10)
    second_fix = new_second / (1.0 - 0.999**10)
    new_weight = master_weight - 0.01 * first_fix / (jnp.sqrt(second_fix) + 1e-08)
    return (
        activation,
        image_grad,
        weight_grad,
        new_weight,
        new_first,
        new_second,
        gain_total * norm_scale,
        bias_total * norm_scale,
    )


def solution(mesh):
    placed = (
        P("fsdp", "tile", None, None, None),
        P("fsdp", "tile"),
        P("fsdp", "tile", None, None, None),
        P("fsdp", None),
        P(),
        P(),
        P("fsdp", None),
        P("fsdp", None),
    )
    return jax.shard_map(
        local,
        mesh=mesh,
        in_specs=placed,
        out_specs=(
            P("fsdp", "tile", None, None, None),
            P("fsdp", "tile", None, None, None),
            P("fsdp", None),
            P("fsdp", None),
            P("fsdp", None),
            P("fsdp", None),
            P(),
            P(),
        ),
        check_vma=False,
    )
```

profile of v0, /device:TPU:1, one launch (start us, length us, event | category | flops | bytes accessed | tf_op | source)
XLA Modules:
  0.0 609.0 jit_solution(12582963821743056391)
XLA Ops:
  7.2 1.7 convert_bitcast_fusion
  9.7 1.2 bitcast_select_fusion
  10.9 8.8 %collective-permute-start = (bf16[1,128,320]{1,2,0:T(8,128)(2,1)S(1)}, bf16[1,128,320]{1,2,0:T(8,128)(2,1)S(1)}, u32[]{:S(2)}, u32[]{:S(2)}) collective-permute-start(bf16[1,128,320]{1,2,0:T(8,128)(2,1)S(1)} %get-tuple-element.46), channel_id=1, source_target_pairs={{16,0},{32,16},{48,32},{64,48},{80,64},{96,80},{112,96},{128,112},... | collective-permute-start | bytes 245768 | tf_op jit(solution)/shard_map/ppermute | solution.py:20
  19.7 1.9 collective-permute-start.1
  21.6 1.5 copy.30
  23.2 1.3 dynamic-slice.4
  25.4 1.1 fusion.5
  26.5 1.0 slice_dynamic-update-slice_fusion.5
  27.5 1.1 fusion.6
  28.6 1.1 fusion.7
  29.7 1.0 slice_dynamic-update-slice_fusion.4
  30.7 1.1 fusion.8
  31.8 1.1 fusion.9
  32.9 1.0 slice_dynamic-update-slice_fusion.3
  33.8 1.1 fusion.10
  34.9 8.4 %copy.29 = bf16[8,128,2880]{2,1,0:T(8,128)(2,1)} copy(bf16[8,128,2880]{1,2,0:T(8,128)(2,1)} %fusion.10) | data formatting | bytes 11796480 | tf_op jit(solution)/shard_map/concatenate | solution.py:48
  43.4 37.7 %all-gather.3.cloned.1.call-done = bf16[16,180,320]{2,1,0:T(8,128)(2,1)} async-done(((bf16[1,180,320]{2,1,0:T(8,128)(2,1)}), bf16[16,180,320]{2,1,0:T(8,128)(2,1)}) %all-gather.3.cloned.1.call-update) | async-done | bytes 1843216 | tf_op jit(solution)/shard_map/all_gather | solution.py:72
  81.1 2.8 reshape.78
  83.8 5.1 multiply_reduce_fusion.3
  89.1 71.5 %psum.49 = f32[32]{0:T(128)S(1)} all-reduce(f32[32]{0:T(128)S(1)} %reduce_sum.67), channel_id=1, replica_groups=mesh['tile'=32,'fsdp'=16] {'tile'}, use_global_device_ids=true, to_apply=%region_2.3 | all-reduce | flops 32 | bytes 256 | tf_op jit(solution)/shard_map/psum | solution.py:74
  161.4 62.7 %psum.50 = f32[32]{0:T(128)S(1)} all-reduce(f32[32]{0:T(128)S(1)} %reduce_sum.73), channel_id=1, replica_groups=mesh['tile'=32,'fsdp'=16] {'tile'}, use_global_device_ids=true, to_apply=%region_5.6 | all-reduce | flops 32 | bytes 256 | tf_op jit(solution)/shard_map/psum | solution.py:76
  224.3 3.5 multiply_reduce_fusion
  228.2 62.9 %all-reduce.5 = (f32[32]{0:T(128)S(1)}, f32[32]{0:T(128)S(1)}) all-reduce(f32[32]{0:T(128)S(1)} %reduce_sum.93, f32[32]{0:T(128)S(1)} %reduce_sum.90), channel_id=1, replica_groups=mesh['tile'=32,'fsdp'=16] {'tile'}, use_global_device_ids=true, to_apply=%region_11.12 | all-reduce | flops 64 | bytes 512 | tf_op jit(solution)/shard_map/psum | solution.py:85
  292.3 7.4 %convolution_convert_fusion = bf16[2880,320]{1,0:T(8,128)(2,1)} fusion(bf16[1024,2880]{1,0:T(8,128)(2,1)} %bitcast.60, bf16[1024,320]{0,1:T(8,128)(2,1)S(1)} %multiply_convert_fusion), kind=kOutput, calls=%fused_computation | convolution fusion | flops 1888358400 | bytes 8396800 | tf_op jit(solution)/shard_map/dot_general | solution.py:108
  300.5 33.6 %fusion = bf16[192,320]{1,0:T(8,128)(2,1)S(1)} fusion(bf16[2880,320]{1,0:T(8,128)(2,1)} %convolution_convert_fusion), kind=kCustom, calls=%all-reduce-scatter | all-reduce-scatter fusion | flops 983041 | bytes 1968128
  334.1 2.7 collective-permute-start.4
  337.5 5.1 collective-permute-start.3
  342.6 5.2 collective-permute-start.2
  347.8 100.6 %all-reduce.4 = (f32[320]{0:T(512)S(1)}, f32[320]{0:T(512)S(1)}) all-reduce(f32[320]{0:T(512)S(1)} %get-tuple-element.32, f32[320]{0:T(512)S(1)} %get-tuple-element.35), channel_id=1, replica_groups=mesh['tile'=32,'fsdp'=16] {'tile','fsdp'}, use_global_device_ids=true, to_apply=%region_15.16 | all-reduce | flops 640 | bytes 5120 | tf_op jit(solution)/shard_map/psum | solution.py:86
  449.0 2.2 reshape.73
  451.2 1.8 reverse_bitcast_fusion
  453.1 2.5 copy.34
  455.6 1.2 copy.38
  456.8 0.9 copy.35
  457.9 1.1 fusion.11
  459.0 1.0 slice_dynamic-update-slice_fusion.2
  460.0 1.1 fusion.12
  461.2 1.1 fusion.13
  462.3 1.0 slice_dynamic-update-slice_fusion.1
  463.3 1.1 fusion.14
  464.3 1.1 fusion.15
  465.4 1.0 slice_dynamic-update-slice_fusion
  466.4 1.1 fusion.16
  467.5 8.6 %copy.33 = bf16[8,128,2880]{2,1,0:T(8,128)(2,1)} copy(bf16[8,128,2880]{1,2,0:T(8,128)(2,1)} %fusion.16) | data formatting | bytes 11796480 | tf_op jit(solution)/shard_map/concatenate | solution.py:48
  477.7 4.9 fusion.4
  482.8 0.9 copy.36
  483.8 116.3 %all-reduce.8.cloned.1.call-done = bf16[180,320]{1,0:T(8,128)(2,1)} async-done(((bf16[180,320]{1,0:T(8,128)(2,1)}), bf16[180,320]{1,0:T(8,128)(2,1)}) %all-reduce.8.cloned.1.call-update) | async-done | bytes 115216 | tf_op jit(solution)/shard_map/psum | solution.py:107
  600.1 2.0 divide_subtract_fusion
  (62 shorter events, 7.3 us)
Async XLA Ops:
  7.2 14.4 %copy-start.3 = (bf16[1,1,8,128,320]{3,4,2,1,0:T(8,128)(2,1)S(1)}, bf16[1,1,8,128,320]{3,4,2,1,0:T(8,128)(2,1)}, u32[]{:S(2)}) copy-start(bf16[1,1,8,128,320]{3,4,2,1,0:T(8,128)(2,1)} %param.10) | copy-start | bytes 1966084
  7.2 73.9 %all-gather.3.cloned.1.call-start = ((), (), s32[]{:S(2)}) async-start(), calls=%async_computation.1 | async-start | bytes 2402304 | tf_op jit(solution)/shard_map/all_gather | solution.py:72
  8.9 591.2 %all-reduce.8.cloned.1.call-start = ((), (), s32[]{:S(2)}) async-start(), calls=%async_computation | async-start | bytes 282624 | tf_op jit(solution)/shard_map/psum | solution.py:107
  10.9 14.3 %collective-permute-start = (bf16[1,128,320]{1,2,0:T(8,128)(2,1)S(1)}, bf16[1,128,320]{1,2,0:T(8,128)(2,1)S(1)}, u32[]{:S(2)}, u32[]{:S(2)}) collective-permute-start(bf16[1,128,320]{1,2,0:T(8,128)(2,1)S(1)} %get-tuple-element.46), channel_id=1, source_target_pairs={{16,0},{32,16},{48,32},{64,48},{80,64},{96,80},{112,96},{128,112},... | collective-permute-start | bytes 245768 | tf_op jit(solution)/shard_map/ppermute | solution.py:20
  19.7 5.5 collective-permute-start.1
  83.8 140.5 %copy-start.6 = (f32[320]{0:T(512)S(1)}, f32[320]{0:T(512)}, u32[]{:S(2)}) copy-start(f32[320]{0:T(512)} %param.12) | copy-start | bytes 3844
  83.8 140.5 %copy-start.7 = (f32[320]{0:T(512)S(1)}, f32[320]{0:T(512)}, u32[]{:S(2)}) copy-start(f32[320]{0:T(512)} %param.13) | copy-start | bytes 3844
  299.8 149.2 %copy-start = (bf16[16,180,320]{2,1,0:T(8,128)(2,1)S(1)}, bf16[16,180,320]{2,1,0:T(8,128)(2,1)}, u32[]{:S(2)}) copy-start(bf16[16,180,320]{2,1,0:T(8,128)(2,1)} %all-gather.3.cloned.1.call-done) | copy-start | bytes 5529604
  334.1 141.9 %collective-permute-start.4 = (bf16[180,320]{1,0:T(8,128)(2,1)S(1)}, bf16[180,320]{1,0:T(8,128)(2,1)S(1)}, u32[]{:S(2)}, u32[]{:S(2)}) collective-permute-start(bf16[180,320]{1,0:T(8,128)(2,1)S(1)} %slice.98), channel_id=1, source_target_pairs={{0,1},{1,2},{2,3},{3,4},{4,5},{5,6},{6,7},{7,8},{8,9},{9,10},{10,1... | collective-permute-start | bytes 345608
  337.5 120.2 %collective-permute-start.3 = (bf16[1,128,320]{1,2,0:T(8,128)(2,1)}, bf16[1,128,320]{1,2,0:T(8,128)(2,1)S(1)}, u32[]{:S(2)}, u32[]{:S(2)}) collective-permute-start(bf16[1,128,320]{1,2,0:T(8,128)(2,1)} %constant_dynamic-slice_fusion.1), channel_id=1, source_target_pairs={{0,16},{16,32},{32,48},{48,64},{64,80},{80,96},{96,112},{112,128},... | collective-permute-start | bytes 245768 | tf_op jit(solution)/shard_map/ppermute | solution.py:18
  342.6 115.2 %collective-permute-start.2 = (bf16[1,128,320]{1,2,0:T(8,128)(2,1)}, bf16[1,128,320]{1,2,0:T(8,128)(2,1)S(1)}, u32[]{:S(2)}, u32[]{:S(2)}) collective-permute-start(bf16[1,128,320]{1,2,0:T(8,128)(2,1)} %slice_bitcast_fusion), channel_id=1, source_target_pairs={{16,0},{32,16},{48,32},{64,48},{80,64},{96,80},{112,96},{128,112},... | collective-permute-start | bytes 245768 | tf_op jit(solution)/shard_map/ppermute | solution.py:20
  467.5 10.2 %copy-start.1 = (bf16[9,320,320]{2,1,0:T(8,128)(2,1)S(1)}, bf16[9,320,320]{2,1,0:T(8,128)(2,1)}, u32[]{:S(2)}) copy-start(bf16[9,320,320]{2,1,0:T(8,128)(2,1)} %copy.34) | copy-start | bytes 5529604
  482.6 117.5 %copy-start.2 = (f32[180,320]{1,0:T(8,128)S(1)}, f32[180,320]{1,0:T(8,128)}, u32[]{:S(2)}) copy-start(f32[180,320]{1,0:T(8,128)} %param.11) | copy-start | bytes 691204
  482.7 117.4 %copy-start.4 = (f32[180,320]{1,0:T(8,128)S(1)}, f32[180,320]{1,0:T(8,128)}, u32[]{:S(2)}) copy-start(f32[180,320]{1,0:T(8,128)} %param.14) | copy-start | bytes 691204
  482.7 117.4 %copy-start.5 = (f32[180,320]{1,0:T(8,128)S(1)}, f32[180,320]{1,0:T(8,128)}, u32[]{:S(2)}) copy-start(f32[180,320]{1,0:T(8,128)} %param.15) | copy-start | bytes 691204
Sparse Core Ops, SparseCore 0:
  10.7 70.3 all-gather.2
  477.8 122.2 all-reduce.7
where the time goes:
time: 610 us; the launch traced here: 609 us
  blocking collectives  331 us (54%)
  waiting for transfers between devices  154 us (25%)
  local copies, waits for them, and re-layouts  55.7 us (9%)
  starting transfers between devices  23.8 us (4%)
  matrix products  17.4 us (3%)
  between operations  15.7 us (3%)
  other arithmetic  11.1 us (2%)
    psum x1, waiting for transfers between devices, local(): lax.psum(lax.dot_general(columns, pre_grad, (((0,), (0,)), ((), ())), pre...  116 us
    psum x1, blocking collectives, local(): lax.psum((jnp.sum(dshift * normed, axis=0), jnp.sum(dshift, axis=0)), ('t...  101 us
    psum x1, blocking collectives, local(): group_mean = lax.psum(grouped(mixed * cell_mask), 'tile') / population  71.5 us
    psum x1, blocking collectives, local(): lax.psum((grouped(scaled), grouped(scaled * normed)), 'tile')  62.9 us
    psum x1, blocking collectives, local(): variance = lax.psum(grouped(centered * centered), 'tile') / population  62.7 us
    all_gather x1, waiting for transfers between devices, local(): lax.all_gather(master_weight.astype(jnp.bfloat16), 'fsdp', axis=0, tiled=...  37.7 us
    unnamed x1, blocking collectives  33.6 us
    unnamed x41, local copies, waits for them, and re-layouts  25.8 us
  transfers between devices with their start and end apart: 7, of which 2 were waited for; matrix products, arithmetic and copies ran while one was open for 9% of the time, Pallas kernels for 0%

commit v1 on v0

v1 whole, which is shorter than its diff:
```python
import jax
import jax.numpy as jnp
from jax import lax
from jax.sharding import Mesh, PartitionSpec as P

GROUPS = 32
ROWS_MEAN = 5
PIECE = 24
TILE = ("y", "x", "core")


def beside(first_row, last_row):
    count = 32
    ends = count - 1
    above = lax.ppermute(last_row, TILE, [(i, (i + 1) % count) for i in range(ends)])
    below = lax.ppermute(first_row, TILE, [((i + 1) % count, i) for i in range(ends)])
    return above, below


def framed(source, above, below, live_count):
    slot_count = source.shape[0]
    zero_row = jnp.zeros_like(source[0:1])
    stacked = jnp.concatenate([above, source, zero_row], axis=0)
    marker = (jnp.arange(slot_count + 2) == live_count + 1)[:, None, None]
    stacked = jnp.where(marker, below, stacked)
    return jnp.pad(stacked, ((0, 0), (1, 1), (0, 0)))


def patches_of(padded, slot_count, cell_cols):
    pieces = [
        padded[row_step : row_step + slot_count, col_step : col_step + cell_cols, :]
        for row_step in range(3)
        for col_step in range(3)
    ]
    return jnp.concatenate(pieces, axis=-1).reshape(slot_count * cell_cols, -1)


def gather_equal(value, axes, count):
    copies = jnp.broadcast_to(value, (count,) + value.shape)
    return lax.all_to_all(copies, axes, 0, 0)


def other_core(value):
    return lax.ppermute(value, "core", [(0, 1), (1, 0)])


def gather_weights(shard):
    core, y = lax.axis_index("core"), lax.axis_index("y")
    channels = shard.shape[1]
    rows = shard.shape[0]
    padded = jnp.pad(shard.astype(jnp.bfloat16), ((0, 8 * PIECE - rows), (0, 0)))
    pieces = padded.reshape(8, PIECE, channels)
    mine = lax.dynamic_index_in_dim(pieces, core * 4 + y, 0, keepdims=False)
    along_z = gather_equal(mine, "fsdp", 16)
    along_y = gather_equal(along_z, "y", 4)
    passed = other_core(along_y)
    first = core == 0
    both = jnp.stack([jnp.where(first, along_y, passed), jnp.where(first, passed, along_y)])
    ordered = both.transpose(2, 0, 1, 3, 4).reshape(16, 8 * PIECE, channels)
    return ordered[:, :rows].reshape(16 * rows, channels)


def reduce_weights(partial, gain_total, bias_total, rows):
    core, y = lax.axis_index("core"), lax.axis_index("y")
    channels = partial.shape[1]
    blocks = jnp.pad(partial.reshape(16, rows, channels), ((0, 0), (0, 8 * PIECE - rows), (0, 0)))
    blocks = blocks.reshape(16, 2, 4, PIECE, channels).transpose(1, 2, 0, 3, 4)
    blocks = blocks.astype(jnp.bfloat16)
    keep = lax.dynamic_index_in_dim(blocks, core, 0, keepdims=False)
    send = lax.dynamic_index_in_dim(blocks, 1 - core, 0, keepdims=False)
    pair = (keep.astype(jnp.float32) + other_core(send).astype(jnp.float32)).astype(jnp.bfloat16)
    quads = lax.all_to_all(pair, "y", 0, 0)
    quad = jnp.sum(quads.astype(jnp.float32), axis=0)
    extra = jnp.stack([gain_total, bias_total])
    high = extra.astype(jnp.bfloat16).astype(jnp.float32)
    rider = jnp.concatenate([high, extra - high], axis=0)
    slot = rows - 7 * PIECE
    rider = jnp.pad(rider, ((slot, PIECE - slot - 4), (0, 0)))
    last = (core * 4 + y) == 7
    quad = (quad + jnp.where(last, rider, 0.0)[None]).astype(jnp.bfloat16)
    frames = lax.all_to_all(quad, "fsdp", 0, 0)
    frame_sum = jnp.sum(frames.astype(jnp.float32), axis=0)
    tiles = gather_equal(frame_sum, TILE, 32).reshape(4, 4, 2, PIECE, channels)
    shard = jnp.sum(tiles, axis=1).transpose(1, 0, 2, 3).reshape(8 * PIECE, channels)
    riders = tiles[3, 0, 1, slot : slot + 4]
    return shard[:rows], riders[0] + riders[2], riders[1] + riders[3]


def local(
    images, tile_rows, cotangent, master_weight, norm_gain, norm_bias, first_moment, second_moment
):
    slot_count, cell_cols, channels = (images.shape[2], images.shape[3], images.shape[4])
    per_group = channels // GROUPS
    population = jnp.float32(ROWS_MEAN * 32 * cell_cols * per_group)
    live_count = tile_rows[0, 0]
    live_rows = jnp.arange(slot_count) < live_count
    cell_mask = jnp.repeat(live_rows, cell_cols).astype(jnp.float32)[:, None]

    def grouped(values):
        return jnp.sum(values.reshape(-1, GROUPS, per_group), axis=(0, 2))

    def spread(stat):
        return jnp.repeat(stat, per_group)

    source = jnp.where(live_rows[:, None, None], images[0, 0], jnp.zeros((), jnp.bfloat16))
    above, below = beside(
        source[0:1], lax.dynamic_slice_in_dim(source, live_count - 1, 1, 0)
    )
    columns = patches_of(framed(source, above, below, live_count), slot_count, cell_cols)
    gathered = gather_weights(master_weight)
    mixed = jnp.dot(columns, gathered, preferred_element_type=jnp.float32)
    own_count = live_count.astype(jnp.float32) * (cell_cols * per_group)
    own_sum = grouped(mixed * cell_mask)
    own_centered = (mixed - spread(own_sum / own_count)) * cell_mask
    own_square = grouped(own_centered * own_centered)
    message = jnp.concatenate([own_sum, own_square, jnp.full((64,), own_count)])
    stats = gather_equal(message, TILE, 32)
    sums, squares, counts = stats[:, :32], stats[:, 32:64], stats[:, 64:65]
    group_mean = jnp.sum(sums, axis=0) / population
    offset = sums / counts - group_mean
    variance = jnp.sum(squares + counts * offset * offset, axis=0) / population
    inverse = lax.rsqrt(variance + 1e-05)
    normed = (mixed - spread(group_mean)) * spread(inverse)
    shifted = normed * norm_gain + norm_bias
    gate_value = jax.nn.sigmoid(shifted)
    activation = (shifted * gate_value * cell_mask).astype(jnp.bfloat16).reshape(images.shape)
    upstream = cotangent[0, 0].reshape(-1, channels).astype(jnp.float32) * cell_mask
    dshift = upstream * gate_value * (1.0 + shifted * (1.0 - gate_value))
    scaled = dshift * norm_gain
    per_channel = jnp.concatenate([jnp.sum(dshift * normed, axis=0), jnp.sum(dshift, axis=0)])
    totals = jnp.sum(gather_equal(per_channel, TILE, 32), axis=0)
    gain_total, bias_total = totals[:channels], totals[channels:]
    delta_sum = jnp.sum((bias_total * norm_gain).reshape(GROUPS, per_group), axis=1)
    cross_sum = jnp.sum((gain_total * norm_gain).reshape(GROUPS, per_group), axis=1)
    norm_scale = jnp.float32(16 * ROWS_MEAN * 32 * cell_cols) ** (-0.5)
    pre_grad = spread(inverse) * (
        scaled - spread(delta_sum / population) - normed * spread(cross_sum / population)
    )
    pre_grad = (pre_grad * cell_mask).astype(jnp.bfloat16)
    grad_field = pre_grad.reshape(slot_count, cell_cols, channels)
    above_grad, below_grad = beside(
        grad_field[0:1], lax.dynamic_slice_in_dim(grad_field, live_count - 1, 1, 0)
    )
    partial = lax.dot_general(
        columns, pre_grad, (((0,), (0,)), ((), ())), preferred_element_type=jnp.float32
    )
    rows = master_weight.shape[0]
    grad_shard, gain_all, bias_all = reduce_weights(partial, gain_total, bias_total, rows)
    grad_columns = patches_of(
        framed(grad_field, above_grad, below_grad, live_count), slot_count, cell_cols
    )
    flipped = (
        gathered.reshape(9, channels, channels)[::-1]
        .transpose(0, 2, 1)
        .reshape(9 * channels, channels)
    )
    image_grad = (
        (jnp.dot(grad_columns, flipped, preferred_element_type=jnp.float32) * cell_mask)
        .astype(jnp.bfloat16)
        .reshape(images.shape)
    )
    weight_grad = grad_shard * norm_scale
    new_first = 0.9 * first_moment + 0.1 * weight_grad
    new_second = 0.999 * second_moment + 0.001 * weight_grad * weight_grad
    first_fix = new_first / (1.0 - 0.9**10)
    second_fix = new_second / (1.0 - 0.999**10)
    new_weight = master_weight - 0.01 * first_fix / (jnp.sqrt(second_fix) + 1e-08)
    return (
        activation,
        image_grad,
        weight_grad,
        new_weight,
        new_first,
        new_second,
        gain_all * norm_scale,
        bias_all * norm_scale,
    )


def solution(mesh):
    fine = Mesh(mesh.devices.reshape(4, 4, 2, 16), ("y", "x", "core", "fsdp"))
    pixels = P("fsdp", TILE, None, None, None)
    placed = (
        pixels,
        P("fsdp", TILE),
        pixels,
        P("fsdp", None),
        P(),
        P(),
        P("fsdp", None),
        P("fsdp", None),
    )
    return jax.shard_map(
        local,
        mesh=fine,
        in_specs=placed,
        out_specs=(
            pixels,
            pixels,
            P("fsdp", None),
            P("fsdp", None),
            P("fsdp", None),
            P("fsdp", None),
            P(),
            P(),
        ),
        check_vma=False,
    )
```

time: 610 us -> 232 us (0.38)
  blocking collectives: 331 us -> 0 us
  waiting for transfers between devices: 154 us -> 35.8 us
  starting transfers between devices: 23.8 us -> 80.3 us
  local copies, waits for them, and re-layouts: 55.7 us -> 75.3 us
  between operations: 15.7 us -> 1.85 us
  other arithmetic: 11.1 us -> 18 us
    psum x4 -> x0, blocking collectives: 298 us -> none  [the longest x1 101 us: local(): lax.psum((jnp.sum(dshift * normed, axis=0), jnp.sum(dshift, axis=0)), ('t...]
    psum x1 -> x0, waiting for transfers between devices: 116 us -> none  [local(): lax.psum(lax.dot_general(columns, pre_grad, (((0,), (0,)), ((), ())), pre...]
    all_to_all x0 -> x7, starting transfers between devices: none -> 56.8 us  [the longest x5 41.9 us: gather_equal(): return lax.all_to_all(copies, axes, 0, 0)]
    all_gather x1 -> x0, waiting for transfers between devices: 37.7 us -> none  [local(): lax.all_gather(master_weight.astype(jnp.bfloat16), 'fsdp', axis=0, tiled=...]
    unnamed x1 -> x0, blocking collectives: 33.6 us -> none
    all_to_all x0 -> x7, waiting for transfers between devices: none -> 31.7 us  [the longest x5 19.7 us: gather_equal(): return lax.all_to_all(copies, axes, 0, 0)]
    dot_general x0 -> x2, local copies, waits for them, and re-layouts: none -> 16.4 us  [local(): lax.dot_general(columns, pre_grad, (((0,), (0,)), ((), ())), preferred_el...]
    ppermute x4 -> x6, starting transfers between devices: 21 us -> 23.5 us  [the longest x2 12.2 us: other_core(): return lax.ppermute(value, 'core', [(0, 1), (1, 0)])]
  transfers between devices with their start and end apart: 7 -> 13, of which waited for: 2 -> 7; matrix products, arithmetic and copies ran while one was open for 9% -> 32% of each run, Pallas kernels for 0% -> 0%
where the time goes in v1:
time: 232 us; the launch traced here: 230 us
  starting transfers between devices  80.3 us (35%)
  local copies, waits for them, and re-layouts  75.3 us (32%)
  waiting for transfers between devices  35.8 us (15%)
  matrix products  18.6 us (8%)
  other arithmetic  18 us (8%)
    all_to_all x5, starting transfers between devices, gather_equal(): return lax.all_to_all(copies, axes, 0, 0)  41.9 us
    unnamed x41, local copies, waits for them, and re-layouts  21.4 us
    all_to_all x5, waiting for transfers between devices, gather_equal(): return lax.all_to_all(copies, axes, 0, 0)  19.7 us
    concatenate x4, local copies, waits for them, and re-layouts, patches_of(): return jnp.concatenate(pieces, axis=-1).reshape(slot_count * cell_cols, -1)  19.1 us
    dot_general x2, local copies, waits for them, and re-layouts, local(): lax.dot_general(columns, pre_grad, (((0,), (0,)), ((), ())), preferred_el...  16.4 us
    ppermute x2, starting transfers between devices, other_core(): return lax.ppermute(value, 'core', [(0, 1), (1, 0)])  12.2 us
    all_to_all x1, starting transfers between devices, reduce_weights(): frames = lax.all_to_all(quad, 'fsdp', 0, 0)  10.8 us
    all_to_all x1, waiting for transfers between devices, reduce_weights(): frames = lax.all_to_all(quad, 'fsdp', 0, 0)  6.91 us
  transfers between devices with their start and end apart: 13, of which 7 were waited for; matrix products, arithmetic and copies ran while one was open for 32% of the time, Pallas kernels for 0%

profile of v1, /device:TPU:1, one launch (start us, length us, event | category | flops | bytes accessed | tf_op | source)
XLA Modules:
  0.0 229.8 jit_solution(7349424495023578375)
XLA Ops:
  2.5 15.7 %all-to-all-start = ((bf16[16,24,320]{2,1,0:T(8,128)(2,1)}), bf16[16,24,320]{2,1,0:T(8,128)(2,1)S(1)}, u32[]{:S(2)}, u32[]{:S(2)}) async-start(bf16[16,24,320]{2,1,0:T(8,128)(2,1)} %broadcast_in_dim.95), calls=%async_computation | async-start | bytes 589824 | tf_op jit(solution)/shard_map/all_to_all | solution.py:40
  19.1 2.9 %collective-permute-start = (bf16[1,128,320]{1,2,0:T(8,128)(2,1)S(1)}, bf16[1,128,320]{1,2,0:T(8,128)(2,1)S(1)}, u32[]{:S(2)}, u32[]{:S(2)}) collective-permute-start(bf16[1,128,320]{1,2,0:T(8,128)(2,1)S(1)} %get-tuple-element.78), channel_id=1, source_target_pairs={{16,0},{32,16},{48,32},{64,48},{80,64},{96,80},{112,96},{128,112},... | collective-permute-start | bytes 245768 | tf_op jit(solution)/shard_map/ppermute | solution.py:16
  21.9 3.0 %collective-permute-start.1 = (bf16[1,128,320]{1,2,0:T(8,128)(2,1)S(1)}, bf16[1,128,320]{1,2,0:T(8,128)(2,1)S(1)}, u32[]{:S(2)}, u32[]{:S(2)}) collective-permute-start(bf16[1,128,320]{1,2,0:T(8,128)(2,1)S(1)} %get-tuple-element.79), channel_id=1, source_target_pairs={{0,16},{16,32},{32,48},{48,64},{64,80},{80,96},{96,112},{112,128},... | collective-permute-start | bytes 245768 | tf_op jit(solution)/shard_map/ppermute | solution.py:15
  25.1 6.9 %all-to-all-done = bf16[16,24,320]{2,1,0:T(8,128)(2,1)S(1)} async-done(((bf16[16,24,320]{2,1,0:T(8,128)(2,1)}), bf16[16,24,320]{2,1,0:T(8,128)(2,1)S(1)}, u32[]{:S(2)}, u32[]{:S(2)}) %all-to-all-start) | async-done | bytes 245792 | tf_op jit(solution)/shard_map/all_to_all | solution.py:40
  32.0 1.1 broadcast_in_dim.96
  33.1 4.2 %all-to-all-start.1 = ((bf16[4,16,24,320]{3,2,1,0:T(8,128)(2,1)}), bf16[4,16,24,320]{3,2,1,0:T(8,128)(2,1)S(1)}, u32[]{:S(2)}, u32[]{:S(2)}) async-start(bf16[4,16,24,320]{3,2,1,0:T(8,128)(2,1)} %broadcast_in_dim.96), calls=%async_computation.1 | async-start | bytes 2359296 | tf_op jit(solution)/shard_map/all_to_all | solution.py:40
  37.5 1.1 fusion.5
  39.6 1.1 fusion.6
  40.7 7.0 %all-to-all-done.1 = bf16[4,16,24,320]{3,2,1,0:T(8,128)(2,1)S(1)} async-done(((bf16[4,16,24,320]{3,2,1,0:T(8,128)(2,1)}), bf16[4,16,24,320]{3,2,1,0:T(8,128)(2,1)S(1)}, u32[]{:S(2)}, u32[]{:S(2)}) %all-to-all-start.1) | async-done | bytes 983072 | tf_op jit(solution)/shard_map/all_to_all | solution.py:40
  47.7 1.2 copy.96
  48.9 9.8 %collective-permute-start.2 = (bf16[4,16,24,320]{3,2,0,1:T(8,128)(2,1)}, bf16[4,16,24,320]{3,2,0,1:T(8,128)(2,1)S(1)}, u32[]{:S(2)}, u32[]{:S(2)}) collective-permute-start(bf16[4,16,24,320]{3,2,0,1:T(8,128)(2,1)} %copy.96), channel_id=1, source_target_pairs={{0,16},{16,0},{1,17},{17,1},{2,18},{18,2},{3,19},{19,3},{4,20},{20... | collective-permute-start | bytes 2949128 | tf_op jit(solution)/shard_map/ppermute | solution.py:44
  58.7 1.1 fusion.7
  65.0 8.4 %copy.94 = bf16[8,128,2880]{2,1,0:T(8,128)(2,1)} copy(bf16[8,128,2880]{1,2,0:T(8,128)(2,1)} %fusion.10) | data formatting | bytes 11796480 | tf_op jit(solution)/shard_map/concatenate | solution.py:35
  74.4 2.2 reshape.119
  76.6 6.7 %multiply_reduce_fusion.2 = (f32[320]{0:T(512)S(1)}, f32[1024,320]{0,1:T(8,128)}) fusion(f32[1024]{0:T(1024)S(1)} %broadcast_bitcast_fusion, bf16[1024,2880]{1,0:T(8,128)(2,1)} %bitcast.86, bf16[2880,320]{1,0:T(8,128)(2,1)} %reshape.119), kind=kOutput, calls=%fused_computation.30 | convolution fusion | flops 1888091904 | bytes 9057536 | tf_op jit(solution)/shard_map/dot_general | solution.py:111
  83.8 1.7 multiply_reduce_fusion.1
  86.4 5.2 %all-to-all-start.2 = ((f32[32,1,128]{2,1,0:T(1,128)}), f32[32,1,128]{2,1,0:T(1,128)S(1)}, u32[]{:S(2)}, u32[]{:S(2)}) async-start(f32[32,1,128]{2,1,0:T(1,128)} %broadcast_in_dim.100), calls=%async_computation.2 | async-start | bytes 32768 | tf_op jit(solution)/shard_map/all_to_all | solution.py:40
  91.6 1.5 copy.99
  93.1 5.4 %all-to-all-done.2 = f32[32,1,128]{2,1,0:T(1,128)S(1)} async-done(((f32[32,1,128]{2,1,0:T(1,128)}), f32[32,1,128]{2,1,0:T(1,128)S(1)}, u32[]{:S(2)}, u32[]{:S(2)}) %all-to-all-start.2) | async-done | bytes 16416 | tf_op jit(solution)/shard_map/all_to_all | solution.py:40
  99.1 4.0 %multiply_reduce_fusion = (f32[320]{0:T(512)S(1)}, f32[320]{0:T(512)S(1)}, f32[1024,320]{0,1:T(8,128)}, bf16[40,8,8,128]{3,1,2,0:T(8,128)(2,1)}) fusion(f32[1024,320]{0,1:T(8,128)} %get-tuple-element.85, f32[320]{0:T(512)S(1)} %mul.187, f32[320]{0:T(512)S(1)} %sub.61, f32[320]{0:T(512)S(1)} %copy-done.9, f32[320]{0:T(512)S(1)} %copy-done.8, ...), kind=kLoop, calls=%fused_computation.24 | loop fusion | flops 6225280 | bytes 4599296 | tf_op jit(solution)/shard_map/reduce_sum | solution.py:130
  103.8 4.2 %all-to-all-start.3 = ((f32[32,1,640]{2,1,0:T(1,128)}), f32[32,1,640]{2,1,0:T(1,128)S(1)}, u32[]{:S(2)}, u32[]{:S(2)}) async-start(f32[32,1,640]{2,1,0:T(1,128)} %broadcast_in_dim.103), calls=%async_computation.3 | async-start | bytes 163840 | tf_op jit(solution)/shard_map/all_to_all | solution.py:40
  108.0 8.4 %copy.105 = bf16[2880,1024]{1,0:T(8,128)(2,1)} copy(bf16[2880,1024]{0,1:T(8,128)(2,1)} %bitcast.87) | data formatting | bytes 11796480 | tf_op jit(solution)/shard_map/dot_general | solution.py:144
  116.4 8.0 %dot_general.16 = bf16[16,180,1024]{2,1,0:T(8,128)(2,1)} reshape(bf16[2880,1024]{1,0:T(8,128)(2,1)} %copy.105) | data formatting | bytes 11796480 | tf_op jit(solution)/shard_map/dot_general | solution.py:144
  125.4 2.5 %multiply_convert_fusion = bf16[1024,320]{0,1:T(8,128)(2,1)S(1)} fusion(f32[1024,320]{0,1:T(8,128)} %get-tuple-element.72, f32[1024,320]{0,1:T(8,128)} %get-tuple-element.85, f32[320]{0:T(512)S(1)} %mul.202, f32[320]{0:T(512)S(1)} %sub.67, f32[320]{0:T(512)S(1)} %copy-done.8, f32[320]{0:T(512)S(1)} %mul.187, f32[320]{0:T(512)S(1)} %sub.61, ...), kind=kLoop, calls=%fused_computation.23 | loop fusion | flops 2949120 | bytes 3287296 | tf_op jit(solution)/shard_map/convert_element_type | solution.py:139
  128.0 6.3 %convolution_convert_fusion = bf16[16,180,320]{2,1,0:T(8,128)(2,1)S(1)} fusion(bf16[16,180,1024]{2,1,0:T(8,128)(2,1)} %dot_general.16, bf16[1024,320]{0,1:T(8,128)(2,1)S(1)} %multiply_convert_fusion), kind=kOutput, calls=%fused_computation.17 | convolution fusion | flops 1888358400 | bytes 8396800 | tf_op jit(solution)/shard_map/dot_general | solution.py:144
  134.9 1.1 copy.127
  136.0 2.4 %collective-permute-start.5 = (bf16[4,16,24,320]{3,2,1,0:T(8,128)(2,1)}, bf16[4,16,24,320]{3,2,1,0:T(8,128)(2,1)}, u32[]{:S(2)}, u32[]{:S(2)}) collective-permute-start(bf16[4,16,24,320]{3,2,1,0:T(8,128)(2,1)} %bitcast.80), channel_id=1, source_target_pairs={{0,16},{16,0},{1,17},{17,1},{2,18},{18,2},{3,19},{19,3},{4,20},{20... | collective-permute-start | bytes 2949128 | tf_op jit(solution)/shard_map/ppermute | solution.py:44
  138.5 2.2 reshape_reshape.3
  140.7 1.8 reverse_bitcast_fusion
  142.6 2.5 %copy.104 = bf16[9,320,320]{2,1,0:T(8,128)(2,1)} copy(bf16[9,320,320]{1,2,0:T(8,128)(2,1)S(1)} %reverse_bitcast_fusion) | data formatting | bytes 3686400 | tf_op jit(solution)/shard_map/transpose | solution.py:154
  145.0 1.3 copy.117
  147.4 2.8 %fusion = bf16[4,16,24,320]{3,2,1,0:T(8,128)(2,1)} fusion(bf16[4,16,24,320]{3,2,1,0:T(8,128)(2,1)} %collective-permute-done.5, bf16[16,1,4,24,320]{4,3,2,1,0:T(8,128)(2,1)S(1)} %get-tuple-element.73), kind=kLoop, calls=%fused_computation.14 | loop fusion | flops 1966080 | bytes 2949120 | tf_op jit(solution)/shard_map/convert_element_type | solution.py:71
  150.2 4.1 %all-to-all-start.4 = ((bf16[4,16,24,320]{3,2,1,0:T(8,128)(2,1)}), bf16[4,16,24,320]{3,2,1,0:T(8,128)(2,1)S(1)}, u32[]{:S(2)}, u32[]{:S(2)}) async-start(bf16[4,16,24,320]{3,2,1,0:T(8,128)(2,1)} %fusion), calls=%async_computation.4 | async-start | bytes 2359296 | tf_op jit(solution)/shard_map/all_to_all | solution.py:72
  154.4 3.4 %collective-permute-start.4 = (bf16[1,128,320]{1,2,0:T(8,128)(2,1)S(1)}, bf16[1,128,320]{1,2,0:T(8,128)(2,1)S(1)}, u32[]{:S(2)}, u32[]{:S(2)}) collective-permute-start(bf16[1,128,320]{1,2,0:T(8,128)(2,1)S(1)} %constant_dynamic-slice_fusion.2), channel_id=1, source_target_pairs={{0,16},{16,32},{32,48},{48,64},{64,80},{80,96},{96,112},{112,128},... | collective-permute-start | bytes 245768 | tf_op jit(solution)/shard_map/ppermute | solution.py:15
  157.8 1.9 collective-permute-start.3
  159.8 4.1 %collective-permute-done.3 = bf16[1,128,320]{1,2,0:T(8,128)(2,1)S(1)} collective-permute-done((bf16[1,128,320]{1,2,0:T(8,128)(2,1)S(1)}, bf16[1,128,320]{1,2,0:T(8,128)(2,1)S(1)}, u32[]{:S(2)}, u32[]{:S(2)}) %collective-permute-start.3) | collective-permute-done | bytes 81952 | tf_op jit(solution)/shard_map/ppermute | solution.py:16
  163.9 1.3 maximum_select_fusion.1
  165.2 1.1 fusion.11
  166.3 5.1 %all-to-all-done.4 = bf16[4,16,24,320]{3,2,1,0:T(8,128)(2,1)S(1)} async-done(((bf16[4,16,24,320]{3,2,1,0:T(8,128)(2,1)}), bf16[4,16,24,320]{3,2,1,0:T(8,128)(2,1)S(1)}, u32[]{:S(2)}, u32[]{:S(2)}) %all-to-all-start.4) | async-done | bytes 983072 | tf_op jit(solution)/shard_map/all_to_all | solution.py:72
  172.3 10.8 %all-to-all-start.5 = ((bf16[16,24,320]{2,1,0:T(8,128)(2,1)}), bf16[16,24,320]{2,1,0:T(8,128)(2,1)S(1)}, u32[]{:S(2)}, u32[]{:S(2)}) async-start(bf16[16,24,320]{2,1,0:T(8,128)(2,1)} %add_convert_fusion), calls=%async_computation.5 | async-start | bytes 589824 | tf_op jit(solution)/shard_map/all_to_all | solution.py:81
  184.2 1.1 fusion.12
  185.3 1.1 fusion.13
  189.5 6.9 %all-to-all-done.5 = bf16[16,24,320]{2,1,0:T(8,128)(2,1)S(1)} async-done(((bf16[16,24,320]{2,1,0:T(8,128)(2,1)}), bf16[16,24,320]{2,1,0:T(8,128)(2,1)S(1)}, u32[]{:S(2)}, u32[]{:S(2)}) %all-to-all-start.5) | async-done | bytes 245792 | tf_op jit(solution)/shard_map/all_to_all | solution.py:81
  196.5 1.1 broadcast_in_dim.109
  197.6 12.6 %all-to-all-start.6 = ((f32[32,24,320]{2,1,0:T(8,128)}), f32[32,24,320]{2,1,0:T(8,128)S(1)}, u32[]{:S(2)}, u32[]{:S(2)}) async-start(f32[32,24,320]{2,1,0:T(8,128)} %broadcast_in_dim.109), calls=%async_computation.6 | async-start | bytes 2359296 | tf_op jit(solution)/shard_map/all_to_all | solution.py:40
  212.3 8.4 %copy.103 = bf16[8,128,2880]{2,1,0:T(8,128)(2,1)} copy(bf16[8,128,2880]{1,2,0:T(8,128)(2,1)} %fusion.16) | data formatting | bytes 11796480 | tf_op jit(solution)/shard_map/concatenate | solution.py:35
  220.8 5.6 %fusion.4 = bf16[40,8,8,128]{3,1,2,0:T(8,128)(2,1)S(1)} fusion(bf16[1024,2880]{1,0:T(8,128)(2,1)} %bitcast.90, bf16[2880,320]{1,0:T(8,128)(2,1)} %bitcast.96, f32[1024]{0:T(1024)S(1)} %broadcast_bitcast_fusion), kind=kOutput, calls=%fused_computation.31 | convolution fusion | flops 1888092160 | bytes 8400896 | tf_op jit(solution)/shard_map/dot_general | solution.py:158
  228.7 1.1 divide_subtract_fusion
  (105 shorter events, 24.3 us)
Async XLA Ops:
  0.6 18.3 %copy-start.4 = (bf16[1,1,8,128,320]{3,4,2,1,0:T(8,128)(2,1)S(1)}, bf16[1,1,8,128,320]{3,4,2,1,0:T(8,128)(2,1)}, u32[]{:S(2)}) copy-start(bf16[1,1,8,128,320]{3,4,2,1,0:T(8,128)(2,1)} %param.8) | copy-start | bytes 1966084
  2.5 29.5 %all-to-all-start = ((bf16[16,24,320]{2,1,0:T(8,128)(2,1)}), bf16[16,24,320]{2,1,0:T(8,128)(2,1)S(1)}, u32[]{:S(2)}, u32[]{:S(2)}) async-start(bf16[16,24,320]{2,1,0:T(8,128)(2,1)} %broadcast_in_dim.95), calls=%async_computation | async-start | bytes 589824 | tf_op jit(solution)/shard_map/all_to_all | solution.py:40
  19.1 18.2 %collective-permute-start = (bf16[1,128,320]{1,2,0:T(8,128)(2,1)S(1)}, bf16[1,128,320]{1,2,0:T(8,128)(2,1)S(1)}, u32[]{:S(2)}, u32[]{:S(2)}) collective-permute-start(bf16[1,128,320]{1,2,0:T(8,128)(2,1)S(1)} %get-tuple-element.78), channel_id=1, source_target_pairs={{16,0},{32,16},{48,32},{64,48},{80,64},{96,80},{112,96},{128,112},... | collective-permute-start | bytes 245768 | tf_op jit(solution)/shard_map/ppermute | solution.py:16
  21.9 15.4 %collective-permute-start.1 = (bf16[1,128,320]{1,2,0:T(8,128)(2,1)S(1)}, bf16[1,128,320]{1,2,0:T(8,128)(2,1)S(1)}, u32[]{:S(2)}, u32[]{:S(2)}) collective-permute-start(bf16[1,128,320]{1,2,0:T(8,128)(2,1)S(1)} %get-tuple-element.79), channel_id=1, source_target_pairs={{0,16},{16,32},{32,48},{48,64},{64,80},{80,96},{96,112},{112,128},... | collective-permute-start | bytes 245768 | tf_op jit(solution)/shard_map/ppermute | solution.py:15
  33.1 14.6 %all-to-all-start.1 = ((bf16[4,16,24,320]{3,2,1,0:T(8,128)(2,1)}), bf16[4,16,24,320]{3,2,1,0:T(8,128)(2,1)S(1)}, u32[]{:S(2)}, u32[]{:S(2)}) async-start(bf16[4,16,24,320]{3,2,1,0:T(8,128)(2,1)} %broadcast_in_dim.96), calls=%async_computation.1 | async-start | bytes 2359296 | tf_op jit(solution)/shard_map/all_to_all | solution.py:40
  48.9 24.6 %collective-permute-start.2 = (bf16[4,16,24,320]{3,2,0,1:T(8,128)(2,1)}, bf16[4,16,24,320]{3,2,0,1:T(8,128)(2,1)S(1)}, u32[]{:S(2)}, u32[]{:S(2)}) collective-permute-start(bf16[4,16,24,320]{3,2,0,1:T(8,128)(2,1)} %copy.96), channel_id=1, source_target_pairs={{0,16},{16,0},{1,17},{17,1},{2,18},{18,2},{3,19},{19,3},{4,20},{20... | collective-permute-start | bytes 2949128 | tf_op jit(solution)/shard_map/ppermute | solution.py:44
  83.3 8.2 %copy-start.5 = (bf16[1,1,8,128,320]{3,4,2,1,0:T(8,128)(2,1)S(1)}, bf16[1,1,8,128,320]{3,4,2,1,0:T(8,128)(2,1)}, u32[]{:S(2)}) copy-start(bf16[1,1,8,128,320]{3,4,2,1,0:T(8,128)(2,1)} %param.10) | copy-start | bytes 1966084
  83.8 15.4 %copy-start.8 = (f32[320]{0:T(512)S(1)}, f32[320]{0:T(512)}, u32[]{:S(2)}) copy-start(f32[320]{0:T(512)} %param.12) | copy-start | bytes 3844
  83.8 15.4 %copy-start.9 = (f32[320]{0:T(512)S(1)}, f32[320]{0:T(512)}, u32[]{:S(2)}) copy-start(f32[320]{0:T(512)} %param.13) | copy-start | bytes 3844
  86.4 12.0 %all-to-all-start.2 = ((f32[32,1,128]{2,1,0:T(1,128)}), f32[32,1,128]{2,1,0:T(1,128)S(1)}, u32[]{:S(2)}, u32[]{:S(2)}) async-start(f32[32,1,128]{2,1,0:T(1,128)} %broadcast_in_dim.100), calls=%async_computation.2 | async-start | bytes 32768 | tf_op jit(solution)/shard_map/all_to_all | solution.py:40
  103.8 20.6 %all-to-all-start.3 = ((f32[32,1,640]{2,1,0:T(1,128)}), f32[32,1,640]{2,1,0:T(1,128)S(1)}, u32[]{:S(2)}, u32[]{:S(2)}) async-start(f32[32,1,640]{2,1,0:T(1,128)} %broadcast_in_dim.103), calls=%async_computation.3 | async-start | bytes 163840 | tf_op jit(solution)/shard_map/all_to_all | solution.py:40
  127.9 6.3 %copy-start.1 = (bf16[1024,320]{0,1:T(8,128)(2,1)}, bf16[1024,320]{0,1:T(8,128)(2,1)S(1)}, u32[]{:S(2)}) copy-start(bf16[1024,320]{0,1:T(8,128)(2,1)S(1)} %multiply_convert_fusion) | copy-start | bytes 1966084
  136.0 11.4 %collective-permute-start.5 = (bf16[4,16,24,320]{3,2,1,0:T(8,128)(2,1)}, bf16[4,16,24,320]{3,2,1,0:T(8,128)(2,1)}, u32[]{:S(2)}, u32[]{:S(2)}) collective-permute-start(bf16[4,16,24,320]{3,2,1,0:T(8,128)(2,1)} %bitcast.80), channel_id=1, source_target_pairs={{0,16},{16,0},{1,17},{17,1},{2,18},{18,2},{3,19},{19,3},{4,20},{20... | collective-permute-start | bytes 2949128 | tf_op jit(solution)/shard_map/ppermute | solution.py:44
  145.0 2.2 copy-start.2
  147.4 6.9 %copy-start = (bf16[8,128,320]{1,2,0:T(8,128)(2,1)}, bf16[8,128,320]{1,2,0:T(8,128)(2,1)S(1)}, u32[]{:S(2)}) copy-start(bf16[8,128,320]{1,2,0:T(8,128)(2,1)S(1)} %copy_bitcast_fusion.1) | copy-start | bytes 1966084
  150.2 21.1 %all-to-all-start.4 = ((bf16[4,16,24,320]{3,2,1,0:T(8,128)(2,1)}), bf16[4,16,24,320]{3,2,1,0:T(8,128)(2,1)S(1)}, u32[]{:S(2)}, u32[]{:S(2)}) async-start(bf16[4,16,24,320]{3,2,1,0:T(8,128)(2,1)} %fusion), calls=%async_computation.4 | async-start | bytes 2359296 | tf_op jit(solution)/shard_map/all_to_all | solution.py:72
  154.4 5.4 %collective-permute-start.4 = (bf16[1,128,320]{1,2,0:T(8,128)(2,1)S(1)}, bf16[1,128,320]{1,2,0:T(8,128)(2,1)S(1)}, u32[]{:S(2)}, u32[]{:S(2)}) collective-permute-start(bf16[1,128,320]{1,2,0:T(8,128)(2,1)S(1)} %constant_dynamic-slice_fusion.2), channel_id=1, source_target_pairs={{0,16},{16,32},{32,48},{48,64},{64,80},{80,96},{96,112},{112,128},... | collective-permute-start | bytes 245768 | tf_op jit(solution)/shard_map/ppermute | solution.py:15
  157.8 6.1 %collective-permute-start.3 = (bf16[1,128,320]{1,2,0:T(8,128)(2,1)S(1)}, bf16[1,128,320]{1,2,0:T(8,128)(2,1)S(1)}, u32[]{:S(2)}, u32[]{:S(2)}) collective-permute-start(bf16[1,128,320]{1,2,0:T(8,128)(2,1)S(1)} %slice_bitcast_fusion), channel_id=1, source_target_pairs={{16,0},{32,16},{48,32},{64,48},{80,64},{96,80},{112,96},{128,112},... | collective-permute-start | bytes 245768 | tf_op jit(solution)/shard_map/ppermute | solution.py:16
  172.3 24.1 %all-to-all-start.5 = ((bf16[16,24,320]{2,1,0:T(8,128)(2,1)}), bf16[16,24,320]{2,1,0:T(8,128)(2,1)S(1)}, u32[]{:S(2)}, u32[]{:S(2)}) async-start(bf16[16,24,320]{2,1,0:T(8,128)(2,1)} %add_convert_fusion), calls=%async_computation.5 | async-start | bytes 589824 | tf_op jit(solution)/shard_map/all_to_all | solution.py:81
  197.6 30.3 %all-to-all-start.6 = ((f32[32,24,320]{2,1,0:T(8,128)}), f32[32,24,320]{2,1,0:T(8,128)S(1)}, u32[]{:S(2)}, u32[]{:S(2)}) async-start(f32[32,24,320]{2,1,0:T(8,128)} %broadcast_in_dim.109), calls=%async_computation.6 | async-start | bytes 2359296 | tf_op jit(solution)/shard_map/all_to_all | solution.py:40
  226.5 2.2 copy-start.3
  226.5 2.2 copy-start.6
  226.5 2.2 copy-start.7

commit v2 on v0

v2 whole, which is shorter than its diff:
```python
import functools
import jax
import jax.numpy as jnp
from jax import lax
from jax.experimental import pallas as pl
from jax.experimental.pallas import tpu as pltpu
from jax.sharding import Mesh, PartitionSpec as P

TILE = ("y", "x", "core")
CH = 320
PER = 10
COLS = 128
CAP = 8
SHARD = 180
WIDE = 192
DEEP = 16 * WIDE
ROWS = 40
LANES = 256
POPULATION = 204800.0
SCALE = 327680.0 ** -0.5
BF = jnp.bfloat16
F32 = jnp.float32
VMEM = pl.BlockSpec(memory_space=pltpu.VMEM)
SMEM = pl.BlockSpec(memory_space=pltpu.SMEM)


def spot(name):
    return lax.axis_index(name)


def call(body, outs, ins, scratch=(), grid=None, cost=1, room=16, **more):
    if grid is not None:
        more["grid"] = grid
    return pl.pallas_call(
        body,
        out_shape=outs,
        in_specs=ins,
        scratch_shapes=list(scratch),
        compiler_params=pltpu.CompilerParams(vmem_limit_bytes=room << 20),
        cost_estimate=pl.CostEstimate(
            flops=cost * 1000000000, bytes_accessed=cost << 21, transcendentals=0
        ),
        **more,
    )


def shape(dims, kind=F32):
    return jax.ShapeDtypeStruct(dims, kind)


def pack_body(weight, out, padded, turned):
    padded[...] = jnp.zeros(padded.shape, F32)
    padded[0:SHARD, 0:CH] = weight[...]
    turned[...] = jnp.transpose(padded[...])
    piece = spot("core") * 4 + spot("y")
    rows = turned[pl.ds(pl.multiple_of(piece * ROWS, 8), ROWS), :]
    odd = (spot("fsdp") % 2) == 1
    rows = jnp.where(odd, pltpu.roll(rows, 64, 1), rows).astype(BF)
    for frame in range(16):
        out[frame] = rows


def pack(weight):
    return call(
        pack_body,
        shape((16, ROWS, LANES), BF),
        [VMEM],
        [pltpu.VMEM((256, 384), F32), pltpu.VMEM((384, 256), F32)],
        out_specs=VMEM,
    )(weight)


def store_taps(row, field, slot, negate):
    lane = lax.broadcasted_iota(jnp.int32, (CH, COLS), 1)
    for b in range(3):
        turn = (1 - b) if not negate else (b - 1)
        if turn == 0:
            moved = row
        elif turn == 1:
            moved = jnp.where(lane == 0, 0.0, pltpu.roll(row, 1, 1))
        else:
            moved = jnp.where(lane == COLS - 1, 0.0, pltpu.roll(row, COLS - 1, 1))
        for a in range(3):
            up = a if not negate else 2 - a
            r = slot - up
            if 0 <= r < CAP:
                field(3 * a + b, r, moved)


def framed_row(slot, own, above, below, live):
    if slot == 0:
        return above[0].astype(F32)
    base = own[slot - 1].astype(F32) if slot <= CAP else jnp.zeros((CH, COLS), F32)
    if slot == 1:
        return base
    under = below[0].astype(F32)
    return jnp.where(slot - 1 < live, base, jnp.where(slot - 1 == live, under, 0.0))


def patch_body(live_ref, own, above, below, out, wide):
    live = live_ref[0, 0]

    def put(tap, r, value):
        start = tap * CH
        while start < (tap + 1) * CH:
            frame = start // SHARD
            stop = min((frame + 1) * SHARD, (tap + 1) * CH)
            wide[r, start + 12 * frame : stop + 12 * frame, :] = value[
                start - tap * CH : stop - tap * CH
            ]
            start = stop

    for frame in range(16):
        first = frame * WIDE + SHARD
        wide[:, first : first + 12, :] = jnp.zeros((CAP, 12, COLS), F32)
    for slot in range(CAP + 2):
        store_taps(framed_row(slot, own, above, below, live), put, slot, False)
    for r in range(CAP):
        out[:, r * COLS : (r + 1) * COLS] = wide[r].astype(BF)


def patches(live, own, above, below):
    return call(
        patch_body,
        shape((DEEP, CAP * COLS), BF),
        [SMEM, VMEM, VMEM, VMEM],
        [pltpu.VMEM((CAP, DEEP, COLS), F32)],
        out_specs=VMEM,
        cost=8,
        room=30,
    )(live, own, above, below)


def one_hot():
    channel = lax.broadcasted_iota(jnp.int32, (CH, COLS), 0)
    lane = lax.broadcasted_iota(jnp.int32, (CH, COLS), 1) * PER
    return jnp.where((channel >= lane) & (channel < lane + PER), 1.0, 0.0)


def to_groups(column, hot):
    return jnp.sum(column * hot, axis=0, keepdims=True)


def from_groups(row, hot):
    return jnp.broadcast_to(jnp.sum(row * hot, axis=1, keepdims=True), (CH, COLS))


def forward_body(live_ref, mine, other, patch, mixed, weight, message):
    step = pl.program_id(0)

    @pl.when(step == 0)
    def _():
        left = lax.broadcasted_iota(jnp.int32, (ROWS, COLS), 1) < 64
        for half, source in ((0, mine), (1, other)):
            side = (spot("core") + half) % 2
            for y in range(4):
                base = pl.multiple_of(side * 160 + y * ROWS, 8)
                for pair in range(8):
                    even, odd = source[y, 2 * pair], source[y, 2 * pair + 1]
                    middle = jnp.where(left, even[:, 128:].astype(F32), odd[:, :128].astype(F32))
                    at = pair * 384
                    weight[pl.ds(base, ROWS), at : at + 128] = even[:, :128]
                    weight[pl.ds(base, ROWS), at + 128 : at + 256] = middle.astype(BF)
                    weight[pl.ds(base, ROWS), at + 256 : at + 384] = odd[:, 128:]

    block = jnp.dot(weight[...], patch[...], preferred_element_type=F32)
    mixed[2 * step] = block[:, :128]
    mixed[2 * step + 1] = block[:, 128:]

    @pl.when(step == 3)
    def _():
        live = live_ref[0, 0]
        hot = one_hot()
        total = jnp.zeros((CH, COLS), F32)
        for r in range(CAP):
            total = total + jnp.where(r < live, mixed[r], 0.0)
        column = jnp.broadcast_to(jnp.sum(total, axis=1, keepdims=True), (CH, COLS))
        sums = to_groups(column, hot)
        count = live.astype(F32) * (COLS * PER)
        mean = from_groups(sums / count, hot)
        square = jnp.zeros((CH, COLS), F32)
        for r in range(CAP):
            away = mixed[r] - mean
            square = square + jnp.where(r < live, away * away, 0.0)
        column = jnp.broadcast_to(jnp.sum(square, axis=1, keepdims=True), (CH, COLS))
        squares = to_groups(column, hot)
        line = lax.broadcasted_iota(jnp.int32, (8, COLS), 0)
        note = jnp.where(line == 0, sums, jnp.where(line == 1, squares, count))
        for tile in range(32):
            message[tile] = note


def forward(live, mine, other, patch):
    whole = lambda *dims: pl.BlockSpec(dims, lambda i: (0,) * len(dims))
    return call(
        forward_body,
        (shape((CAP, CH, COLS)), shape((CH, DEEP), BF), shape((32, 8, COLS))),
        [
            SMEM,
            whole(4, 16, ROWS, LANES),
            whole(4, 16, ROWS, LANES),
            pl.BlockSpec((DEEP, 256), lambda i: (0, i)),
        ],
        grid=(4,),
        out_specs=(whole(CAP, CH, COLS), whole(CH, DEEP), whole(32, 8, COLS)),
        cost=6,
        room=24,
    )(live, mine, other, patch)


def to_row(value, spare):
    spare[...] = jnp.zeros(spare.shape, F32)
    spare[0:CH, :] = value
    return jnp.sum(jnp.transpose(spare[...]), axis=0, keepdims=True)


def norm_body(
    live_ref, stats, mixed, upstream, gain, bias, active, dshift, moments, message, sums, spare
):
    live = live_ref[0, 0]
    hot = one_hot()
    part, square, count = stats[:, 0, :], stats[:, 1, :], stats[:, 2, :]
    mean_row = jnp.sum(part, axis=0, keepdims=True) * (1.0 / POPULATION)
    offset = part / count - mean_row
    spread = jnp.sum(square + count * offset * offset, axis=0, keepdims=True)
    inverse_row = lax.rsqrt(spread * (1.0 / POPULATION) + 1e-05)
    moments[0] = from_groups(mean_row, hot)
    moments[1] = from_groups(inverse_row, hot)
    sums[...] = jnp.zeros(sums.shape, F32)

    def row(r, carry):
        alive = r < live
        for part in range(8):
            at = pl.ds(part * ROWS, ROWS)
            normed = (mixed[r, at, :] - moments[0, at, :]) * moments[1, at, :]
            shifted = normed * gain[at, :] + bias[at, :]
            gate = jax.nn.sigmoid(shifted)
            active[r, at, :] = jnp.where(alive, shifted * gate, 0.0).astype(BF)
            above = upstream[r, at, :].astype(F32)
            change = jnp.where(alive, above * gate * (1.0 + shifted * (1.0 - gate)), 0.0)
            dshift[r, at, :] = change
            sums[0, at, :] += change * normed
            sums[1, at, :] += change
        return carry

    lax.fori_loop(0, CAP, row, 0)
    gain_row = to_row(sums[0], spare)
    bias_row = to_row(sums[1], spare)
    line = lax.broadcasted_iota(jnp.int32, (8, 384), 0)
    note = jnp.where(line == 0, gain_row, bias_row)
    for tile in range(32):
        message[tile] = note[0:2]


def normalize(live, stats, mixed, upstream, gain, bias):
    return call(
        norm_body,
        (
            shape((CAP, CH, COLS), BF),
            shape((CAP, CH, COLS)),
            shape((2, CH, COLS)),
            shape((32, 2, 384)),
        ),
        [SMEM] + [VMEM] * 5,
        [pltpu.VMEM((2, CH, COLS), F32), pltpu.VMEM((384, COLS), F32)],
        out_specs=(VMEM,) * 4,
        cost=4,
    )(live, stats, mixed, upstream, gain, bias)


def to_column(row):
    return jnp.transpose(jnp.broadcast_to(row, (COLS, 384)))[:CH]


def grad_body(
    live_ref, notes, mixed, dshift, moments, gain, patch, pre, keep, send, riders, field
):
    step = pl.program_id(0)
    core = spot("core")

    @pl.when(step == 0)
    def _():
        live = live_ref[0, 0]
        hot = one_hot()
        totals = jnp.sum(notes[...], axis=0)
        gain_total = to_column(totals[0:1])
        bias_total = to_column(totals[1:2])
        lane = lax.broadcasted_iota(jnp.int32, (CH, COLS), 1)
        gain_high = gain_total.astype(BF).astype(F32)
        bias_high = bias_total.astype(BF).astype(F32)
        packed = jnp.where(lane == 0, gain_high, jnp.where(lane == 1, gain_total - gain_high, 0.0))
        packed = jnp.where(lane == 2, bias_high, packed)
        riders[...] = jnp.where(lane == 3, bias_total - bias_high, packed)
        share = 1.0 / POPULATION
        delta = from_groups(to_groups(bias_total * gain[...], hot) * share, hot)
        cross = from_groups(to_groups(gain_total * gain[...], hot) * share, hot)
        for r in range(CAP):
            normed = (mixed[r] - moments[0]) * moments[1]
            value = moments[1] * (dshift[r] * gain[...] - delta - normed * cross)
            value = jnp.where(r < live, value, 0.0).astype(BF)
            pre[r] = value
            field[:, r * COLS : (r + 1) * COLS] = value

    block = lax.dot_general(
        field[...], patch[...], (((1,), (1,)), ((), ())), preferred_element_type=F32
    )

    def write(target, side):
        for y in range(4):
            rows = block[side * 160 + y * ROWS : side * 160 + (y + 1) * ROWS]
            for local_frame in range(4):
                at = (local_frame // 2) * 384 + (local_frame % 2) * 128
                target[y, local_frame] = rows[:, at : at + LANES].astype(BF)

    @pl.when(core == 0)
    def _():
        write(keep, 0)
        write(send, 1)

    @pl.when(core == 1)
    def _():
        write(keep, 1)
        write(send, 0)


def gradients(live, notes, mixed, dshift, moments, gain, patch):
    whole = lambda *dims: pl.BlockSpec(dims, lambda i: (0,) * len(dims))
    halves = pl.BlockSpec((4, 4, ROWS, LANES), lambda i: (0, i, 0, 0))
    return call(
        grad_body,
        (
            shape((CAP, CH, COLS), BF),
            shape((4, 16, ROWS, LANES), BF),
            shape((4, 16, ROWS, LANES), BF),
            shape((CH, COLS)),
        ),
        [
            SMEM,
            whole(32, 2, 384),
            whole(CAP, CH, COLS),
            whole(CAP, CH, COLS),
            whole(2, CH, COLS),
            whole(CH, COLS),
            pl.BlockSpec((768, CAP * COLS), lambda i: (i, 0)),
        ],
        [pltpu.VMEM((CH, CAP * COLS), BF)],
        grid=(4,),
        out_specs=(whole(CAP, CH, COLS), halves, halves, whole(CH, COLS)),
        cost=7,
        room=24,
    )(live, notes, mixed, dshift, moments, gain, patch)


def quad_body(quads, riders, out):
    piece = spot("core") * 4 + spot("y")
    lane = lax.broadcasted_iota(jnp.int32, (ROWS, COLS), 1)
    ride = riders[pl.ds(pl.multiple_of(piece * ROWS, 8), ROWS), :]
    ride = jnp.where(spot("x") == 0, ride, 0.0)
    even = pltpu.roll(ride, SHARD - 128, 1)
    odd = pltpu.roll(ride, SHARD - 64, 1)
    for frame in range(16):
        total = quads[0, frame].astype(F32)
        for y in range(1, 4):
            total = total + quads[y, frame].astype(F32)
        first = SHARD - 128 if frame % 2 == 0 else SHARD - 64
        moved = even if frame % 2 == 0 else odd
        inside = (lane >= first) & (lane < first + 4)
        out[frame, :, 0:128] = total[:, :128].astype(BF)
        out[frame, :, 128:256] = jnp.where(inside, moved, total[:, 128:]).astype(BF)


def quad_sum(quads, riders):
    return call(
        quad_body, shape((16, ROWS, LANES), BF), [VMEM, VMEM], out_specs=VMEM
    )(quads, riders)


def frame_body(frames, out):
    total = frames[0].astype(F32)
    for frame in range(1, 16):
        total = total + frames[frame].astype(F32)
    first = SHARD + 64 * (spot("fsdp") % 2)
    lane = lax.broadcasted_iota(jnp.int32, (ROWS, LANES), 1)
    after = pltpu.roll(total, LANES - 1, 1)
    before = pltpu.roll(total, 1, 1)
    both = jnp.where((lane == first) | (lane == first + 2), total + after, total + before)
    high = both.astype(BF).astype(F32)
    riding = (lane >= first) & (lane < first + 4)
    leads = (lane == first) | (lane == first + 2)
    value = jnp.where(riding, jnp.where(leads, high, both - high), total).astype(BF)
    for tile in range(32):
        out[tile] = value


def frame_sum(frames):
    return call(frame_body, shape((32, ROWS, LANES), BF), [VMEM], out_specs=VMEM)(frames)


def adam_body(
    tiles, master, first, second, grad, weight_out, first_out, second_out, gain, bias, square
):
    for core in range(2):
        for y in range(4):
            total = tiles[y * 8 + core].astype(F32)
            for x in range(1, 4):
                total = total + tiles[y * 8 + x * 2 + core].astype(F32)
            at = (core * 4 + y) * ROWS
            square[at : at + ROWS, :] = total
    square[CH:, :] = jnp.zeros((64, LANES), F32)
    turned = jnp.transpose(square[...])[:, :CH] * SCALE
    odd = (spot("fsdp") % 2) == 1
    rows = jnp.where(odd, turned[64:256], turned[0:192])
    gain[...] = rows[SHARD : SHARD + 1] + rows[SHARD + 1 : SHARD + 2]
    bias[...] = rows[SHARD + 2 : SHARD + 3] + rows[SHARD + 3 : SHARD + 4]
    value = rows[:SHARD]
    grad[...] = value
    new_first = 0.9 * first[...] + 0.1 * value
    new_second = 0.999 * second[...] + 0.001 * value * value
    first_out[...] = new_first
    second_out[...] = new_second
    first_fix = new_first / (1.0 - 0.9**10)
    second_fix = new_second / (1.0 - 0.999**10)
    weight_out[...] = master[...] - 0.01 * first_fix / (jnp.sqrt(second_fix) + 1e-08)


def adam(tiles, master, first, second):
    return call(
        adam_body,
        (shape((SHARD, CH)),) * 4 + (shape((1, CH)),) * 2,
        [VMEM] * 4,
        [pltpu.VMEM((384, LANES), F32)],
        out_specs=(VMEM,) * 6,
    )(tiles, master, first, second)


def back_body(live_ref, weight, pre, above, below, out, field, total):
    live = live_ref[0, 0]

    def put(tap, r, value):
        field[tap, :, r * COLS : (r + 1) * COLS] = value.astype(BF)

    for slot in range(CAP + 2):
        store_taps(framed_row(slot, pre, above, below, live), put, slot, True)
    for tap in range(9):
        start = tap * CH
        parts = []
        while start < (tap + 1) * CH:
            frame = start // SHARD
            stop = min((frame + 1) * SHARD, (tap + 1) * CH)
            parts.append(weight[:, start + 12 * frame : stop + 12 * frame])
            start = stop
        left = jnp.concatenate(parts, axis=1)
        block = lax.dot_general(
            left, field[tap], (((0,), (0,)), ((), ())), preferred_element_type=F32
        )
        total[...] = block if tap == 0 else total[...] + block
    for r in range(CAP):
        value = total[:, r * COLS : (r + 1) * COLS]
        out[r] = jnp.where(r < live, value, 0.0).astype(BF)


def back(live, weight, pre, above, below):
    return call(
        back_body,
        shape((CAP, CH, COLS), BF),
        [SMEM] + [VMEM] * 4,
        [pltpu.VMEM((9, CH, CAP * COLS), BF), pltpu.VMEM((CH, CAP * COLS), F32)],
        out_specs=VMEM,
        cost=14,
        room=24,
    )(live, weight, pre, above, below)


def beside(first_row, last_row):
    count = 32
    ends = count - 1
    above = lax.ppermute(last_row, TILE, [(i, (i + 1) % count) for i in range(ends)])
    below = lax.ppermute(first_row, TILE, [((i + 1) % count, i) for i in range(ends)])
    return above, below


def gather_equal(value, axes, count):
    copies = jnp.broadcast_to(value, (count,) + value.shape)
    return lax.all_to_all(copies, axes, 0, 0)


def other_core(value):
    return lax.ppermute(value, "core", [(0, 1), (1, 0)])


def local(
    images, tile_rows, cotangent, master_weight, norm_gain, norm_bias, first_moment, second_moment
):
    live = tile_rows[0, 0]
    own = jnp.swapaxes(images[0, 0], 1, 2)
    upstream = jnp.swapaxes(cotangent[0, 0], 1, 2)
    along_z = lax.all_to_all(pack(master_weight), "fsdp", 0, 0)
    above, below = beside(own[0:1], lax.dynamic_slice_in_dim(own, live - 1, 1, 0))
    patch = patches(tile_rows, own, above, below)
    along_z, patch = lax.optimization_barrier((along_z, patch))
    mine = gather_equal(along_z, "y", 4)
    other = other_core(mine)
    mixed, weight, message = forward(tile_rows, mine, other, patch)
    stats = lax.all_to_all(message, TILE, 0, 0)
    gain = jnp.broadcast_to(norm_gain[:, None], (CH, COLS))
    bias = jnp.broadcast_to(norm_bias[:, None], (CH, COLS))
    active, dshift, moments, note = normalize(tile_rows, stats, mixed, upstream, gain, bias)
    notes = lax.all_to_all(note, TILE, 0, 0)
    pre, keep, send, riders = gradients(tile_rows, notes, mixed, dshift, moments, gain, patch)
    above_grad, below_grad = beside(pre[0:1], lax.dynamic_slice_in_dim(pre, live - 1, 1, 0))
    pair = (keep.astype(F32) + other_core(send).astype(F32)).astype(BF)
    quads = lax.all_to_all(pair, "y", 0, 0)
    frames = lax.all_to_all(quad_sum(quads, riders), "fsdp", 0, 0)
    image_grad = back(tile_rows, weight, pre, above_grad, below_grad)
    tiles = lax.all_to_all(frame_sum(frames), TILE, 0, 0)
    grad, new_weight, new_first, new_second, gain_grad, bias_grad = adam(
        tiles, master_weight, first_moment, second_moment
    )
    return (
        jnp.swapaxes(active, 1, 2)[None, None],
        jnp.swapaxes(image_grad, 1, 2)[None, None],
        grad,
        new_weight,
        new_first,
        new_second,
        gain_grad.reshape(CH),
        bias_grad.reshape(CH),
    )


def solution(mesh):
    fine = Mesh(mesh.devices.reshape(4, 4, 2, 16), ("y", "x", "core", "fsdp"))
    pixels = P("fsdp", TILE, None, None, None)
    rows = P("fsdp", None)
    return jax.shard_map(
        local,
        mesh=fine,
        in_specs=(pixels, P("fsdp", TILE), pixels, rows, P(), P(), rows, rows),
        out_specs=(pixels, pixels, rows, rows, rows, rows, P(), P()),
        check_vma=False,
    )
```

time: 610 us -> 180 us (0.30)
  blocking collectives: 331 us -> 60.4 us
  waiting for transfers between devices: 154 us -> 24.6 us
  local copies, waits for them, and re-layouts: 55.7 us -> 8.33 us
  starting transfers between devices: 23.8 us -> 61.7 us
  Pallas kernels: 0 us -> 21.4 us
  matrix products: 17.4 us -> 0 us
  between operations: 15.7 us -> 1.55 us
  other arithmetic: 11.1 us -> 1.54 us
    psum x4 -> x0, blocking collectives: 298 us -> none  [the longest x1 101 us: local(): lax.psum((jnp.sum(dshift * normed, axis=0), jnp.sum(dshift, axis=0)), ('t...]
    psum x1 -> x0, waiting for transfers between devices: 116 us -> none  [local(): lax.psum(lax.dot_general(columns, pre_grad, (((0,), (0,)), ((), ())), pre...]
    all_to_all x0 -> x4, blocking collectives: none -> 60.4 us  [the longest x1 20.1 us: local(): quads = lax.all_to_all(pair, 'y', 0, 0)]
    all_to_all x0 -> x3, starting transfers between devices: none -> 37.9 us  [the longest x1 15.7 us: local(): along_z = lax.all_to_all(pack(master_weight), 'fsdp', 0, 0)]
    all_gather x1 -> x0, waiting for transfers between devices: 37.7 us -> none  [local(): lax.all_gather(master_weight.astype(jnp.bfloat16), 'fsdp', axis=0, tiled=...]
    unnamed x1 -> x0, blocking collectives: 33.6 us -> none
    pallas_call x0 -> x9, Pallas kernels: none -> 21.4 us  [the longest x1 4.92 us: back(): call(back_body, shape((CAP, CH, COLS), BF), [SMEM] + [VMEM] * 4, [pltpu.V...]
    concatenate x5 -> x0, local copies, waits for them, and re-layouts: 19.3 us -> none  [the longest x4 19.2 us: patches_of(): return jnp.concatenate(pieces, axis=-1).reshape(slot_count * cell_cols, -1)]
  transfers between devices with their start and end apart: 7 -> 9, of which waited for: 2 -> 6; matrix products, arithmetic and copies ran while one was open for 9% -> 0% of each run, Pallas kernels for 0% -> 4%
where the time goes in v2:
time: 180 us
  starting transfers between devices  61.7 us (34%)
  blocking collectives  60.4 us (34%)
  waiting for transfers between devices  24.6 us (14%)
  Pallas kernels  21.4 us (12%)
  local copies, waits for them, and re-layouts  8.33 us (5%)
    all_to_all x1, blocking collectives, local(): quads = lax.all_to_all(pair, 'y', 0, 0)  20.1 us
    all_to_all x1, starting transfers between devices, local(): along_z = lax.all_to_all(pack(master_weight), 'fsdp', 0, 0)  15.7 us
    all_to_all x1, blocking collectives, gather_equal(): return lax.all_to_all(copies, axes, 0, 0)  15.1 us
    all_to_all x1, blocking collectives, local(): stats = lax.all_to_all(message, TILE, 0, 0)  14.2 us
    ppermute x2, starting transfers between devices, other_core(): return lax.ppermute(value, 'core', [(0, 1), (1, 0)])  12.3 us
    all_to_all x1, starting transfers between devices, local(): tiles = lax.all_to_all(frame_sum(frames), TILE, 0, 0)  11.2 us
    all_to_all x1, blocking collectives, local(): notes = lax.all_to_all(note, TILE, 0, 0)  11 us
    all_to_all x1, starting transfers between devices, local(): frames = lax.all_to_all(quad_sum(quads, riders), 'fsdp', 0, 0)  11 us
  transfers between devices with their start and end apart: 9, of which 6 were waited for; matrix products, arithmetic and copies ran while one was open for 0% of the time, Pallas kernels for 4%

profile of v2, /device:TPU:1, one launch (start us, length us, event | category | flops | bytes accessed | tf_op | source)
XLA Modules:
  0.0 179.5 jit_solution(3968581661734374202)
XLA Ops:
  0.6 0.0 copy-start
  0.6 0.0 copy-start.2
  0.7 1.0 copy-done.2
  1.7 1.0 shard_map.143
  2.7 15.7 %all-to-all-start = ((bf16[16,40,256]{2,1,0:T(8,128)(2,1)}), bf16[16,40,256]{2,1,0:T(8,128)(2,1)S(1)}, u32[]{:S(2)}, u32[]{:S(2)}) async-start(bf16[16,40,256]{2,1,0:T(8,128)(2,1)} %shard_map.143), calls=%async_computation | async-start | bytes 655360 | tf_op jit(solution)/shard_map/all_to_all | solution.py:497
  19.1 0.0 copy-done
  19.1 4.0 %collective-permute-start = (bf16[1,320,128]{2,1,0:T(8,128)(2,1)S(1)}, bf16[1,320,128]{2,1,0:T(8,128)(2,1)S(1)}, u32[]{:S(2)}, u32[]{:S(2)}) collective-permute-start(bf16[1,320,128]{2,1,0:T(8,128)(2,1)S(1)} %dynamic-slice_bitcast_fusion), channel_id=1, source_target_pairs={{0,16},{16,32},{32,48},{48,64},{64,80},{80,96},{96,112},{112,128},... | collective-permute-start | bytes 245768 | tf_op jit(solution)/shard_map/ppermute | solution.py:477
  23.1 1.9 %collective-permute-start.1 = (bf16[1,320,128]{2,1,0:T(8,128)(2,1)S(1)}, bf16[1,320,128]{2,1,0:T(8,128)(2,1)S(1)}, u32[]{:S(2)}, u32[]{:S(2)}) collective-permute-start(bf16[1,320,128]{2,1,0:T(8,128)(2,1)S(1)} %slice.8), channel_id=1, source_target_pairs={{16,0},{32,16},{48,32},{64,48},{80,64},{96,80},{112,96},{128,112},... | collective-permute-start | bytes 245768 | tf_op jit(solution)/shard_map/ppermute | solution.py:478
  25.0 0.0 collective-permute-done.above
  25.0 3.8 %collective-permute-done.1.below = bf16[1,320,128]{2,1,0:T(8,128)(2,1)S(1)} collective-permute-done((bf16[1,320,128]{2,1,0:T(8,128)(2,1)S(1)}, bf16[1,320,128]{2,1,0:T(8,128)(2,1)S(1)}, u32[]{:S(2)}, u32[]{:S(2)}) %collective-permute-start.1) | collective-permute-done | bytes 81952 | tf_op jit(solution)/shard_map/ppermute | solution.py:478
  28.8 1.8 %shard_map.144.patch = bf16[3072,1024]{1,0:T(8,128)(2,1)S(1)} custom-call(s32[1,1]{1,0:T(1,128)S(6)} %copy.16.live_ref, bf16[8,320,128]{2,1,0:T(8,128)(2,1)S(1)} %bitcast.19, bf16[1,320,128]{2,1,0:T(8,128)(2,1)S(1)} %collective-permute-done.above, bf16[1,320,128]{2,1,0:T(8,128)(2,1)S(1)} %collective-permute-done.1.below), custom_call_target="tpu_custom_call" | custom-call | flops 8000000000 | bytes 16777216 | tf_op jit(solution)/shard_map/pallas_call | solution.py:123
  30.7 0.0 copy-start.6
  30.7 2.6 %copy-done.6 = bf16[3072,1024]{1,0:T(8,128)(2,1)} copy-done((bf16[3072,1024]{1,0:T(8,128)(2,1)}, bf16[3072,1024]{1,0:T(8,128)(2,1)S(1)}, u32[]{:S(2)}) %copy-start.6) | copy-done | bytes 6291480
  33.3 0.3 all-to-all-done
  33.6 0.1 broadcast_in_dim.10
  33.7 0.0 copy-start.10
  33.7 0.0 copy-start.11
  33.7 15.1 %all_to_all.35.mine = bf16[4,16,40,256]{3,2,1,0:T(8,128)(2,1)S(1)} all-to-all(bf16[4,16,40,256]{3,2,1,0:T(8,128)(2,1)S(1)} %broadcast_in_dim.10), channel_id=1, replica_groups=mesh['y'=4,'x'=4,'core'=2,'fsdp'=16] {'y'}, dimensions={0} | all-to-all | bytes 2621440 | tf_op jit(solution)/shard_map/all_to_all | solution.py:484
  48.9 10.0 %collective-permute-start.2 = (bf16[4,16,40,256]{3,2,1,0:T(8,128)(2,1)S(1)}, bf16[4,16,40,256]{3,2,1,0:T(8,128)(2,1)S(1)}, u32[]{:S(2)}, u32[]{:S(2)}) collective-permute-start(bf16[4,16,40,256]{3,2,1,0:T(8,128)(2,1)S(1)} %all_to_all.35.mine), channel_id=1, source_target_pairs={{0,16},{16,0},{1,17},{17,1},{2,18},{18,2},{3,19},{19,3},{4,20},{20... | collective-permute-start | bytes 3932168 | tf_op jit(solution)/shard_map/ppermute | solution.py:488
  58.9 2.6 %collective-permute-done.2.other = bf16[4,16,40,256]{3,2,1,0:T(8,128)(2,1)S(1)} collective-permute-done((bf16[4,16,40,256]{3,2,1,0:T(8,128)(2,1)S(1)}, bf16[4,16,40,256]{3,2,1,0:T(8,128)(2,1)S(1)}, u32[]{:S(2)}, u32[]{:S(2)}) %collective-permute-start.2) | collective-permute-done | bytes 1310752 | tf_op jit(solution)/shard_map/ppermute | solution.py:488
  61.5 2.8 %copy-done.7 = bf16[3072,1024]{1,0:T(8,128)(2,1)S(1)} copy-done((bf16[3072,1024]{1,0:T(8,128)(2,1)S(1)}, bf16[3072,1024]{1,0:T(8,128)(2,1)}, u32[]{:S(2)}) %copy-start.7) | copy-done | bytes 6291480
  64.3 4.4 %shard_map.145 = (f32[8,320,128]{2,1,0:T(8,128)S(1)}, bf16[320,3072]{1,0:T(8,128)(2,1)S(1)}, f32[32,8,128]{2,1,0:T(8,128)S(1)}) custom-call(s32[1,1]{1,0:T(1,128)S(6)} %copy.16.live_ref, bf16[4,16,40,256]{3,2,1,0:T(8,128)(2,1)S(1)} %all_to_all.35.mine, bf16[4,16,40,256]{3,2,1,0:T(8,128)(2,1)S(1)} %collective-permute-done.2.other, ...), custom_call_target="tpu_custom_call" | custom-call | flops 6000000000 | bytes 12582912 | tf_op jit(solution)/shard_map/pallas_call | solution.py:195
  68.7 0.0 copy-start.8
  68.7 14.2 %all_to_all.36.stats = f32[32,8,128]{2,1,0:T(8,128)S(1)} all-to-all(f32[32,8,128]{2,1,0:T(8,128)S(1)} %get-tuple-element.29), channel_id=1, replica_groups=mesh['y'=4,'x'=4,'core'=2,'fsdp'=16] {'y','x','core'}, dimensions={0} | all-to-all | bytes 262144 | tf_op jit(solution)/shard_map/all_to_all | solution.py:504
  82.9 0.1 broadcast_in_dim.22.gain
  83.0 0.1 broadcast_in_dim.23.bias
  83.2 1.9 %shard_map.146 = (bf16[8,320,128]{2,1,0:T(8,128)(2,1)}, f32[8,320,128]{2,1,0:T(8,128)S(1)}, f32[2,320,128]{2,1,0:T(8,128)S(1)}, f32[32,2,384]{2,1,0:T(2,128)S(1)}) custom-call(s32[1,1]{1,0:T(1,128)S(6)} %copy.16.live_ref, f32[32,8,128]{2,1,0:T(8,128)S(1)} %all_to_all.36.stats, f32[8,320,128]{2,1,0:T(8,128)S(1)} %get-tuple-element.30.mixed, ...), custom_call_target="tpu_custom_call" | custom-call | flops 4000000000 | bytes 8388608 | tf_op jit(solution)/shard_map/pallas_call | solution.py:256
  85.1 11.0 %all_to_all.37.notes = f32[32,2,384]{2,1,0:T(2,128)S(1)} all-to-all(f32[32,2,384]{2,1,0:T(2,128)S(1)} %get-tuple-element.33), channel_id=1, replica_groups=mesh['y'=4,'x'=4,'core'=2,'fsdp'=16] {'y','x','core'}, dimensions={0} | all-to-all | bytes 196608 | tf_op jit(solution)/shard_map/all_to_all | solution.py:508
  96.1 4.1 %shard_map.147 = (bf16[8,320,128]{2,1,0:T(8,128)(2,1)S(1)}, bf16[4,16,40,256]{3,2,1,0:T(8,128)(2,1)S(1)}, bf16[4,16,40,256]{3,2,1,0:T(8,128)(2,1)S(1)}, f32[320,128]{1,0:T(8,128)S(1)}) custom-call(s32[1,1]{1,0:T(1,128)S(6)} %copy.16.live_ref, f32[32,2,384]{2,1,0:T(2,128)S(1)} %all_to_all.37.notes, f32[8,320,128]{2,1,0:T(8,128)S(1)} %get-tuple-element.30.mixed, ...), custom_call_target="tpu_custom_call" | custom-call | flops 7000000000 | bytes 14680064 | tf_op jit(solution)/shard_map/pallas_call | solution.py:329
  100.2 2.3 %collective-permute-start.5 = (bf16[4,16,40,256]{3,2,1,0:T(8,128)(2,1)S(1)}, bf16[4,16,40,256]{3,2,1,0:T(8,128)(2,1)S(1)}, u32[]{:S(2)}, u32[]{:S(2)}) collective-permute-start(bf16[4,16,40,256]{3,2,1,0:T(8,128)(2,1)S(1)} %get-tuple-element.38), channel_id=1, source_target_pairs={{0,16},{16,0},{1,17},{17,1},{2,18},{18,2},{3,19},{19,3},{4,20},{20... | collective-permute-start | bytes 3932168 | tf_op jit(solution)/shard_map/ppermute | solution.py:488
  102.5 2.6 %collective-permute-done.5 = bf16[4,16,40,256]{3,2,1,0:T(8,128)(2,1)S(1)} collective-permute-done((bf16[4,16,40,256]{3,2,1,0:T(8,128)(2,1)S(1)}, bf16[4,16,40,256]{3,2,1,0:T(8,128)(2,1)S(1)}, u32[]{:S(2)}, u32[]{:S(2)}) %collective-permute-start.5) | collective-permute-done | bytes 1310752 | tf_op jit(solution)/shard_map/ppermute | solution.py:488
  105.1 0.4 add_convert_fusion
  105.5 20.1 %all_to_all.38.quads = bf16[4,16,40,256]{3,2,1,0:T(8,128)(2,1)S(1)} all-to-all(bf16[4,16,40,256]{3,2,1,0:T(8,128)(2,1)S(1)} %add_convert_fusion), channel_id=1, replica_groups=mesh['y'=4,'x'=4,'core'=2,'fsdp'=16] {'y'}, dimensions={0} | all-to-all | bytes 2621440 | tf_op jit(solution)/shard_map/all_to_all | solution.py:512
  125.6 0.9 shard_map.149
  126.5 11.0 %all-to-all-start.5 = ((bf16[16,40,256]{2,1,0:T(8,128)(2,1)}), bf16[16,40,256]{2,1,0:T(8,128)(2,1)S(1)}, u32[]{:S(2)}, u32[]{:S(2)}) async-start(bf16[16,40,256]{2,1,0:T(8,128)(2,1)} %shard_map.149), calls=%async_computation.5 | async-start | bytes 655360 | tf_op jit(solution)/shard_map/all_to_all | solution.py:513
  137.6 3.4 %collective-permute-start.4 = (bf16[1,320,128]{2,1,0:T(8,128)(2,1)S(1)}, bf16[1,320,128]{2,1,0:T(8,128)(2,1)S(1)}, u32[]{:S(2)}, u32[]{:S(2)}) collective-permute-start(bf16[1,320,128]{2,1,0:T(8,128)(2,1)S(1)} %get-tuple-element.46), channel_id=1, source_target_pairs={{16,0},{32,16},{48,32},{64,48},{80,64},{96,80},{112,96},{128,112},... | collective-permute-start | bytes 245768 | tf_op jit(solution)/shard_map/ppermute | solution.py:478
  141.0 2.2 %collective-permute-start.3 = (bf16[1,320,128]{2,1,0:T(8,128)(2,1)S(1)}, bf16[1,320,128]{2,1,0:T(8,128)(2,1)S(1)}, u32[]{:S(2)}, u32[]{:S(2)}) collective-permute-start(bf16[1,320,128]{2,1,0:T(8,128)(2,1)S(1)} %get-tuple-element.47), channel_id=1, source_target_pairs={{0,16},{16,32},{32,48},{48,64},{64,80},{80,96},{96,112},{112,128},... | collective-permute-start | bytes 245768 | tf_op jit(solution)/shard_map/ppermute | solution.py:477
  143.1 8.7 %all-to-all-done.5.frames = bf16[16,40,256]{2,1,0:T(8,128)(2,1)S(1)} async-done(((bf16[16,40,256]{2,1,0:T(8,128)(2,1)}), bf16[16,40,256]{2,1,0:T(8,128)(2,1)S(1)}, u32[]{:S(2)}, u32[]{:S(2)}) %all-to-all-start.5) | async-done | bytes 327712 | tf_op jit(solution)/shard_map/all_to_all | solution.py:513
  151.8 1.0 shard_map.150
  152.8 11.2 %all-to-all-start.6 = ((bf16[32,40,256]{2,1,0:T(8,128)(2,1)}), bf16[32,40,256]{2,1,0:T(8,128)(2,1)S(1)}, u32[]{:S(2)}, u32[]{:S(2)}) async-start(bf16[32,40,256]{2,1,0:T(8,128)(2,1)} %shard_map.150), calls=%async_computation.6 | async-start | bytes 1310720 | tf_op jit(solution)/shard_map/all_to_all | solution.py:515
  164.0 0.0 collective-permute-done.4.below
  164.0 0.0 collective-permute-done.3.above
  164.0 1.5 copy-done.9
  165.6 4.9 %shard_map.148 = bf16[8,320,128]{2,1,0:T(8,128)(2,1)} custom-call(s32[1,1]{1,0:T(1,128)S(6)} %copy.16.live_ref, bf16[320,3072]{1,0:T(8,128)(2,1)S(1)} %copy-done.9, bf16[8,320,128]{2,1,0:T(8,128)(2,1)S(1)} %get-tuple-element.36.pre, bf16[1,320,128]{2,1,0:T(8,128)(2,1)S(1)} %collective-permute-done.3.above, bf16[1,320,128]{2,1,0:T(8,128)(2,1)S(1)} %collective-permute-done.4.below), custom_call_target="tpu_custom_call" | custom-call | flops 14000000000 | bytes 29360128 | tf_op jit(solution)/shard_map/pallas_call | solution.py:463
  170.5 6.5 %all-to-all-done.6.tiles = bf16[32,40,256]{2,1,0:T(8,128)(2,1)S(1)} async-done(((bf16[32,40,256]{2,1,0:T(8,128)(2,1)}), bf16[32,40,256]{2,1,0:T(8,128)(2,1)S(1)}, u32[]{:S(2)}, u32[]{:S(2)}) %all-to-all-start.6) | async-done | bytes 655392 | tf_op jit(solution)/shard_map/all_to_all | solution.py:515
  177.0 1.3 shard_map.151
  178.3 0.6 reduce
  178.9 0.6 reduce.1
  (16 shorter events, 0.1 us)
Async XLA Ops:
  0.6 18.4 %copy-start = (bf16[1,1,8,128,320]{3,4,2,1,0:T(8,128)(2,1)S(1)}, bf16[1,1,8,128,320]{3,4,2,1,0:T(8,128)(2,1)}, u32[]{:S(2)}) copy-start(bf16[1,1,8,128,320]{3,4,2,1,0:T(8,128)(2,1)} %param.8) | copy-start | bytes 1966084
  0.6 1.0 copy-start.2
  2.7 31.0 %all-to-all-start = ((bf16[16,40,256]{2,1,0:T(8,128)(2,1)}), bf16[16,40,256]{2,1,0:T(8,128)(2,1)S(1)}, u32[]{:S(2)}, u32[]{:S(2)}) async-start(bf16[16,40,256]{2,1,0:T(8,128)(2,1)} %shard_map.143), calls=%async_computation | async-start | bytes 655360 | tf_op jit(solution)/shard_map/all_to_all | solution.py:497
  19.1 5.9 %collective-permute-start = (bf16[1,320,128]{2,1,0:T(8,128)(2,1)S(1)}, bf16[1,320,128]{2,1,0:T(8,128)(2,1)S(1)}, u32[]{:S(2)}, u32[]{:S(2)}) collective-permute-start(bf16[1,320,128]{2,1,0:T(8,128)(2,1)S(1)} %dynamic-slice_bitcast_fusion), channel_id=1, source_target_pairs={{0,16},{16,32},{32,48},{48,64},{64,80},{80,96},{96,112},{112,128},... | collective-permute-start | bytes 245768 | tf_op jit(solution)/shard_map/ppermute | solution.py:477
  23.1 5.8 %collective-permute-start.1 = (bf16[1,320,128]{2,1,0:T(8,128)(2,1)S(1)}, bf16[1,320,128]{2,1,0:T(8,128)(2,1)S(1)}, u32[]{:S(2)}, u32[]{:S(2)}) collective-permute-start(bf16[1,320,128]{2,1,0:T(8,128)(2,1)S(1)} %slice.8), channel_id=1, source_target_pairs={{16,0},{32,16},{48,32},{64,48},{80,64},{96,80},{112,96},{128,112},... | collective-permute-start | bytes 245768 | tf_op jit(solution)/shard_map/ppermute | solution.py:478
  30.7 2.7 %copy-start.6 = (bf16[3072,1024]{1,0:T(8,128)(2,1)}, bf16[3072,1024]{1,0:T(8,128)(2,1)S(1)}, u32[]{:S(2)}) copy-start(bf16[3072,1024]{1,0:T(8,128)(2,1)S(1)} %shard_map.144.patch) | copy-start | bytes 18874372
  33.7 49.2 %copy-start.10 = (f32[320]{0:T(512)S(1)}, f32[320]{0:T(512)}, u32[]{:S(2)}) copy-start(f32[320]{0:T(512)} %param.12) | copy-start | bytes 3844
  33.7 49.3 %copy-start.11 = (f32[320]{0:T(512)S(1)}, f32[320]{0:T(512)}, u32[]{:S(2)}) copy-start(f32[320]{0:T(512)} %param.13) | copy-start | bytes 3844
  48.9 34.3 %copy-start.1 = (bf16[1,1,8,128,320]{3,4,2,1,0:T(8,128)(2,1)S(1)}, bf16[1,1,8,128,320]{3,4,2,1,0:T(8,128)(2,1)}, u32[]{:S(2)}) copy-start(bf16[1,1,8,128,320]{3,4,2,1,0:T(8,128)(2,1)} %param.10) | copy-start | bytes 1966084
  48.9 12.6 %collective-permute-start.2 = (bf16[4,16,40,256]{3,2,1,0:T(8,128)(2,1)S(1)}, bf16[4,16,40,256]{3,2,1,0:T(8,128)(2,1)S(1)}, u32[]{:S(2)}, u32[]{:S(2)}) collective-permute-start(bf16[4,16,40,256]{3,2,1,0:T(8,128)(2,1)S(1)} %all_to_all.35.mine), channel_id=1, source_target_pairs={{0,16},{16,0},{1,17},{17,1},{2,18},{18,2},{3,19},{19,3},{4,20},{20... | collective-permute-start | bytes 3932168 | tf_op jit(solution)/shard_map/ppermute | solution.py:488
  61.5 2.8 %copy-start.7 = (bf16[3072,1024]{1,0:T(8,128)(2,1)S(1)}, bf16[3072,1024]{1,0:T(8,128)(2,1)}, u32[]{:S(2)}) copy-start(bf16[3072,1024]{1,0:T(8,128)(2,1)} %copy-done.6) | copy-start | bytes 18874372
  68.7 16.3 %copy-start.8 = (bf16[320,3072]{1,0:T(8,128)(2,1)}, bf16[320,3072]{1,0:T(8,128)(2,1)S(1)}, u32[]{:S(2)}) copy-start(bf16[320,3072]{1,0:T(8,128)(2,1)S(1)} %get-tuple-element.32.weight) | copy-start | bytes 5898244
  100.2 5.0 %collective-permute-start.5 = (bf16[4,16,40,256]{3,2,1,0:T(8,128)(2,1)S(1)}, bf16[4,16,40,256]{3,2,1,0:T(8,128)(2,1)S(1)}, u32[]{:S(2)}, u32[]{:S(2)}) collective-permute-start(bf16[4,16,40,256]{3,2,1,0:T(8,128)(2,1)S(1)} %get-tuple-element.38), channel_id=1, source_target_pairs={{0,16},{16,0},{1,17},{17,1},{2,18},{18,2},{3,19},{19,3},{4,20},{20... | collective-permute-start | bytes 3932168 | tf_op jit(solution)/shard_map/ppermute | solution.py:488
  126.5 25.3 %all-to-all-start.5 = ((bf16[16,40,256]{2,1,0:T(8,128)(2,1)}), bf16[16,40,256]{2,1,0:T(8,128)(2,1)S(1)}, u32[]{:S(2)}, u32[]{:S(2)}) async-start(bf16[16,40,256]{2,1,0:T(8,128)(2,1)} %shard_map.149), calls=%async_computation.5 | async-start | bytes 655360 | tf_op jit(solution)/shard_map/all_to_all | solution.py:513
  137.6 26.4 %collective-permute-start.4 = (bf16[1,320,128]{2,1,0:T(8,128)(2,1)S(1)}, bf16[1,320,128]{2,1,0:T(8,128)(2,1)S(1)}, u32[]{:S(2)}, u32[]{:S(2)}) collective-permute-start(bf16[1,320,128]{2,1,0:T(8,128)(2,1)S(1)} %get-tuple-element.46), channel_id=1, source_target_pairs={{16,0},{32,16},{48,32},{64,48},{80,64},{96,80},{112,96},{128,112},... | collective-permute-start | bytes 245768 | tf_op jit(solution)/shard_map/ppermute | solution.py:478
  141.0 23.0 %collective-permute-start.3 = (bf16[1,320,128]{2,1,0:T(8,128)(2,1)S(1)}, bf16[1,320,128]{2,1,0:T(8,128)(2,1)S(1)}, u32[]{:S(2)}, u32[]{:S(2)}) collective-permute-start(bf16[1,320,128]{2,1,0:T(8,128)(2,1)S(1)} %get-tuple-element.47), channel_id=1, source_target_pairs={{0,16},{16,32},{32,48},{48,64},{64,80},{80,96},{96,112},{112,128},... | collective-permute-start | bytes 245768 | tf_op jit(solution)/shard_map/ppermute | solution.py:477
  152.8 24.2 %all-to-all-start.6 = ((bf16[32,40,256]{2,1,0:T(8,128)(2,1)}), bf16[32,40,256]{2,1,0:T(8,128)(2,1)S(1)}, u32[]{:S(2)}, u32[]{:S(2)}) async-start(bf16[32,40,256]{2,1,0:T(8,128)(2,1)} %shard_map.150), calls=%async_computation.6 | async-start | bytes 1310720 | tf_op jit(solution)/shard_map/all_to_all | solution.py:515
  164.0 1.5 copy-start.9
  165.6 11.4 %copy-start.3 = (f32[180,320]{1,0:T(8,128)S(1)}, f32[180,320]{1,0:T(8,128)}, u32[]{:S(2)}) copy-start(f32[180,320]{1,0:T(8,128)} %master.1) | copy-start | bytes 691204
  165.6 11.4 %copy-start.4 = (f32[180,320]{1,0:T(8,128)S(1)}, f32[180,320]{1,0:T(8,128)}, u32[]{:S(2)}) copy-start(f32[180,320]{1,0:T(8,128)} %first.1) | copy-start | bytes 691204
  165.6 11.4 %copy-start.5 = (f32[180,320]{1,0:T(8,128)S(1)}, f32[180,320]{1,0:T(8,128)}, u32[]{:S(2)}) copy-start(f32[180,320]{1,0:T(8,128)} %second.1) | copy-start | bytes 691204

commit v3 on v2

--- a/solution.py
+++ b/solution.py
@@ -48,26 +48,75 @@
     return jax.ShapeDtypeStruct(dims, kind)
 
 
-def pack_body(weight, out, padded, turned):
+def compact(main, rest):
+    left = lax.broadcasted_iota(jnp.int32, (8, COLS), 1) < 64
+    tiles = [main(group) for group in range(5)]
+    for low in (0, 2):
+        tiles.append(jnp.where(left, rest(low, 0), rest(low + 1, 1)))
+    tiles.append(jnp.where(left, rest(4, 0), 0.0))
+    return tiles
+
+
+def pack_body(weight, out, padded, turned, tight):
     padded[...] = jnp.zeros(padded.shape, F32)
     padded[0:SHARD, 0:CH] = weight[...]
     turned[...] = jnp.transpose(padded[...])
     piece = spot("core") * 4 + spot("y")
     rows = turned[pl.ds(pl.multiple_of(piece * ROWS, 8), ROWS), :]
     odd = (spot("fsdp") % 2) == 1
-    rows = jnp.where(odd, pltpu.roll(rows, 64, 1), rows).astype(BF)
+
+    def main(group):
+        value = rows[group * 8 : group * 8 + 8, 0:128]
+        return jnp.where(odd, pltpu.roll(value, 64, 1), value)
+
+    def rest(group, side):
+        value = rows[group * 8 : group * 8 + 8, 128:256]
+        return pltpu.roll(value, 64, 1) if side else value
+
+    for index, tile in enumerate(compact(main, rest)):
+        tight[index * 8 : index * 8 + 8] = tile
+    mine = tight[pl.ds(pl.multiple_of(spot("x") * 16, 8), 16), :].astype(BF)
     for frame in range(16):
-        out[frame] = rows
+        out[frame] = mine
 
 
 def pack(weight):
     return call(
         pack_body,
-        shape((16, ROWS, LANES), BF),
+        shape((16, 16, COLS), BF),
         [VMEM],
-        [pltpu.VMEM((256, 384), F32), pltpu.VMEM((384, 256), F32)],
+        [
+            pltpu.VMEM((256, 384), F32),
+            pltpu.VMEM((384, 256), F32),
+            pltpu.VMEM((64, COLS), F32),
+        ],
         out_specs=VMEM,
     )(weight)
+
+
+def edge_body(live_ref, own, token, first_row, last_row):
+    first_row[0] = own[0]
+    last_row[0] = own[live_ref[0, 0] - 1]
+
+
+def edges(live, own, token):
+    return call(
+        edge_body,
+        (shape((1, CH, COLS), BF),) * 2,
+        [SMEM, VMEM, pl.BlockSpec(memory_space=pl.ANY)],
+        out_specs=(VMEM, VMEM),
+    )(live, own, token)
+
+
+def copies_body(value, out):
+    for index in range(out.shape[0]):
+        out[index] = value[...]
+
+
+def copies(value, count):
+    return call(
+        copies_body, shape((count,) + value.shape, value.dtype), [VMEM], out_specs=VMEM
+    )(value)
 
 
 def store_taps(row, field, slot, negate):
@@ -145,25 +194,53 @@
     return jnp.broadcast_to(jnp.sum(row * hot, axis=1, keepdims=True), (CH, COLS))
 
 
-def forward_body(live_ref, mine, other, patch, mixed, weight, message):
+def forward_body(live_ref, mine, other, patch, mixed, weight, message, held, arrived):
     step = pl.program_id(0)
+
+    def block_copy(index):
+        return pltpu.make_async_copy(
+            patch.at[:, index * 256 : (index + 1) * 256], held.at[index], arrived.at[index]
+        )
 
     @pl.when(step == 0)
     def _():
-        left = lax.broadcasted_iota(jnp.int32, (ROWS, COLS), 1) < 64
+        for index in range(4):
+            block_copy(index).start()
+        left = lax.broadcasted_iota(jnp.int32, (8, COLS), 1) < 64
         for half, source in ((0, mine), (1, other)):
             side = (spot("core") + half) % 2
             for y in range(4):
                 base = pl.multiple_of(side * 160 + y * ROWS, 8)
                 for pair in range(8):
-                    even, odd = source[y, 2 * pair], source[y, 2 * pair + 1]
-                    middle = jnp.where(left, even[:, 128:].astype(F32), odd[:, :128].astype(F32))
                     at = pair * 384
-                    weight[pl.ds(base, ROWS), at : at + 128] = even[:, :128]
-                    weight[pl.ds(base, ROWS), at + 128 : at + 256] = middle.astype(BF)
-                    weight[pl.ds(base, ROWS), at + 256 : at + 384] = odd[:, 128:]
-
-    block = jnp.dot(weight[...], patch[...], preferred_element_type=F32)
+
+                    def tile(frame, index):
+                        row = (index % 2) * 8
+                        value = source[y * 4 + index // 2, 2 * pair + frame, row : row + 8, :]
+                        return value.astype(F32)
+
+                    even = [tile(0, index) for index in range(8)]
+                    odd = [tile(1, index) for index in range(8)]
+                    first, middle, last = [], [], []
+                    for group in range(5):
+                        rest = [even[5 + group // 2], odd[5 + group // 2]]
+                        turn = 1 - group % 2
+                        rest[turn] = pltpu.roll(rest[turn], 64, 1)
+                        first.append(even[group])
+                        middle.append(jnp.where(left, rest[0], odd[group]))
+                        last.append(jnp.where(left, odd[group], rest[1]))
+                    for place, parts in ((0, first), (128, middle), (256, last)):
+                        weight[pl.ds(base, ROWS), at + place : at + place + 128] = (
+                            jnp.concatenate(parts, axis=0).astype(BF)
+                        )
+
+    for index in range(4):
+
+        @pl.when(step == index)
+        def _():
+            block_copy(index).wait()
+
+    block = jnp.dot(weight[...], held[step], preferred_element_type=F32)
     mixed[2 * step] = block[:, :128]
     mixed[2 * step + 1] = block[:, 128:]
 
@@ -197,10 +274,11 @@
         (shape((CAP, CH, COLS)), shape((CH, DEEP), BF), shape((32, 8, COLS))),
         [
             SMEM,
-            whole(4, 16, ROWS, LANES),
-            whole(4, 16, ROWS, LANES),
-            pl.BlockSpec((DEEP, 256), lambda i: (0, i)),
+            whole(16, 16, 16, COLS),
+            whole(16, 16, 16, COLS),
+            pl.BlockSpec(memory_space=pltpu.HBM),
         ],
+        [pltpu.VMEM((4, DEEP, 256), BF), pltpu.SemaphoreType.DMA((4,))],
         grid=(4,),
         out_specs=(whole(CAP, CH, COLS), whole(CH, DEEP), whole(32, 8, COLS)),
         cost=6,
@@ -273,13 +351,35 @@
 
 
 def grad_body(
-    live_ref, notes, mixed, dshift, moments, gain, patch, pre, keep, send, riders, field
+    live_ref,
+    notes,
+    mixed,
+    dshift,
+    moments,
+    gain,
+    patch,
+    pre,
+    keep,
+    send,
+    riders,
+    first_row,
+    last_row,
+    field,
+    held,
+    arrived,
 ):
     step = pl.program_id(0)
     core = spot("core")
 
+    def block_copy(index):
+        return pltpu.make_async_copy(
+            patch.at[index * 768 : (index + 1) * 768], held.at[index], arrived.at[index]
+        )
+
     @pl.when(step == 0)
     def _():
+        for index in range(4):
+            block_copy(index).start()
         live = live_ref[0, 0]
         hot = one_hot()
         totals = jnp.sum(notes[...], axis=0)
@@ -300,17 +400,46 @@
             value = jnp.where(r < live, value, 0.0).astype(BF)
             pre[r] = value
             field[:, r * COLS : (r + 1) * COLS] = value
+        first_row[0] = pre[0]
+        last_row[0] = pre[live - 1]
+
+    for index in range(4):
+
+        @pl.when(step == index)
+        def _():
+            block_copy(index).wait()
 
     block = lax.dot_general(
-        field[...], patch[...], (((1,), (1,)), ((), ())), preferred_element_type=F32
+        field[...], held[step], (((1,), (1,)), ((), ())), preferred_element_type=F32
     )
+
+    left = lax.broadcasted_iota(jnp.int32, (8, COLS), 1) < 64
 
     def write(target, side):
         for y in range(4):
-            rows = block[side * 160 + y * ROWS : side * 160 + (y + 1) * ROWS]
-            for local_frame in range(4):
-                at = (local_frame // 2) * 384 + (local_frame % 2) * 128
-                target[y, local_frame] = rows[:, at : at + LANES].astype(BF)
+            base = side * 160 + y * ROWS
+            for frame in range(4):
+                at = (frame // 2) * 384 + (frame % 2) * 128
+                odd = frame % 2
+
+                def part(group, offset):
+                    row = base + group * 8
+                    return block[row : row + 8, at + offset : at + offset + 128]
+
+                def main(group):
+                    if odd:
+                        return jnp.where(left, part(group, 128), part(group, 0))
+                    return part(group, 0)
+
+                def rest(group, place):
+                    value = part(group, 128)
+                    return value if place == odd else pltpu.roll(value, 64, 1)
+
+                tiles = compact(main, rest)
+                for x in range(4):
+                    target[y * 4 + x, frame] = jnp.concatenate(
+                        tiles[2 * x : 2 * x + 2], axis=0
+                    ).astype(BF)
 
     @pl.when(core == 0)
     def _():
@@ -325,14 +454,16 @@
 
 def gradients(live, notes, mixed, dshift, moments, gain, patch):
     whole = lambda *dims: pl.BlockSpec(dims, lambda i: (0,) * len(dims))
-    halves = pl.BlockSpec((4, 4, ROWS, LANES), lambda i: (0, i, 0, 0))
+    halves = pl.BlockSpec((16, 4, 16, COLS), lambda i: (0, i, 0, 0))
     return call(
         grad_body,
         (
             shape((CAP, CH, COLS), BF),
-            shape((4, 16, ROWS, LANES), BF),
-            shape((4, 16, ROWS, LANES), BF),
+            shape((16, 16, 16, COLS), BF),
+            shape((16, 16, 16, COLS), BF),
             shape((CH, COLS)),
+            shape((1, CH, COLS), BF),
+            shape((1, CH, COLS), BF),
         ),
         [
             SMEM,
@@ -341,78 +472,104 @@
             whole(CAP, CH, COLS),
             whole(2, CH, COLS),
             whole(CH, COLS),
-            pl.BlockSpec((768, CAP * COLS), lambda i: (i, 0)),
+            pl.BlockSpec(memory_space=pltpu.HBM),
         ],
-        [pltpu.VMEM((CH, CAP * COLS), BF)],
+        [
+            pltpu.VMEM((CH, CAP * COLS), BF),
+            pltpu.VMEM((4, 768, CAP * COLS), BF),
+            pltpu.SemaphoreType.DMA((4,)),
+        ],
         grid=(4,),
-        out_specs=(whole(CAP, CH, COLS), halves, halves, whole(CH, COLS)),
+        out_specs=(
+            whole(CAP, CH, COLS),
+            halves,
+            halves,
+            whole(CH, COLS),
+            whole(1, CH, COLS),
+            whole(1, CH, COLS),
+        ),
         cost=7,
         room=24,
     )(live, notes, mixed, dshift, moments, gain, patch)
 
 
-def quad_body(quads, riders, out):
+def add_body(keep, passed, out):
+    for index in range(16):
+        out[index] = (keep[index].astype(F32) + passed[index].astype(F32)).astype(BF)
+
+
+def add_pair(keep, passed):
+    return call(
+        add_body, shape((16, 16, 16, COLS), BF), [VMEM, VMEM], out_specs=VMEM
+    )(keep, passed)
+
+
+def plane_body(parts, riders, out):
     piece = spot("core") * 4 + spot("y")
-    lane = lax.broadcasted_iota(jnp.int32, (ROWS, COLS), 1)
-    ride = riders[pl.ds(pl.multiple_of(piece * ROWS, 8), ROWS), :]
-    ride = jnp.where(spot("x") == 0, ride, 0.0)
-    even = pltpu.roll(ride, SHARD - 128, 1)
-    odd = pltpu.roll(ride, SHARD - 64, 1)
+    ride = jnp.zeros((8, COLS), F32)
+    for group in range(5):
+        at = pl.multiple_of(piece * ROWS + group * 8, 8)
+        ride = ride + pltpu.roll(riders[pl.ds(at, 8), :], 64 + 4 * group, 1)
+    ride = jnp.where(spot("x") == 3, ride, 0.0)
+    ride = jnp.concatenate([jnp.zeros((8, COLS), F32), ride], axis=0)
     for frame in range(16):
-        total = quads[0, frame].astype(F32)
-        for y in range(1, 4):
-            total = total + quads[y, frame].astype(F32)
-        first = SHARD - 128 if frame % 2 == 0 else SHARD - 64
-        moved = even if frame % 2 == 0 else odd
-        inside = (lane >= first) & (lane < first + 4)
-        out[frame, :, 0:128] = total[:, :128].astype(BF)
-        out[frame, :, 128:256] = jnp.where(inside, moved, total[:, 128:]).astype(BF)
-
-
-def quad_sum(quads, riders):
-    return call(
-        quad_body, shape((16, ROWS, LANES), BF), [VMEM, VMEM], out_specs=VMEM
-    )(quads, riders)
+        total = parts[0, frame].astype(F32)
+        for part in range(1, 16):
+            total = total + parts[part, frame].astype(F32)
+        out[frame] = (total + ride).astype(BF)
+
+
+def plane_sum(parts, riders):
+    return call(
+        plane_body, shape((16, 16, COLS), BF), [VMEM, VMEM], out_specs=VMEM
+    )(parts, riders)
 
 
 def frame_body(frames, out):
     total = frames[0].astype(F32)
     for frame in range(1, 16):
         total = total + frames[frame].astype(F32)
-    first = SHARD + 64 * (spot("fsdp") % 2)
-    lane = lax.broadcasted_iota(jnp.int32, (ROWS, LANES), 1)
-    after = pltpu.roll(total, LANES - 1, 1)
-    before = pltpu.roll(total, 1, 1)
-    both = jnp.where((lane == first) | (lane == first + 2), total + after, total + before)
+    lane = lax.broadcasted_iota(jnp.int32, (16, COLS), 1)
+    row = lax.broadcasted_iota(jnp.int32, (16, COLS), 0)
+    leads = lane % 2 == 0
+    both = total + jnp.where(leads, pltpu.roll(total, COLS - 1, 1), pltpu.roll(total, 1, 1))
     high = both.astype(BF).astype(F32)
-    riding = (lane >= first) & (lane < first + 4)
-    leads = (lane == first) | (lane == first + 2)
+    riding = (lane >= 64) & (row >= 8) & (spot("x") == 3)
     value = jnp.where(riding, jnp.where(leads, high, both - high), total).astype(BF)
     for tile in range(32):
         out[tile] = value
 
 
 def frame_sum(frames):
-    return call(frame_body, shape((32, ROWS, LANES), BF), [VMEM], out_specs=VMEM)(frames)
+    return call(frame_body, shape((32, 16, COLS), BF), [VMEM], out_specs=VMEM)(frames)
 
 
 def adam_body(
     tiles, master, first, second, grad, weight_out, first_out, second_out, gain, bias, square
 ):
+    odd = (spot("fsdp") % 2) == 1
+    lane = lax.broadcasted_iota(jnp.int32, (8, COLS), 1)
     for core in range(2):
         for y in range(4):
-            total = tiles[y * 8 + core].astype(F32)
-            for x in range(1, 4):
-                total = total + tiles[y * 8 + x * 2 + core].astype(F32)
-            at = (core * 4 + y) * ROWS
-            square[at : at + ROWS, :] = total
+            part = [
+                tiles[y * 8 + (index // 2) * 2 + core, (index % 2) * 8 : (index % 2) * 8 + 8, :]
+                for index in range(8)
+            ]
+            part = [value.astype(F32) for value in part]
+            for group in range(5):
+                at = (core * 4 + y) * ROWS + group * 8
+                main = part[group]
+                rest = part[5 + group // 2]
+                if group % 2:
+                    rest = pltpu.roll(rest, 64, 1)
+                ride = pltpu.roll(part[7], COLS - 4 * group, 1)
+                square[at : at + 8, 0:128] = jnp.where(odd, pltpu.roll(main, 64, 1), main)
+                square[at : at + 8, 128:256] = jnp.where(lane < 64, rest, ride)
     square[CH:, :] = jnp.zeros((64, LANES), F32)
     turned = jnp.transpose(square[...])[:, :CH] * SCALE
-    odd = (spot("fsdp") % 2) == 1
-    rows = jnp.where(odd, turned[64:256], turned[0:192])
-    gain[...] = rows[SHARD : SHARD + 1] + rows[SHARD + 1 : SHARD + 2]
-    bias[...] = rows[SHARD + 2 : SHARD + 3] + rows[SHARD + 3 : SHARD + 4]
-    value = rows[:SHARD]
+    gain[...] = (turned[192:193] + turned[193:194])[0]
+    bias[...] = (turned[194:195] + turned[195:196])[0]
+    value = turned[:SHARD]
     grad[...] = value
     new_first = 0.9 * first[...] + 0.1 * value
     new_second = 0.999 * second[...] + 0.001 * value * value
@@ -426,7 +583,7 @@
 def adam(tiles, master, first, second):
     return call(
         adam_body,
-        (shape((SHARD, CH)),) * 4 + (shape((1, CH)),) * 2,
+        (shape((SHARD, CH)),) * 4 + (shape((CH,)),) * 2,
         [VMEM] * 4,
         [pltpu.VMEM((384, LANES), F32)],
         out_specs=(VMEM,) * 6,
@@ -479,11 +636,6 @@
     return above, below
 
 
-def gather_equal(value, axes, count):
-    copies = jnp.broadcast_to(value, (count,) + value.shape)
-    return lax.all_to_all(copies, axes, 0, 0)
-
-
 def other_core(value):
     return lax.ppermute(value, "core", [(0, 1), (1, 0)])
 
@@ -491,14 +643,15 @@
 def local(
     images, tile_rows, cotangent, master_weight, norm_gain, norm_bias, first_moment, second_moment
 ):
-    live = tile_rows[0, 0]
     own = jnp.swapaxes(images[0, 0], 1, 2)
     upstream = jnp.swapaxes(cotangent[0, 0], 1, 2)
-    along_z = lax.all_to_all(pack(master_weight), "fsdp", 0, 0)
-    above, below = beside(own[0:1], lax.dynamic_slice_in_dim(own, live - 1, 1, 0))
+    packed = pack(master_weight)
+    along_z = lax.all_to_all(packed, "fsdp", 0, 0)
+    above, below = beside(*edges(tile_rows, own, packed))
     patch = patches(tile_rows, own, above, below)
+    patch = pltpu.with_memory_space_constraint(patch, pltpu.HBM)
     along_z, patch = lax.optimization_barrier((along_z, patch))
-    mine = gather_equal(along_z, "y", 4)
+    mine = lax.all_to_all(copies(along_z, 16), ("y", "x"), 0, 0)
     other = other_core(mine)
     mixed, weight, message = forward(tile_rows, mine, other, patch)
     stats = lax.all_to_all(message, TILE, 0, 0)
@@ -506,11 +659,12 @@
     bias = jnp.broadcast_to(norm_bias[:, None], (CH, COLS))
     active, dshift, moments, note = normalize(tile_rows, stats, mixed, upstream, gain, bias)
     notes = lax.all_to_all(note, TILE, 0, 0)
-    pre, keep, send, riders = gradients(tile_rows, notes, mixed, dshift, moments, gain, patch)
-    above_grad, below_grad = beside(pre[0:1], lax.dynamic_slice_in_dim(pre, live - 1, 1, 0))
-    pair = (keep.astype(F32) + other_core(send).astype(F32)).astype(BF)
-    quads = lax.all_to_all(pair, "y", 0, 0)
-    frames = lax.all_to_all(quad_sum(quads, riders), "fsdp", 0, 0)
+    pre, keep, send, riders, pre_first, pre_last = gradients(
+        tile_rows, notes, mixed, dshift, moments, gain, patch
+    )
+    above_grad, below_grad = beside(pre_first, pre_last)
+    parts = lax.all_to_all(add_pair(keep, other_core(send)), ("y", "x"), 0, 0)
+    frames = lax.all_to_all(plane_sum(parts, riders), "fsdp", 0, 0)
     image_grad = back(tile_rows, weight, pre, above_grad, below_grad)
     tiles = lax.all_to_all(frame_sum(frames), TILE, 0, 0)
     grad, new_weight, new_first, new_second, gain_grad, bias_grad = adam(
@@ -523,8 +677,8 @@
         new_weight,
         new_first,
         new_second,
-        gain_grad.reshape(CH),
-        bias_grad.reshape(CH),
+        gain_grad,
+        bias_grad,
     )
 
 

time: 180 us -> 157 us (0.87)
  starting transfers between devices: 61.7 us -> 46.5 us
  waiting for transfers between devices: 24.6 us -> 19.2 us
  local copies, waits for them, and re-layouts: 8.33 us -> 4.9 us
    all_to_all x2, starting transfers between devices: 26.8 us -> 15.6 us  [the longest x1 11.3 us: local(): along_z = lax.all_to_all(packed, 'fsdp', 0, 0)]
    all_to_all x1, waiting for transfers between devices: 6.52 us -> 1.62 us  [local(): tiles = lax.all_to_all(frame_sum(frames), TILE, 0, 0)]
    all_to_all x2, blocking collectives: 35.2 us -> 39.7 us  [the longest x1 20.5 us: local(): mine = lax.all_to_all(copies(along_z, 16), ('y', 'x'), 0, 0)]
    ppermute x2, starting transfers between devices: 12.3 us -> 7.89 us  [other_core(): return lax.ppermute(value, 'core', [(0, 1), (1, 0)])]
    all_to_all x1, starting transfers between devices: 11.2 us -> 6.8 us  [local(): tiles = lax.all_to_all(frame_sum(frames), TILE, 0, 0)]
    all_to_all x2, waiting for transfers between devices: 8.97 us -> 13 us  [the longest x1 7.5 us: local(): along_z = lax.all_to_all(packed, 'fsdp', 0, 0)]
    ppermute x2, waiting for transfers between devices: 3.82 us -> 0.01 us  [beside(): lax.ppermute(first_row, TILE, [((i + 1) % count, i) for i in range(ends)])]
    unnamed x24 -> x22, local copies, waits for them, and re-layouts: 8.02 us -> 4.71 us
  transfers between devices with their start and end apart: 9 -> 9, of which waited for: 6 -> 5; matrix products, arithmetic and copies ran while one was open for 0% -> 0% of each run, Pallas kernels for 4% -> 5%
where the time goes in v3:
time: 157 us
  blocking collectives  61.6 us (39%)
  starting transfers between devices  46.5 us (30%)
  Pallas kernels  23.1 us (15%)
  waiting for transfers between devices  19.2 us (12%)
  local copies, waits for them, and re-layouts  4.9 us (3%)
  between operations  1.57 us (1%)
    all_to_all x1, blocking collectives, local(): mine = lax.all_to_all(copies(along_z, 16), ('y', 'x'), 0, 0)  20.5 us
    all_to_all x1, blocking collectives, local(): parts = lax.all_to_all(add_pair(keep, other_core(send)), ('y', 'x'), 0, 0)  19.2 us
    all_to_all x1, starting transfers between devices, local(): along_z = lax.all_to_all(packed, 'fsdp', 0, 0)  11.3 us
    all_to_all x1, blocking collectives, local(): notes = lax.all_to_all(note, TILE, 0, 0)  11 us
    all_to_all x1, blocking collectives, local(): stats = lax.all_to_all(message, TILE, 0, 0)  10.9 us
    ppermute x2, starting transfers between devices, beside(): lax.ppermute(last_row, TILE, [(i, (i + 1) % count) for i in range(ends)])  8.64 us
    ppermute x2, starting transfers between devices, other_core(): return lax.ppermute(value, 'core', [(0, 1), (1, 0)])  7.89 us
    all_to_all x1, waiting for transfers between devices, local(): along_z = lax.all_to_all(packed, 'fsdp', 0, 0)  7.5 us
  transfers between devices with their start and end apart: 9, of which 5 were waited for; matrix products, arithmetic and copies ran while one was open for 0% of the time, Pallas kernels for 5%

profile of v3, /device:TPU:1, one launch (start us, length us, event | category | flops | bytes accessed | tf_op | source)
XLA Modules:
  0.0 156.8 jit_solution(15208761817489538184)
XLA Ops:
  0.6 0.0 copy-start
  1.4 0.0 copy-start.2
  1.4 0.9 copy-done.2
  2.3 0.9 shard_map.143.token
  3.2 0.0 copy-done
  3.2 4.5 %collective-permute-start = (bf16[1,320,128]{2,1,0:T(8,128)(2,1)S(1)}, bf16[1,320,128]{2,1,0:T(8,128)(2,1)S(1)}, u32[]{:S(2)}, u32[]{:S(2)}) collective-permute-start(bf16[1,320,128]{2,1,0:T(8,128)(2,1)S(1)} %get-tuple-element.31), channel_id=1, source_target_pairs={{0,16},{16,32},{32,48},{48,64},{64,80},{80,96},{96,112},{112,128},... | collective-permute-start | bytes 245768 | tf_op jit(solution)/shard_map/ppermute | solution.py:634
  7.7 5.6 %collective-permute-start.1 = (bf16[1,320,128]{2,1,0:T(8,128)(2,1)S(1)}, bf16[1,320,128]{2,1,0:T(8,128)(2,1)S(1)}, u32[]{:S(2)}, u32[]{:S(2)}) collective-permute-start(bf16[1,320,128]{2,1,0:T(8,128)(2,1)S(1)} %get-tuple-element.32), channel_id=1, source_target_pairs={{16,0},{32,16},{48,32},{64,48},{80,64},{96,80},{112,96},{128,112},... | collective-permute-start | bytes 245768 | tf_op jit(solution)/shard_map/ppermute | solution.py:635
  13.3 11.3 %all-to-all-start = ((bf16[16,16,128]{2,1,0:T(8,128)(2,1)}), bf16[16,16,128]{2,1,0:T(8,128)(2,1)S(1)}, u32[]{:S(2)}, u32[]{:S(2)}) async-start(bf16[16,16,128]{2,1,0:T(8,128)(2,1)} %shard_map.143.token), calls=%async_computation | async-start | bytes 131072 | tf_op jit(solution)/shard_map/all_to_all | solution.py:649
  24.6 0.0 collective-permute-done.above
  24.6 0.0 collective-permute-done.1.below
  24.6 1.8 %shard_map.145.patch = bf16[3072,1024]{1,0:T(8,128)(2,1)S(1)} custom-call(s32[1,1]{1,0:T(1,128)S(6)} %copy.16.live_ref, bf16[8,320,128]{2,1,0:T(8,128)(2,1)S(1)} %bitcast.13, bf16[1,320,128]{2,1,0:T(8,128)(2,1)S(1)} %collective-permute-done.above, bf16[1,320,128]{2,1,0:T(8,128)(2,1)S(1)} %collective-permute-done.1.below), custom_call_target="tpu_custom_call" | custom-call | flops 8000000000 | bytes 16777216 | tf_op jit(solution)/shard_map/pallas_call | solution.py:172
  26.5 0.0 copy-start.6
  26.5 2.6 %copy-done.6 = bf16[3072,1024]{1,0:T(8,128)(2,1)} copy-done((bf16[3072,1024]{1,0:T(8,128)(2,1)}, bf16[3072,1024]{1,0:T(8,128)(2,1)S(1)}, u32[]{:S(2)}) %copy-start.6) | copy-done | bytes 6291480
  29.1 7.5 %all-to-all-done.value = bf16[16,16,128]{2,1,0:T(8,128)(2,1)S(1)} async-done(((bf16[16,16,128]{2,1,0:T(8,128)(2,1)}), bf16[16,16,128]{2,1,0:T(8,128)(2,1)S(1)}, u32[]{:S(2)}, u32[]{:S(2)}) %all-to-all-start) | async-done | bytes 65568 | tf_op jit(solution)/shard_map/all_to_all | solution.py:649
  36.6 0.1 shard_map.146
  36.7 20.5 %all_to_all.35.mine = bf16[16,16,16,128]{3,2,1,0:T(8,128)(2,1)S(1)} all-to-all(bf16[16,16,16,128]{3,2,1,0:T(8,128)(2,1)S(1)} %shard_map.146), channel_id=1, replica_groups=mesh['y'=4,'x'=4,'core'=2,'fsdp'=16] {'y','x'}, dimensions={0} | all-to-all | bytes 2097152 | tf_op jit(solution)/shard_map/all_to_all | solution.py:654
  57.2 5.6 %collective-permute-start.2 = (bf16[16,16,16,128]{3,2,1,0:T(8,128)(2,1)S(1)}, bf16[16,16,16,128]{3,2,1,0:T(8,128)(2,1)S(1)}, u32[]{:S(2)}, u32[]{:S(2)}) collective-permute-start(bf16[16,16,16,128]{3,2,1,0:T(8,128)(2,1)S(1)} %all_to_all.35.mine), channel_id=1, source_target_pairs={{0,16},{16,0},{1,17},{17,1},{2,18},{18,2},{3,19},{19,3},{4,20},{20... | collective-permute-start | bytes 3145736 | tf_op jit(solution)/shard_map/ppermute | solution.py:640
  62.8 2.3 %collective-permute-done.2.other = bf16[16,16,16,128]{3,2,1,0:T(8,128)(2,1)S(1)} collective-permute-done((bf16[16,16,16,128]{3,2,1,0:T(8,128)(2,1)S(1)}, bf16[16,16,16,128]{3,2,1,0:T(8,128)(2,1)S(1)}, u32[]{:S(2)}, u32[]{:S(2)}) %collective-permute-start.2) | collective-permute-done | bytes 1048608 | tf_op jit(solution)/shard_map/ppermute | solution.py:640
  65.1 4.8 %shard_map.147 = (f32[8,320,128]{2,1,0:T(8,128)S(1)}, bf16[320,3072]{1,0:T(8,128)(2,1)S(1)}, f32[32,8,128]{2,1,0:T(8,128)S(1)}) custom-call(s32[1,1]{1,0:T(1,128)S(6)} %copy.16.live_ref, bf16[16,16,16,128]{3,2,1,0:T(8,128)(2,1)S(1)} %all_to_all.35.mine, bf16[16,16,16,128]{3,2,1,0:T(8,128)(2,1)S(1)} %collective-permute-done.2.other, bf16[3072,1024]{1,0:T(8,128)(2,1)} %copy-done.6), custom_call_target="tpu_custom_call" | custom-call | flops 6000000000 | bytes 12582912 | tf_op jit(solution)/shard_map/pallas_call | solution.py:272
  69.9 10.9 %all_to_all.36.stats = f32[32,8,128]{2,1,0:T(8,128)S(1)} all-to-all(f32[32,8,128]{2,1,0:T(8,128)S(1)} %get-tuple-element.35), channel_id=1, replica_groups=mesh['y'=4,'x'=4,'core'=2,'fsdp'=16] {'y','x','core'}, dimensions={0} | all-to-all | bytes 262144 | tf_op jit(solution)/shard_map/all_to_all | solution.py:657
  80.8 0.0 copy-done.9
  80.8 0.1 broadcast_in_dim.8.gain
  80.9 0.0 copy-done.10
  80.9 0.1 broadcast_in_dim.9.bias
  81.0 0.0 copy-done.1
  81.1 1.9 %shard_map.148 = (bf16[8,320,128]{2,1,0:T(8,128)(2,1)}, f32[8,320,128]{2,1,0:T(8,128)S(1)}, f32[2,320,128]{2,1,0:T(8,128)S(1)}, f32[32,2,384]{2,1,0:T(2,128)S(1)}) custom-call(s32[1,1]{1,0:T(1,128)S(6)} %copy.16.live_ref, f32[32,8,128]{2,1,0:T(8,128)S(1)} %all_to_all.36.stats, f32[8,320,128]{2,1,0:T(8,128)S(1)} %get-tuple-element.36.mixed, ...), custom_call_target="tpu_custom_call" | custom-call | flops 4000000000 | bytes 8388608 | tf_op jit(solution)/shard_map/pallas_call | solution.py:334
  83.0 11.0 %all_to_all.37.notes = f32[32,2,384]{2,1,0:T(2,128)S(1)} all-to-all(f32[32,2,384]{2,1,0:T(2,128)S(1)} %get-tuple-element.39), channel_id=1, replica_groups=mesh['y'=4,'x'=4,'core'=2,'fsdp'=16] {'y','x','core'}, dimensions={0} | all-to-all | bytes 196608 | tf_op jit(solution)/shard_map/all_to_all | solution.py:661
  94.0 5.3 %shard_map.149 = (bf16[8,320,128]{2,1,0:T(8,128)(2,1)S(1)}, bf16[16,16,16,128]{3,2,1,0:T(8,128)(2,1)S(1)}, bf16[16,16,16,128]{3,2,1,0:T(8,128)(2,1)S(1)}, f32[32...) custom-call(s32[1,1]{1,0:T(1,128)S(6)} %copy.16.live_ref, ...), custom_call_target="tpu_custom_call" | custom-call | flops 7000000000 | bytes 14680064 | tf_op jit(solution)/shard_map/pallas_call | solution.py:458
  99.4 0.0 copy-start.7
  99.4 2.3 %collective-permute-start.5 = (bf16[16,16,16,128]{3,2,1,0:T(8,128)(2,1)S(1)}, bf16[16,16,16,128]{3,2,1,0:T(8,128)(2,1)S(1)}, u32[]{:S(2)}, u32[]{:S(2)}) collective-permute-start(bf16[16,16,16,128]{3,2,1,0:T(8,128)(2,1)S(1)} %get-tuple-element.46), channel_id=1, source_target_pairs={{0,16},{16,0},{1,17},{17,1},{2,18},{18,2},{3,19},{19,3},{4,20},{20... | collective-permute-start | bytes 3145736 | tf_op jit(solution)/shard_map/ppermute | solution.py:640
  101.7 2.3 %collective-permute-done.5.passed = bf16[16,16,16,128]{3,2,1,0:T(8,128)(2,1)S(1)} collective-permute-done((bf16[16,16,16,128]{3,2,1,0:T(8,128)(2,1)S(1)}, bf16[16,16,16,128]{3,2,1,0:T(8,128)(2,1)S(1)}, u32[]{:S(2)}, u32[]{:S(2)}) %collective-permute-start.5) | collective-permute-done | bytes 1048608 | tf_op jit(solution)/shard_map/ppermute | solution.py:640
  104.0 0.2 shard_map.151
  104.2 19.2 %all_to_all.38.parts = bf16[16,16,16,128]{3,2,1,0:T(8,128)(2,1)S(1)} all-to-all(bf16[16,16,16,128]{3,2,1,0:T(8,128)(2,1)S(1)} %shard_map.151), channel_id=1, replica_groups=mesh['y'=4,'x'=4,'core'=2,'fsdp'=16] {'y','x'}, dimensions={0} | all-to-all | bytes 2097152 | tf_op jit(solution)/shard_map/all_to_all | solution.py:666
  123.4 0.8 shard_map.152
  124.2 4.4 %all-to-all-start.5 = ((bf16[16,16,128]{2,1,0:T(8,128)(2,1)}), bf16[16,16,128]{2,1,0:T(8,128)(2,1)S(1)}, u32[]{:S(2)}, u32[]{:S(2)}) async-start(bf16[16,16,128]{2,1,0:T(8,128)(2,1)} %shard_map.152), calls=%async_computation.5 | async-start | bytes 131072 | tf_op jit(solution)/shard_map/all_to_all | solution.py:667
  128.5 4.1 %collective-permute-start.3 = (bf16[1,320,128]{2,1,0:T(8,128)(2,1)S(1)}, bf16[1,320,128]{2,1,0:T(8,128)(2,1)S(1)}, u32[]{:S(2)}, u32[]{:S(2)}) collective-permute-start(bf16[1,320,128]{2,1,0:T(8,128)(2,1)S(1)} %get-tuple-element.43), channel_id=1, source_target_pairs={{0,16},{16,32},{32,48},{48,64},{64,80},{80,96},{96,112},{112,128},... | collective-permute-start | bytes 245768 | tf_op jit(solution)/shard_map/ppermute | solution.py:634
  132.7 1.9 %collective-permute-start.4 = (bf16[1,320,128]{2,1,0:T(8,128)(2,1)S(1)}, bf16[1,320,128]{2,1,0:T(8,128)(2,1)S(1)}, u32[]{:S(2)}, u32[]{:S(2)}) collective-permute-start(bf16[1,320,128]{2,1,0:T(8,128)(2,1)S(1)} %get-tuple-element.44), channel_id=1, source_target_pairs={{16,0},{32,16},{48,32},{64,48},{80,64},{96,80},{112,96},{128,112},... | collective-permute-start | bytes 245768 | tf_op jit(solution)/shard_map/ppermute | solution.py:635
  134.6 5.5 %all-to-all-done.5.frames = bf16[16,16,128]{2,1,0:T(8,128)(2,1)S(1)} async-done(((bf16[16,16,128]{2,1,0:T(8,128)(2,1)}), bf16[16,16,128]{2,1,0:T(8,128)(2,1)S(1)}, u32[]{:S(2)}, u32[]{:S(2)}) %all-to-all-start.5) | async-done | bytes 65568 | tf_op jit(solution)/shard_map/all_to_all | solution.py:667
  140.1 0.8 shard_map.153
  140.9 6.8 %all-to-all-start.6 = ((bf16[32,16,128]{2,1,0:T(8,128)(2,1)}), bf16[32,16,128]{2,1,0:T(8,128)(2,1)S(1)}, u32[]{:S(2)}, u32[]{:S(2)}) async-start(bf16[32,16,128]{2,1,0:T(8,128)(2,1)} %shard_map.153), calls=%async_computation.6 | async-start | bytes 262144 | tf_op jit(solution)/shard_map/all_to_all | solution.py:669
  147.7 0.0 collective-permute-done.3.above
  147.7 0.0 collective-permute-done.4.below
  147.7 0.0 copy-start.8
  147.7 1.1 copy-done.8
  148.8 5.0 %shard_map.150 = bf16[8,320,128]{2,1,0:T(8,128)(2,1)} custom-call(s32[1,1]{1,0:T(1,128)S(6)} %copy.16.live_ref, bf16[320,3072]{1,0:T(8,128)(2,1)S(1)} %get-tuple-element.38.weight, bf16[8,320,128]{2,1,0:T(8,128)(2,1)S(1)} %copy-done.8, bf16[1,320,128]{2,1,0:T(8,128)(2,1)S(1)} %collective-permute-done.3.above, ...), custom_call_target="tpu_custom_call" | custom-call | flops 14000000000 | bytes 29360128 | tf_op jit(solution)/shard_map/pallas_call | solution.py:620
  153.8 1.6 %all-to-all-done.6.tiles = bf16[32,16,128]{2,1,0:T(8,128)(2,1)S(1)} async-done(((bf16[32,16,128]{2,1,0:T(8,128)(2,1)}), bf16[32,16,128]{2,1,0:T(8,128)(2,1)S(1)}, u32[]{:S(2)}, u32[]{:S(2)}) %all-to-all-start.6) | async-done | bytes 131104 | tf_op jit(solution)/shard_map/all_to_all | solution.py:669
  155.4 0.0 copy-done.5
  155.4 1.4 shard_map.154
  (10 shorter events, 0.0 us)
Async XLA Ops:
  0.6 2.6 %copy-start = (bf16[1,1,8,128,320]{3,4,2,1,0:T(8,128)(2,1)S(1)}, bf16[1,1,8,128,320]{3,4,2,1,0:T(8,128)(2,1)}, u32[]{:S(2)}) copy-start(bf16[1,1,8,128,320]{3,4,2,1,0:T(8,128)(2,1)} %param.8) | copy-start | bytes 1966084
  1.4 1.0 copy-start.2
  3.2 21.4 %collective-permute-start = (bf16[1,320,128]{2,1,0:T(8,128)(2,1)S(1)}, bf16[1,320,128]{2,1,0:T(8,128)(2,1)S(1)}, u32[]{:S(2)}, u32[]{:S(2)}) collective-permute-start(bf16[1,320,128]{2,1,0:T(8,128)(2,1)S(1)} %get-tuple-element.31), channel_id=1, source_target_pairs={{0,16},{16,32},{32,48},{48,64},{64,80},{80,96},{96,112},{112,128},... | collective-permute-start | bytes 245768 | tf_op jit(solution)/shard_map/ppermute | solution.py:634
  7.7 16.9 %collective-permute-start.1 = (bf16[1,320,128]{2,1,0:T(8,128)(2,1)S(1)}, bf16[1,320,128]{2,1,0:T(8,128)(2,1)S(1)}, u32[]{:S(2)}, u32[]{:S(2)}) collective-permute-start(bf16[1,320,128]{2,1,0:T(8,128)(2,1)S(1)} %get-tuple-element.32), channel_id=1, source_target_pairs={{16,0},{32,16},{48,32},{64,48},{80,64},{96,80},{112,96},{128,112},... | collective-permute-start | bytes 245768 | tf_op jit(solution)/shard_map/ppermute | solution.py:635
  13.3 23.3 %all-to-all-start = ((bf16[16,16,128]{2,1,0:T(8,128)(2,1)}), bf16[16,16,128]{2,1,0:T(8,128)(2,1)S(1)}, u32[]{:S(2)}, u32[]{:S(2)}) async-start(bf16[16,16,128]{2,1,0:T(8,128)(2,1)} %shard_map.143.token), calls=%async_computation | async-start | bytes 131072 | tf_op jit(solution)/shard_map/all_to_all | solution.py:649
  26.5 2.6 %copy-start.6 = (bf16[3072,1024]{1,0:T(8,128)(2,1)}, bf16[3072,1024]{1,0:T(8,128)(2,1)S(1)}, u32[]{:S(2)}) copy-start(bf16[3072,1024]{1,0:T(8,128)(2,1)S(1)} %shard_map.145.patch) | copy-start | bytes 18874372
  57.2 23.6 %copy-start.9 = (f32[320]{0:T(512)S(1)}, f32[320]{0:T(512)}, u32[]{:S(2)}) copy-start(f32[320]{0:T(512)} %param.12) | copy-start | bytes 3844
  57.2 23.7 %copy-start.10 = (f32[320]{0:T(512)S(1)}, f32[320]{0:T(512)}, u32[]{:S(2)}) copy-start(f32[320]{0:T(512)} %param.13) | copy-start | bytes 3844
  57.2 23.8 %copy-start.1 = (bf16[1,1,8,128,320]{3,4,2,1,0:T(8,128)(2,1)S(1)}, bf16[1,1,8,128,320]{3,4,2,1,0:T(8,128)(2,1)}, u32[]{:S(2)}) copy-start(bf16[1,1,8,128,320]{3,4,2,1,0:T(8,128)(2,1)} %param.10) | copy-start | bytes 1966084
  57.2 7.9 %collective-permute-start.2 = (bf16[16,16,16,128]{3,2,1,0:T(8,128)(2,1)S(1)}, bf16[16,16,16,128]{3,2,1,0:T(8,128)(2,1)S(1)}, u32[]{:S(2)}, u32[]{:S(2)}) collective-permute-start(bf16[16,16,16,128]{3,2,1,0:T(8,128)(2,1)S(1)} %all_to_all.35.mine), channel_id=1, source_target_pairs={{0,16},{16,0},{1,17},{17,1},{2,18},{18,2},{3,19},{19,3},{4,20},{20... | collective-permute-start | bytes 3145736 | tf_op jit(solution)/shard_map/ppermute | solution.py:640
  99.4 24.0 %copy-start.7 = (bf16[8,320,128]{2,1,0:T(8,128)(2,1)}, bf16[8,320,128]{2,1,0:T(8,128)(2,1)S(1)}, u32[]{:S(2)}) copy-start(bf16[8,320,128]{2,1,0:T(8,128)(2,1)S(1)} %get-tuple-element.42.pre) | copy-start | bytes 1966084
  99.4 4.6 %collective-permute-start.5 = (bf16[16,16,16,128]{3,2,1,0:T(8,128)(2,1)S(1)}, bf16[16,16,16,128]{3,2,1,0:T(8,128)(2,1)S(1)}, u32[]{:S(2)}, u32[]{:S(2)}) collective-permute-start(bf16[16,16,16,128]{3,2,1,0:T(8,128)(2,1)S(1)} %get-tuple-element.46), channel_id=1, source_target_pairs={{0,16},{16,0},{1,17},{17,1},{2,18},{18,2},{3,19},{19,3},{4,20},{20... | collective-permute-start | bytes 3145736 | tf_op jit(solution)/shard_map/ppermute | solution.py:640
  124.2 15.9 %all-to-all-start.5 = ((bf16[16,16,128]{2,1,0:T(8,128)(2,1)}), bf16[16,16,128]{2,1,0:T(8,128)(2,1)S(1)}, u32[]{:S(2)}, u32[]{:S(2)}) async-start(bf16[16,16,128]{2,1,0:T(8,128)(2,1)} %shard_map.152), calls=%async_computation.5 | async-start | bytes 131072 | tf_op jit(solution)/shard_map/all_to_all | solution.py:667
  128.5 19.1 %collective-permute-start.3 = (bf16[1,320,128]{2,1,0:T(8,128)(2,1)S(1)}, bf16[1,320,128]{2,1,0:T(8,128)(2,1)S(1)}, u32[]{:S(2)}, u32[]{:S(2)}) collective-permute-start(bf16[1,320,128]{2,1,0:T(8,128)(2,1)S(1)} %get-tuple-element.43), channel_id=1, source_target_pairs={{0,16},{16,32},{32,48},{48,64},{64,80},{80,96},{96,112},{112,128},... | collective-permute-start | bytes 245768 | tf_op jit(solution)/shard_map/ppermute | solution.py:634
  132.7 15.0 %collective-permute-start.4 = (bf16[1,320,128]{2,1,0:T(8,128)(2,1)S(1)}, bf16[1,320,128]{2,1,0:T(8,128)(2,1)S(1)}, u32[]{:S(2)}, u32[]{:S(2)}) collective-permute-start(bf16[1,320,128]{2,1,0:T(8,128)(2,1)S(1)} %get-tuple-element.44), channel_id=1, source_target_pairs={{16,0},{32,16},{48,32},{64,48},{80,64},{96,80},{112,96},{128,112},... | collective-permute-start | bytes 245768 | tf_op jit(solution)/shard_map/ppermute | solution.py:635
  140.9 14.5 %all-to-all-start.6 = ((bf16[32,16,128]{2,1,0:T(8,128)(2,1)}), bf16[32,16,128]{2,1,0:T(8,128)(2,1)S(1)}, u32[]{:S(2)}, u32[]{:S(2)}) async-start(bf16[32,16,128]{2,1,0:T(8,128)(2,1)} %shard_map.153), calls=%async_computation.6 | async-start | bytes 262144 | tf_op jit(solution)/shard_map/all_to_all | solution.py:669
  147.7 1.1 copy-start.8
  148.8 6.6 %copy-start.3 = (f32[180,320]{1,0:T(8,128)S(1)}, f32[180,320]{1,0:T(8,128)}, u32[]{:S(2)}) copy-start(f32[180,320]{1,0:T(8,128)} %master.1) | copy-start | bytes 691204
  148.8 6.6 %copy-start.4 = (f32[180,320]{1,0:T(8,128)S(1)}, f32[180,320]{1,0:T(8,128)}, u32[]{:S(2)}) copy-start(f32[180,320]{1,0:T(8,128)} %first.1) | copy-start | bytes 691204
  148.8 6.6 %copy-start.5 = (f32[180,320]{1,0:T(8,128)S(1)}, f32[180,320]{1,0:T(8,128)}, u32[]{:S(2)}) copy-start(f32[180,320]{1,0:T(8,128)} %second.1) | copy-start | bytes 691204

commit v4 on v3

--- a/solution.py
+++ b/solution.py
@@ -175,7 +175,7 @@
         [SMEM, VMEM, VMEM, VMEM],
         [pltpu.VMEM((CAP, DEEP, COLS), F32)],
         out_specs=VMEM,
-        cost=8,
+        cost=1,
         room=30,
     )(live, own, above, below)
 
@@ -204,8 +204,8 @@
 
     @pl.when(step == 0)
     def _():
-        for index in range(4):
-            block_copy(index).start()
+        block_copy(0).start()
+        block_copy(1).start()
         left = lax.broadcasted_iota(jnp.int32, (8, COLS), 1) < 64
         for half, source in ((0, mine), (1, other)):
             side = (spot("core") + half) % 2
@@ -239,6 +239,8 @@
         @pl.when(step == index)
         def _():
             block_copy(index).wait()
+            if index < 2:
+                block_copy(index + 2).start()
 
     block = jnp.dot(weight[...], held[step], preferred_element_type=F32)
     mixed[2 * step] = block[:, :128]
@@ -378,8 +380,8 @@
 
     @pl.when(step == 0)
     def _():
-        for index in range(4):
-            block_copy(index).start()
+        block_copy(0).start()
+        block_copy(1).start()
         live = live_ref[0, 0]
         hot = one_hot()
         totals = jnp.sum(notes[...], axis=0)
@@ -408,6 +410,8 @@
         @pl.when(step == index)
         def _():
             block_copy(index).wait()
+            if index < 2:
+                block_copy(index + 2).start()
 
     block = lax.dot_general(
         field[...], held[step], (((1,), (1,)), ((), ())), preferred_element_type=F32

time: 157 us -> 161 us (1.025)
  starting transfers between devices: 46.5 us -> 50.6 us
  waiting for transfers between devices: 19.2 us -> 16.1 us
  blocking collectives: 61.6 us -> 64.3 us
    all_to_all x1, waiting for transfers between devices: 7.5 us -> 0.01 us  [local(): along_z = lax.all_to_all(packed, 'fsdp', 0, 0)]
    all_to_all x1, starting transfers between devices: 4.37 us -> 11.8 us  [local(): frames = lax.all_to_all(plane_sum(parts, riders), 'fsdp', 0, 0)]
    all_to_all x1, starting transfers between devices: 11.3 us -> 15.7 us  [local(): along_z = lax.all_to_all(packed, 'fsdp', 0, 0)]
    ppermute x2, waiting for transfers between devices: 0.01 us -> 4.12 us  [beside(): lax.ppermute(first_row, TILE, [((i + 1) % count, i) for i in range(ends)])]
    ppermute x2, starting transfers between devices: 7.49 us -> 3.84 us  [beside(): lax.ppermute(first_row, TILE, [((i + 1) % count, i) for i in range(ends)])]
    ppermute x2, starting transfers between devices: 7.89 us -> 4.35 us  [other_core(): return lax.ppermute(value, 'core', [(0, 1), (1, 0)])]
    all_to_all x1, blocking collectives: 20.5 us -> 23.4 us  [local(): mine = lax.all_to_all(copies(along_z, 16), ('y', 'x'), 0, 0)]
where the time goes in v4:
time: 161 us
  blocking collectives  64.3 us (40%)
  starting transfers between devices  50.6 us (31%)
  Pallas kernels  23.2 us (14%)
  waiting for transfers between devices  16.1 us (10%)
  local copies, waits for them, and re-layouts  4.97 us (3%)
    all_to_all x1, blocking collectives, local(): mine = lax.all_to_all(copies(along_z, 16), ('y', 'x'), 0, 0)  23.4 us
    all_to_all x1, blocking collectives, local(): parts = lax.all_to_all(add_pair(keep, other_core(send)), ('y', 'x'), 0, 0)  19.2 us
    all_to_all x1, starting transfers between devices, local(): along_z = lax.all_to_all(packed, 'fsdp', 0, 0)  15.7 us
    all_to_all x1, starting transfers between devices, local(): frames = lax.all_to_all(plane_sum(parts, riders), 'fsdp', 0, 0)  11.8 us
    all_to_all x1, blocking collectives, local(): notes = lax.all_to_all(note, TILE, 0, 0)  11 us
    all_to_all x1, blocking collectives, local(): stats = lax.all_to_all(message, TILE, 0, 0)  10.7 us
    ppermute x2, starting transfers between devices, beside(): lax.ppermute(last_row, TILE, [(i, (i + 1) % count) for i in range(ends)])  8.09 us
    all_to_all x1, starting transfers between devices, local(): tiles = lax.all_to_all(frame_sum(frames), TILE, 0, 0)  6.8 us
  transfers between devices with their start and end apart: 9, of which 5 were waited for; matrix products, arithmetic and copies ran while one was open for 0% of the time, Pallas kernels for 5%

profile of v4, /device:TPU:1, one launch (start us, length us, event | category | flops | bytes accessed | tf_op | source)
XLA Modules:
  0.0 160.7 jit_solution(14628015626306581259)
XLA Ops:
  0.6 0.0 copy-start.1
  0.6 0.0 copy-start.3
  0.7 1.0 copy-done.3
  1.7 0.9 shard_map.143.token
  2.5 15.7 %all-to-all-start = ((bf16[16,16,128]{2,1,0:T(8,128)(2,1)}), bf16[16,16,128]{2,1,0:T(8,128)(2,1)S(1)}, u32[]{:S(2)}, u32[]{:S(2)}) async-start(bf16[16,16,128]{2,1,0:T(8,128)(2,1)} %shard_map.143.token), calls=%async_computation | async-start | bytes 131072 | tf_op jit(solution)/shard_map/all_to_all | solution.py:653
  18.9 0.0 copy-done.1
  19.0 4.0 %collective-permute-start = (bf16[1,320,128]{2,1,0:T(8,128)(2,1)S(1)}, bf16[1,320,128]{2,1,0:T(8,128)(2,1)S(1)}, u32[]{:S(2)}, u32[]{:S(2)}) collective-permute-start(bf16[1,320,128]{2,1,0:T(8,128)(2,1)S(1)} %get-tuple-element.31), channel_id=1, source_target_pairs={{0,16},{16,32},{32,48},{48,64},{64,80},{80,96},{96,112},{112,128},... | collective-permute-start | bytes 245768 | tf_op jit(solution)/shard_map/ppermute | solution.py:638
  22.9 1.9 %collective-permute-start.1 = (bf16[1,320,128]{2,1,0:T(8,128)(2,1)S(1)}, bf16[1,320,128]{2,1,0:T(8,128)(2,1)S(1)}, u32[]{:S(2)}, u32[]{:S(2)}) collective-permute-start(bf16[1,320,128]{2,1,0:T(8,128)(2,1)S(1)} %get-tuple-element.32), channel_id=1, source_target_pairs={{16,0},{32,16},{48,32},{64,48},{80,64},{96,80},{112,96},{128,112},... | collective-permute-start | bytes 245768 | tf_op jit(solution)/shard_map/ppermute | solution.py:639
  24.9 0.0 collective-permute-done.above
  24.9 4.1 %collective-permute-done.1.below = bf16[1,320,128]{2,1,0:T(8,128)(2,1)S(1)} collective-permute-done((bf16[1,320,128]{2,1,0:T(8,128)(2,1)S(1)}, bf16[1,320,128]{2,1,0:T(8,128)(2,1)S(1)}, u32[]{:S(2)}, u32[]{:S(2)}) %collective-permute-start.1) | collective-permute-done | bytes 81952 | tf_op jit(solution)/shard_map/ppermute | solution.py:639
  29.0 1.8 %shard_map.145.patch = bf16[3072,1024]{1,0:T(8,128)(2,1)S(1)} custom-call(s32[1,1]{1,0:T(1,128)S(6)} %copy.16.live_ref, bf16[8,320,128]{2,1,0:T(8,128)(2,1)S(1)} %bitcast.13, bf16[1,320,128]{2,1,0:T(8,128)(2,1)S(1)} %collective-permute-done.above, bf16[1,320,128]{2,1,0:T(8,128)(2,1)S(1)} %collective-permute-done.1.below), custom_call_target="tpu_custom_call" | custom-call | flops 1000000000 | bytes 2097152 | tf_op jit(solution)/shard_map/pallas_call | solution.py:172
  30.8 0.0 copy-start
  30.9 2.6 %copy-done = bf16[3072,1024]{1,0:T(8,128)(2,1)} copy-done((bf16[3072,1024]{1,0:T(8,128)(2,1)}, bf16[3072,1024]{1,0:T(8,128)(2,1)S(1)}, u32[]{:S(2)}) %copy-start) | copy-done | bytes 6291480
  33.5 0.0 all-to-all-done.value
  33.5 0.1 shard_map.146
  33.6 23.4 %all_to_all.35.mine = bf16[16,16,16,128]{3,2,1,0:T(8,128)(2,1)S(1)} all-to-all(bf16[16,16,16,128]{3,2,1,0:T(8,128)(2,1)S(1)} %shard_map.146), channel_id=1, replica_groups=mesh['y'=4,'x'=4,'core'=2,'fsdp'=16] {'y','x'}, dimensions={0} | all-to-all | bytes 2097152 | tf_op jit(solution)/shard_map/all_to_all | solution.py:658
  57.0 2.0 %collective-permute-start.2 = (bf16[16,16,16,128]{3,2,1,0:T(8,128)(2,1)S(1)}, bf16[16,16,16,128]{3,2,1,0:T(8,128)(2,1)S(1)}, u32[]{:S(2)}, u32[]{:S(2)}) collective-permute-start(bf16[16,16,16,128]{3,2,1,0:T(8,128)(2,1)S(1)} %all_to_all.35.mine), channel_id=1, source_target_pairs={{0,16},{16,0},{1,17},{17,1},{2,18},{18,2},{3,19},{19,3},{4,20},{20... | collective-permute-start | bytes 3145736 | tf_op jit(solution)/shard_map/ppermute | solution.py:644
  59.0 2.6 %collective-permute-done.2.other = bf16[16,16,16,128]{3,2,1,0:T(8,128)(2,1)S(1)} collective-permute-done((bf16[16,16,16,128]{3,2,1,0:T(8,128)(2,1)S(1)}, bf16[16,16,16,128]{3,2,1,0:T(8,128)(2,1)S(1)}, u32[]{:S(2)}, u32[]{:S(2)}) %collective-permute-start.2) | collective-permute-done | bytes 1048608 | tf_op jit(solution)/shard_map/ppermute | solution.py:644
  61.7 4.9 %shard_map.147 = (f32[8,320,128]{2,1,0:T(8,128)S(1)}, bf16[320,3072]{1,0:T(8,128)(2,1)S(1)}, f32[32,8,128]{2,1,0:T(8,128)S(1)}) custom-call(s32[1,1]{1,0:T(1,128)S(6)} %copy.16.live_ref, bf16[16,16,16,128]{3,2,1,0:T(8,128)(2,1)S(1)} %all_to_all.35.mine, bf16[16,16,16,128]{3,2,1,0:T(8,128)(2,1)S(1)} %collective-permute-done.2.other, bf16[3072,1024]{1,0:T(8,128)(2,1)} %copy-done), custom_call_target="tpu_custom_call" | custom-call | flops 6000000000 | bytes 12582912 | tf_op jit(solution)/shard_map/pallas_call | solution.py:274
  66.6 10.7 %all_to_all.36.stats = f32[32,8,128]{2,1,0:T(8,128)S(1)} all-to-all(f32[32,8,128]{2,1,0:T(8,128)S(1)} %get-tuple-element.35), channel_id=1, replica_groups=mesh['y'=4,'x'=4,'core'=2,'fsdp'=16] {'y','x','core'}, dimensions={0} | all-to-all | bytes 262144 | tf_op jit(solution)/shard_map/all_to_all | solution.py:661
  77.3 0.0 copy-done.9
  77.3 0.1 broadcast_in_dim.8.gain
  77.4 0.0 copy-done.10
  77.4 0.1 broadcast_in_dim.9.bias
  77.5 0.0 copy-done.2
  77.5 1.9 %shard_map.148 = (bf16[8,320,128]{2,1,0:T(8,128)(2,1)}, f32[8,320,128]{2,1,0:T(8,128)S(1)}, f32[2,320,128]{2,1,0:T(8,128)S(1)}, f32[32,2,384]{2,1,0:T(2,128)S(1)}) custom-call(s32[1,1]{1,0:T(1,128)S(6)} %copy.16.live_ref, f32[32,8,128]{2,1,0:T(8,128)S(1)} %all_to_all.36.stats, f32[8,320,128]{2,1,0:T(8,128)S(1)} %get-tuple-element.36.mixed, ...), custom_call_target="tpu_custom_call" | custom-call | flops 4000000000 | bytes 8388608 | tf_op jit(solution)/shard_map/pallas_call | solution.py:336
  79.4 11.0 %all_to_all.37.notes = f32[32,2,384]{2,1,0:T(2,128)S(1)} all-to-all(f32[32,2,384]{2,1,0:T(2,128)S(1)} %get-tuple-element.39), channel_id=1, replica_groups=mesh['y'=4,'x'=4,'core'=2,'fsdp'=16] {'y','x','core'}, dimensions={0} | all-to-all | bytes 196608 | tf_op jit(solution)/shard_map/all_to_all | solution.py:665
  90.5 5.3 %shard_map.149 = (bf16[8,320,128]{2,1,0:T(8,128)(2,1)S(1)}, bf16[16,16,16,128]{3,2,1,0:T(8,128)(2,1)S(1)}, bf16[16,16,16,128]{3,2,1,0:T(8,128)(2,1)S(1)}, f32[32...) custom-call(s32[1,1]{1,0:T(1,128)S(6)} %copy.16.live_ref, ...), custom_call_target="tpu_custom_call" | custom-call | flops 7000000000 | bytes 14680064 | tf_op jit(solution)/shard_map/pallas_call | solution.py:462
  95.8 0.0 copy-start.7
  95.8 2.3 %collective-permute-start.5 = (bf16[16,16,16,128]{3,2,1,0:T(8,128)(2,1)S(1)}, bf16[16,16,16,128]{3,2,1,0:T(8,128)(2,1)S(1)}, u32[]{:S(2)}, u32[]{:S(2)}) collective-permute-start(bf16[16,16,16,128]{3,2,1,0:T(8,128)(2,1)S(1)} %get-tuple-element.46), channel_id=1, source_target_pairs={{0,16},{16,0},{1,17},{17,1},{2,18},{18,2},{3,19},{19,3},{4,20},{20... | collective-permute-start | bytes 3145736 | tf_op jit(solution)/shard_map/ppermute | solution.py:644
  98.1 2.3 %collective-permute-done.5.passed = bf16[16,16,16,128]{3,2,1,0:T(8,128)(2,1)S(1)} collective-permute-done((bf16[16,16,16,128]{3,2,1,0:T(8,128)(2,1)S(1)}, bf16[16,16,16,128]{3,2,1,0:T(8,128)(2,1)S(1)}, u32[]{:S(2)}, u32[]{:S(2)}) %collective-permute-start.5) | collective-permute-done | bytes 1048608 | tf_op jit(solution)/shard_map/ppermute | solution.py:644
  100.4 0.2 shard_map.151
  100.6 19.2 %all_to_all.38.parts = bf16[16,16,16,128]{3,2,1,0:T(8,128)(2,1)S(1)} all-to-all(bf16[16,16,16,128]{3,2,1,0:T(8,128)(2,1)S(1)} %shard_map.151), channel_id=1, replica_groups=mesh['y'=4,'x'=4,'core'=2,'fsdp'=16] {'y','x'}, dimensions={0} | all-to-all | bytes 2097152 | tf_op jit(solution)/shard_map/all_to_all | solution.py:670
  119.9 0.8 shard_map.152
  120.6 11.8 %all-to-all-start.5 = ((bf16[16,16,128]{2,1,0:T(8,128)(2,1)}), bf16[16,16,128]{2,1,0:T(8,128)(2,1)S(1)}, u32[]{:S(2)}, u32[]{:S(2)}) async-start(bf16[16,16,128]{2,1,0:T(8,128)(2,1)} %shard_map.152), calls=%async_computation.5 | async-start | bytes 131072 | tf_op jit(solution)/shard_map/all_to_all | solution.py:671
  132.4 4.1 %collective-permute-start.3 = (bf16[1,320,128]{2,1,0:T(8,128)(2,1)S(1)}, bf16[1,320,128]{2,1,0:T(8,128)(2,1)S(1)}, u32[]{:S(2)}, u32[]{:S(2)}) collective-permute-start(bf16[1,320,128]{2,1,0:T(8,128)(2,1)S(1)} %get-tuple-element.43), channel_id=1, source_target_pairs={{0,16},{16,32},{32,48},{48,64},{64,80},{80,96},{96,112},{112,128},... | collective-permute-start | bytes 245768 | tf_op jit(solution)/shard_map/ppermute | solution.py:638
  136.6 1.9 %collective-permute-start.4 = (bf16[1,320,128]{2,1,0:T(8,128)(2,1)S(1)}, bf16[1,320,128]{2,1,0:T(8,128)(2,1)S(1)}, u32[]{:S(2)}, u32[]{:S(2)}) collective-permute-start(bf16[1,320,128]{2,1,0:T(8,128)(2,1)S(1)} %get-tuple-element.44), channel_id=1, source_target_pairs={{16,0},{32,16},{48,32},{64,48},{80,64},{96,80},{112,96},{128,112},... | collective-permute-start | bytes 245768 | tf_op jit(solution)/shard_map/ppermute | solution.py:639
  138.5 5.5 %all-to-all-done.5.frames = bf16[16,16,128]{2,1,0:T(8,128)(2,1)S(1)} async-done(((bf16[16,16,128]{2,1,0:T(8,128)(2,1)}), bf16[16,16,128]{2,1,0:T(8,128)(2,1)S(1)}, u32[]{:S(2)}, u32[]{:S(2)}) %all-to-all-start.5) | async-done | bytes 65568 | tf_op jit(solution)/shard_map/all_to_all | solution.py:671
  144.0 0.8 shard_map.153
  144.8 6.8 %all-to-all-start.6 = ((bf16[32,16,128]{2,1,0:T(8,128)(2,1)}), bf16[32,16,128]{2,1,0:T(8,128)(2,1)S(1)}, u32[]{:S(2)}, u32[]{:S(2)}) async-start(bf16[32,16,128]{2,1,0:T(8,128)(2,1)} %shard_map.153), calls=%async_computation.6 | async-start | bytes 262144 | tf_op jit(solution)/shard_map/all_to_all | solution.py:673
  151.6 0.0 collective-permute-done.3.above
  151.6 0.0 collective-permute-done.4.below
  151.6 0.0 copy-start.8
  151.6 1.1 copy-done.8
  152.7 5.0 %shard_map.150 = bf16[8,320,128]{2,1,0:T(8,128)(2,1)} custom-call(s32[1,1]{1,0:T(1,128)S(6)} %copy.16.live_ref, bf16[320,3072]{1,0:T(8,128)(2,1)S(1)} %get-tuple-element.38.weight, bf16[8,320,128]{2,1,0:T(8,128)(2,1)S(1)} %copy-done.8, bf16[1,320,128]{2,1,0:T(8,128)(2,1)S(1)} %collective-permute-done.3.above, ...), custom_call_target="tpu_custom_call" | custom-call | flops 14000000000 | bytes 29360128 | tf_op jit(solution)/shard_map/pallas_call | solution.py:624
  157.7 1.6 %all-to-all-done.6.tiles = bf16[32,16,128]{2,1,0:T(8,128)(2,1)S(1)} async-done(((bf16[32,16,128]{2,1,0:T(8,128)(2,1)}), bf16[32,16,128]{2,1,0:T(8,128)(2,1)S(1)}, u32[]{:S(2)}, u32[]{:S(2)}) %all-to-all-start.6) | async-done | bytes 131104 | tf_op jit(solution)/shard_map/all_to_all | solution.py:673
  159.3 0.0 copy-done.5
  159.3 1.4 shard_map.154
  (10 shorter events, 0.0 us)
Async XLA Ops:
  0.6 18.3 %copy-start.1 = (bf16[1,1,8,128,320]{3,4,2,1,0:T(8,128)(2,1)S(1)}, bf16[1,1,8,128,320]{3,4,2,1,0:T(8,128)(2,1)}, u32[]{:S(2)}) copy-start(bf16[1,1,8,128,320]{3,4,2,1,0:T(8,128)(2,1)} %param.8) | copy-start | bytes 1966084
  0.6 1.0 copy-start.3
  2.5 30.9 %all-to-all-start = ((bf16[16,16,128]{2,1,0:T(8,128)(2,1)}), bf16[16,16,128]{2,1,0:T(8,128)(2,1)S(1)}, u32[]{:S(2)}, u32[]{:S(2)}) async-start(bf16[16,16,128]{2,1,0:T(8,128)(2,1)} %shard_map.143.token), calls=%async_computation | async-start | bytes 131072 | tf_op jit(solution)/shard_map/all_to_all | solution.py:653
  19.0 5.9 %collective-permute-start = (bf16[1,320,128]{2,1,0:T(8,128)(2,1)S(1)}, bf16[1,320,128]{2,1,0:T(8,128)(2,1)S(1)}, u32[]{:S(2)}, u32[]{:S(2)}) collective-permute-start(bf16[1,320,128]{2,1,0:T(8,128)(2,1)S(1)} %get-tuple-element.31), channel_id=1, source_target_pairs={{0,16},{16,32},{32,48},{48,64},{64,80},{80,96},{96,112},{112,128},... | collective-permute-start | bytes 245768 | tf_op jit(solution)/shard_map/ppermute | solution.py:638
  22.9 6.1 %collective-permute-start.1 = (bf16[1,320,128]{2,1,0:T(8,128)(2,1)S(1)}, bf16[1,320,128]{2,1,0:T(8,128)(2,1)S(1)}, u32[]{:S(2)}, u32[]{:S(2)}) collective-permute-start(bf16[1,320,128]{2,1,0:T(8,128)(2,1)S(1)} %get-tuple-element.32), channel_id=1, source_target_pairs={{16,0},{32,16},{48,32},{64,48},{80,64},{96,80},{112,96},{128,112},... | collective-permute-start | bytes 245768 | tf_op jit(solution)/shard_map/ppermute | solution.py:639
  30.8 2.6 %copy-start = (bf16[3072,1024]{1,0:T(8,128)(2,1)}, bf16[3072,1024]{1,0:T(8,128)(2,1)S(1)}, u32[]{:S(2)}) copy-start(bf16[3072,1024]{1,0:T(8,128)(2,1)S(1)} %shard_map.145.patch) | copy-start | bytes 18874372
  57.0 20.3 %copy-start.9 = (f32[320]{0:T(512)S(1)}, f32[320]{0:T(512)}, u32[]{:S(2)}) copy-start(f32[320]{0:T(512)} %param.12) | copy-start | bytes 3844
  57.0 20.4 %copy-start.10 = (f32[320]{0:T(512)S(1)}, f32[320]{0:T(512)}, u32[]{:S(2)}) copy-start(f32[320]{0:T(512)} %param.13) | copy-start | bytes 3844
  57.0 20.5 %copy-start.2 = (bf16[1,1,8,128,320]{3,4,2,1,0:T(8,128)(2,1)S(1)}, bf16[1,1,8,128,320]{3,4,2,1,0:T(8,128)(2,1)}, u32[]{:S(2)}) copy-start(bf16[1,1,8,128,320]{3,4,2,1,0:T(8,128)(2,1)} %param.10) | copy-start | bytes 1966084
  57.0 4.7 %collective-permute-start.2 = (bf16[16,16,16,128]{3,2,1,0:T(8,128)(2,1)S(1)}, bf16[16,16,16,128]{3,2,1,0:T(8,128)(2,1)S(1)}, u32[]{:S(2)}, u32[]{:S(2)}) collective-permute-start(bf16[16,16,16,128]{3,2,1,0:T(8,128)(2,1)S(1)} %all_to_all.35.mine), channel_id=1, source_target_pairs={{0,16},{16,0},{1,17},{17,1},{2,18},{18,2},{3,19},{19,3},{4,20},{20... | collective-permute-start | bytes 3145736 | tf_op jit(solution)/shard_map/ppermute | solution.py:644
  95.8 24.1 %copy-start.7 = (bf16[8,320,128]{2,1,0:T(8,128)(2,1)}, bf16[8,320,128]{2,1,0:T(8,128)(2,1)S(1)}, u32[]{:S(2)}) copy-start(bf16[8,320,128]{2,1,0:T(8,128)(2,1)S(1)} %get-tuple-element.42.pre) | copy-start | bytes 1966084
  95.8 4.6 %collective-permute-start.5 = (bf16[16,16,16,128]{3,2,1,0:T(8,128)(2,1)S(1)}, bf16[16,16,16,128]{3,2,1,0:T(8,128)(2,1)S(1)}, u32[]{:S(2)}, u32[]{:S(2)}) collective-permute-start(bf16[16,16,16,128]{3,2,1,0:T(8,128)(2,1)S(1)} %get-tuple-element.46), channel_id=1, source_target_pairs={{0,16},{16,0},{1,17},{17,1},{2,18},{18,2},{3,19},{19,3},{4,20},{20... | collective-permute-start | bytes 3145736 | tf_op jit(solution)/shard_map/ppermute | solution.py:644
  120.6 23.4 %all-to-all-start.5 = ((bf16[16,16,128]{2,1,0:T(8,128)(2,1)}), bf16[16,16,128]{2,1,0:T(8,128)(2,1)S(1)}, u32[]{:S(2)}, u32[]{:S(2)}) async-start(bf16[16,16,128]{2,1,0:T(8,128)(2,1)} %shard_map.152), calls=%async_computation.5 | async-start | bytes 131072 | tf_op jit(solution)/shard_map/all_to_all | solution.py:671
  132.4 19.1 %collective-permute-start.3 = (bf16[1,320,128]{2,1,0:T(8,128)(2,1)S(1)}, bf16[1,320,128]{2,1,0:T(8,128)(2,1)S(1)}, u32[]{:S(2)}, u32[]{:S(2)}) collective-permute-start(bf16[1,320,128]{2,1,0:T(8,128)(2,1)S(1)} %get-tuple-element.43), channel_id=1, source_target_pairs={{0,16},{16,32},{32,48},{48,64},{64,80},{80,96},{96,112},{112,128},... | collective-permute-start | bytes 245768 | tf_op jit(solution)/shard_map/ppermute | solution.py:638
  136.6 15.0 %collective-permute-start.4 = (bf16[1,320,128]{2,1,0:T(8,128)(2,1)S(1)}, bf16[1,320,128]{2,1,0:T(8,128)(2,1)S(1)}, u32[]{:S(2)}, u32[]{:S(2)}) collective-permute-start(bf16[1,320,128]{2,1,0:T(8,128)(2,1)S(1)} %get-tuple-element.44), channel_id=1, source_target_pairs={{16,0},{32,16},{48,32},{64,48},{80,64},{96,80},{112,96},{128,112},... | collective-permute-start | bytes 245768 | tf_op jit(solution)/shard_map/ppermute | solution.py:639
  144.8 14.5 %all-to-all-start.6 = ((bf16[32,16,128]{2,1,0:T(8,128)(2,1)}), bf16[32,16,128]{2,1,0:T(8,128)(2,1)S(1)}, u32[]{:S(2)}, u32[]{:S(2)}) async-start(bf16[32,16,128]{2,1,0:T(8,128)(2,1)} %shard_map.153), calls=%async_computation.6 | async-start | bytes 262144 | tf_op jit(solution)/shard_map/all_to_all | solution.py:673
  151.6 1.1 copy-start.8
  152.7 6.6 %copy-start.4 = (f32[180,320]{1,0:T(8,128)S(1)}, f32[180,320]{1,0:T(8,128)}, u32[]{:S(2)}) copy-start(f32[180,320]{1,0:T(8,128)} %master.1) | copy-start | bytes 691204
  152.7 6.6 %copy-start.5 = (f32[180,320]{1,0:T(8,128)S(1)}, f32[180,320]{1,0:T(8,128)}, u32[]{:S(2)}) copy-start(f32[180,320]{1,0:T(8,128)} %first.1) | copy-start | bytes 691204
  152.7 6.6 %copy-start.6 = (f32[180,320]{1,0:T(8,128)S(1)}, f32[180,320]{1,0:T(8,128)}, u32[]{:S(2)}) copy-start(f32[180,320]{1,0:T(8,128)} %second.1) | copy-start | bytes 691204

commit v5 on v3

--- a/solution.py
+++ b/solution.py
@@ -24,6 +24,14 @@
 SMEM = pl.BlockSpec(memory_space=pltpu.SMEM)
 
 
+def place_of(y, x):
+    return y * 4 + (x if y % 2 == 0 else 3 - x)
+
+
+SNAKE = sorted(range(16), key=lambda i: place_of(i // 4, i % 4))
+PLANES = [[2 * i + core for i in SNAKE] for core in range(2)]
+
+
 def spot(name):
     return lax.axis_index(name)
 
@@ -216,7 +224,7 @@
 
                     def tile(frame, index):
                         row = (index % 2) * 8
-                        value = source[y * 4 + index // 2, 2 * pair + frame, row : row + 8, :]
+                        value = source[place_of(y, index // 2), 2 * pair + frame, row : row + 8, :]
                         return value.astype(F32)
 
                     even = [tile(0, index) for index in range(8)]
@@ -437,7 +445,7 @@
 
                 tiles = compact(main, rest)
                 for x in range(4):
-                    target[y * 4 + x, frame] = jnp.concatenate(
+                    target[place_of(y, x), frame] = jnp.concatenate(
                         tiles[2 * x : 2 * x + 2], axis=0
                     ).astype(BF)
 
@@ -651,7 +659,7 @@
     patch = patches(tile_rows, own, above, below)
     patch = pltpu.with_memory_space_constraint(patch, pltpu.HBM)
     along_z, patch = lax.optimization_barrier((along_z, patch))
-    mine = lax.all_to_all(copies(along_z, 16), ("y", "x"), 0, 0)
+    mine = lax.all_to_all(copies(along_z, 16), TILE, 0, 0, axis_index_groups=PLANES)
     other = other_core(mine)
     mixed, weight, message = forward(tile_rows, mine, other, patch)
     stats = lax.all_to_all(message, TILE, 0, 0)
@@ -663,7 +671,7 @@
         tile_rows, notes, mixed, dshift, moments, gain, patch
     )
     above_grad, below_grad = beside(pre_first, pre_last)
-    parts = lax.all_to_all(add_pair(keep, other_core(send)), ("y", "x"), 0, 0)
+    parts = lax.all_to_all(add_pair(keep, other_core(send)), TILE, 0, 0, axis_index_groups=PLANES)
     frames = lax.all_to_all(plane_sum(parts, riders), "fsdp", 0, 0)
     image_grad = back(tile_rows, weight, pre, above_grad, below_grad)
     tiles = lax.all_to_all(frame_sum(frames), TILE, 0, 0)

time: 157 us -> 157 us (level)
  blocking collectives: 61.6 us -> 59.5 us
  starting transfers between devices: 46.5 us -> 48.6 us
    all_to_all x2, blocking collectives: 39.7 us -> 36.8 us  [the longest x1 18.9 us: local(): lax.all_to_all(copies(along_z, 16), TILE, 0, 0, axis_index_groups=PLANES)]
where the time goes in v5:
time: 157 us; the launch traced here: 156 us
  blocking collectives  59.5 us (38%)
  starting transfers between devices  48.6 us (31%)
  Pallas kernels  23.1 us (15%)
  waiting for transfers between devices  18.6 us (12%)
  local copies, waits for them, and re-layouts  4.9 us (3%)
  between operations  1.57 us (1%)
    all_to_all x1, blocking collectives, local(): lax.all_to_all(copies(along_z, 16), TILE, 0, 0, axis_index_groups=PLANES)  18.9 us
    all_to_all x1, blocking collectives, local(): lax.all_to_all(add_pair(keep, other_core(send)), TILE, 0, 0, axis_index_g...  17.9 us
    all_to_all x1, blocking collectives, local(): stats = lax.all_to_all(message, TILE, 0, 0)  11.7 us
    all_to_all x1, starting transfers between devices, local(): along_z = lax.all_to_all(packed, 'fsdp', 0, 0)  11.3 us
    all_to_all x1, blocking collectives, local(): notes = lax.all_to_all(note, TILE, 0, 0)  11 us
    ppermute x2, starting transfers between devices, beside(): lax.ppermute(last_row, TILE, [(i, (i + 1) % count) for i in range(ends)])  9.11 us
    ppermute x2, starting transfers between devices, other_core(): return lax.ppermute(value, 'core', [(0, 1), (1, 0)])  8.67 us
    all_to_all x1, starting transfers between devices, local(): tiles = lax.all_to_all(frame_sum(frames), TILE, 0, 0)  7.69 us
  transfers between devices with their start and end apart: 9, of which 5 were waited for; matrix products, arithmetic and copies ran while one was open for 0% of the time, Pallas kernels for 5%

profile of v5, /device:TPU:1, one launch (start us, length us, event | category | flops | bytes accessed | tf_op | source)
XLA Modules:
  0.0 156.2 jit_solution(11383154014744680336)
XLA Ops:
  0.6 0.0 copy-start
  1.4 0.0 copy-start.2
  1.4 0.9 copy-done.2
  2.3 0.9 shard_map.143.token
  3.2 0.0 copy-done
  3.2 4.5 %collective-permute-start = (bf16[1,320,128]{2,1,0:T(8,128)(2,1)S(1)}, bf16[1,320,128]{2,1,0:T(8,128)(2,1)S(1)}, u32[]{:S(2)}, u32[]{:S(2)}) collective-permute-start(bf16[1,320,128]{2,1,0:T(8,128)(2,1)S(1)} %get-tuple-element.31), channel_id=1, source_target_pairs={{0,16},{16,32},{32,48},{48,64},{64,80},{80,96},{96,112},{112,128},... | collective-permute-start | bytes 245768 | tf_op jit(solution)/shard_map/ppermute | solution.py:642
  7.7 5.6 %collective-permute-start.1 = (bf16[1,320,128]{2,1,0:T(8,128)(2,1)S(1)}, bf16[1,320,128]{2,1,0:T(8,128)(2,1)S(1)}, u32[]{:S(2)}, u32[]{:S(2)}) collective-permute-start(bf16[1,320,128]{2,1,0:T(8,128)(2,1)S(1)} %get-tuple-element.32), channel_id=1, source_target_pairs={{16,0},{32,16},{48,32},{64,48},{80,64},{96,80},{112,96},{128,112},... | collective-permute-start | bytes 245768 | tf_op jit(solution)/shard_map/ppermute | solution.py:643
  13.3 11.3 %all-to-all-start = ((bf16[16,16,128]{2,1,0:T(8,128)(2,1)}), bf16[16,16,128]{2,1,0:T(8,128)(2,1)S(1)}, u32[]{:S(2)}, u32[]{:S(2)}) async-start(bf16[16,16,128]{2,1,0:T(8,128)(2,1)} %shard_map.143.token), calls=%async_computation | async-start | bytes 131072 | tf_op jit(solution)/shard_map/all_to_all | solution.py:657
  24.6 0.0 collective-permute-done.above
  24.6 0.0 collective-permute-done.1.below
  24.6 1.8 %shard_map.145.patch = bf16[3072,1024]{1,0:T(8,128)(2,1)S(1)} custom-call(s32[1,1]{1,0:T(1,128)S(6)} %copy.16.live_ref, bf16[8,320,128]{2,1,0:T(8,128)(2,1)S(1)} %bitcast.13, bf16[1,320,128]{2,1,0:T(8,128)(2,1)S(1)} %collective-permute-done.above, bf16[1,320,128]{2,1,0:T(8,128)(2,1)S(1)} %collective-permute-done.1.below), custom_call_target="tpu_custom_call" | custom-call | flops 8000000000 | bytes 16777216 | tf_op jit(solution)/shard_map/pallas_call | solution.py:180
  26.5 0.0 copy-start.6
  26.5 2.6 %copy-done.6 = bf16[3072,1024]{1,0:T(8,128)(2,1)} copy-done((bf16[3072,1024]{1,0:T(8,128)(2,1)}, bf16[3072,1024]{1,0:T(8,128)(2,1)S(1)}, u32[]{:S(2)}) %copy-start.6) | copy-done | bytes 6291480
  29.1 7.5 %all-to-all-done.value = bf16[16,16,128]{2,1,0:T(8,128)(2,1)S(1)} async-done(((bf16[16,16,128]{2,1,0:T(8,128)(2,1)}), bf16[16,16,128]{2,1,0:T(8,128)(2,1)S(1)}, u32[]{:S(2)}, u32[]{:S(2)}) %all-to-all-start) | async-done | bytes 65568 | tf_op jit(solution)/shard_map/all_to_all | solution.py:657
  36.6 0.1 shard_map.146
  36.7 18.9 %all_to_all.35.mine = bf16[16,16,16,128]{3,2,1,0:T(8,128)(2,1)S(1)} all-to-all(bf16[16,16,16,128]{3,2,1,0:T(8,128)(2,1)S(1)} %shard_map.146), channel_id=1, replica_groups={{0,32,64,96,224,192,160,128,256,288,320,352,480,448,416,384},{16,48,80,..., dimensions={0} | all-to-all | bytes 2097152 | tf_op jit(solution)/shard_map/all_to_all | solution.py:662
  55.6 6.4 %collective-permute-start.2 = (bf16[16,16,16,128]{3,2,1,0:T(8,128)(2,1)S(1)}, bf16[16,16,16,128]{3,2,1,0:T(8,128)(2,1)S(1)}, u32[]{:S(2)}, u32[]{:S(2)}) collective-permute-start(bf16[16,16,16,128]{3,2,1,0:T(8,128)(2,1)S(1)} %all_to_all.35.mine), channel_id=1, source_target_pairs={{0,16},{16,0},{1,17},{17,1},{2,18},{18,2},{3,19},{19,3},{4,20},{20... | collective-permute-start | bytes 3145736 | tf_op jit(solution)/shard_map/ppermute | solution.py:648
  62.0 2.3 %collective-permute-done.2.other = bf16[16,16,16,128]{3,2,1,0:T(8,128)(2,1)S(1)} collective-permute-done((bf16[16,16,16,128]{3,2,1,0:T(8,128)(2,1)S(1)}, bf16[16,16,16,128]{3,2,1,0:T(8,128)(2,1)S(1)}, u32[]{:S(2)}, u32[]{:S(2)}) %collective-permute-start.2) | collective-permute-done | bytes 1048608 | tf_op jit(solution)/shard_map/ppermute | solution.py:648
  64.3 4.8 %shard_map.147 = (f32[8,320,128]{2,1,0:T(8,128)S(1)}, bf16[320,3072]{1,0:T(8,128)(2,1)S(1)}, f32[32,8,128]{2,1,0:T(8,128)S(1)}) custom-call(s32[1,1]{1,0:T(1,128)S(6)} %copy.16.live_ref, bf16[16,16,16,128]{3,2,1,0:T(8,128)(2,1)S(1)} %all_to_all.35.mine, bf16[16,16,16,128]{3,2,1,0:T(8,128)(2,1)S(1)} %collective-permute-done.2.other, bf16[3072,1024]{1,0:T(8,128)(2,1)} %copy-done.6), custom_call_target="tpu_custom_call" | custom-call | flops 6000000000 | bytes 12582912 | tf_op jit(solution)/shard_map/pallas_call | solution.py:280
  69.1 11.7 %all_to_all.36.stats = f32[32,8,128]{2,1,0:T(8,128)S(1)} all-to-all(f32[32,8,128]{2,1,0:T(8,128)S(1)} %get-tuple-element.35), channel_id=1, replica_groups=mesh['y'=4,'x'=4,'core'=2,'fsdp'=16] {'y','x','core'}, dimensions={0} | all-to-all | bytes 262144 | tf_op jit(solution)/shard_map/all_to_all | solution.py:665
  80.7 0.0 copy-done.9
  80.7 0.1 broadcast_in_dim.8.gain
  80.8 0.0 copy-done.10
  80.8 0.1 broadcast_in_dim.9.bias
  80.9 0.0 copy-done.1
  80.9 1.9 %shard_map.148 = (bf16[8,320,128]{2,1,0:T(8,128)(2,1)}, f32[8,320,128]{2,1,0:T(8,128)S(1)}, f32[2,320,128]{2,1,0:T(8,128)S(1)}, f32[32,2,384]{2,1,0:T(2,128)S(1)}) custom-call(s32[1,1]{1,0:T(1,128)S(6)} %copy.16.live_ref, f32[32,8,128]{2,1,0:T(8,128)S(1)} %all_to_all.36.stats, f32[8,320,128]{2,1,0:T(8,128)S(1)} %get-tuple-element.36.mixed, ...), custom_call_target="tpu_custom_call" | custom-call | flops 4000000000 | bytes 8388608 | tf_op jit(solution)/shard_map/pallas_call | solution.py:342
  82.9 11.0 %all_to_all.37.notes = f32[32,2,384]{2,1,0:T(2,128)S(1)} all-to-all(f32[32,2,384]{2,1,0:T(2,128)S(1)} %get-tuple-element.39), channel_id=1, replica_groups=mesh['y'=4,'x'=4,'core'=2,'fsdp'=16] {'y','x','core'}, dimensions={0} | all-to-all | bytes 196608 | tf_op jit(solution)/shard_map/all_to_all | solution.py:669
  93.9 5.3 %shard_map.149 = (bf16[8,320,128]{2,1,0:T(8,128)(2,1)S(1)}, bf16[16,16,16,128]{3,2,1,0:T(8,128)(2,1)S(1)}, bf16[16,16,16,128]{3,2,1,0:T(8,128)(2,1)S(1)}, f32[32...) custom-call(s32[1,1]{1,0:T(1,128)S(6)} %copy.16.live_ref, ...), custom_call_target="tpu_custom_call" | custom-call | flops 7000000000 | bytes 14680064 | tf_op jit(solution)/shard_map/pallas_call | solution.py:466
  99.2 0.0 copy-start.7
  99.3 2.3 %collective-permute-start.5 = (bf16[16,16,16,128]{3,2,1,0:T(8,128)(2,1)S(1)}, bf16[16,16,16,128]{3,2,1,0:T(8,128)(2,1)S(1)}, u32[]{:S(2)}, u32[]{:S(2)}) collective-permute-start(bf16[16,16,16,128]{3,2,1,0:T(8,128)(2,1)S(1)} %get-tuple-element.46), channel_id=1, source_target_pairs={{0,16},{16,0},{1,17},{17,1},{2,18},{18,2},{3,19},{19,3},{4,20},{20... | collective-permute-start | bytes 3145736 | tf_op jit(solution)/shard_map/ppermute | solution.py:648
  101.6 2.3 %collective-permute-done.5.passed = bf16[16,16,16,128]{3,2,1,0:T(8,128)(2,1)S(1)} collective-permute-done((bf16[16,16,16,128]{3,2,1,0:T(8,128)(2,1)S(1)}, bf16[16,16,16,128]{3,2,1,0:T(8,128)(2,1)S(1)}, u32[]{:S(2)}, u32[]{:S(2)}) %collective-permute-start.5) | collective-permute-done | bytes 1048608 | tf_op jit(solution)/shard_map/ppermute | solution.py:648
  103.8 0.2 shard_map.151
  104.1 17.9 %all_to_all.38.parts = bf16[16,16,16,128]{3,2,1,0:T(8,128)(2,1)S(1)} all-to-all(bf16[16,16,16,128]{3,2,1,0:T(8,128)(2,1)S(1)} %shard_map.151), channel_id=1, replica_groups={{0,32,64,96,224,192,160,128,256,288,320,352,480,448,416,384},{16,48,80,..., dimensions={0} | all-to-all | bytes 2097152 | tf_op jit(solution)/shard_map/all_to_all | solution.py:674
  122.0 0.0 copy-done.7
  122.0 0.8 shard_map.152
  122.8 4.4 %all-to-all-start.5 = ((bf16[16,16,128]{2,1,0:T(8,128)(2,1)}), bf16[16,16,128]{2,1,0:T(8,128)(2,1)S(1)}, u32[]{:S(2)}, u32[]{:S(2)}) async-start(bf16[16,16,128]{2,1,0:T(8,128)(2,1)} %shard_map.152), calls=%async_computation.5 | async-start | bytes 131072 | tf_op jit(solution)/shard_map/all_to_all | solution.py:675
  127.2 4.6 %collective-permute-start.3 = (bf16[1,320,128]{2,1,0:T(8,128)(2,1)S(1)}, bf16[1,320,128]{2,1,0:T(8,128)(2,1)S(1)}, u32[]{:S(2)}, u32[]{:S(2)}) collective-permute-start(bf16[1,320,128]{2,1,0:T(8,128)(2,1)S(1)} %get-tuple-element.43), channel_id=1, source_target_pairs={{0,16},{16,32},{32,48},{48,64},{64,80},{80,96},{96,112},{112,128},... | collective-permute-start | bytes 245768 | tf_op jit(solution)/shard_map/ppermute | solution.py:642
  131.8 1.9 %collective-permute-start.4 = (bf16[1,320,128]{2,1,0:T(8,128)(2,1)S(1)}, bf16[1,320,128]{2,1,0:T(8,128)(2,1)S(1)}, u32[]{:S(2)}, u32[]{:S(2)}) collective-permute-start(bf16[1,320,128]{2,1,0:T(8,128)(2,1)S(1)} %get-tuple-element.44), channel_id=1, source_target_pairs={{16,0},{32,16},{48,32},{64,48},{80,64},{96,80},{112,96},{128,112},... | collective-permute-start | bytes 245768 | tf_op jit(solution)/shard_map/ppermute | solution.py:643
  133.7 5.0 %all-to-all-done.5.frames = bf16[16,16,128]{2,1,0:T(8,128)(2,1)S(1)} async-done(((bf16[16,16,128]{2,1,0:T(8,128)(2,1)}), bf16[16,16,128]{2,1,0:T(8,128)(2,1)S(1)}, u32[]{:S(2)}, u32[]{:S(2)}) %all-to-all-start.5) | async-done | bytes 65568 | tf_op jit(solution)/shard_map/all_to_all | solution.py:675
  138.7 0.8 shard_map.153
  139.5 7.7 %all-to-all-start.6 = ((bf16[32,16,128]{2,1,0:T(8,128)(2,1)}), bf16[32,16,128]{2,1,0:T(8,128)(2,1)S(1)}, u32[]{:S(2)}, u32[]{:S(2)}) async-start(bf16[32,16,128]{2,1,0:T(8,128)(2,1)} %shard_map.153), calls=%async_computation.6 | async-start | bytes 262144 | tf_op jit(solution)/shard_map/all_to_all | solution.py:677
  147.2 0.0 collective-permute-done.3.above
  147.2 0.0 collective-permute-done.4.below
  147.2 0.0 copy-start.8
  147.2 1.1 copy-done.8
  148.3 5.0 %shard_map.150 = bf16[8,320,128]{2,1,0:T(8,128)(2,1)} custom-call(s32[1,1]{1,0:T(1,128)S(6)} %copy.16.live_ref, bf16[320,3072]{1,0:T(8,128)(2,1)S(1)} %get-tuple-element.38.weight, bf16[8,320,128]{2,1,0:T(8,128)(2,1)S(1)} %copy-done.8, bf16[1,320,128]{2,1,0:T(8,128)(2,1)S(1)} %collective-permute-done.3.above, ...), custom_call_target="tpu_custom_call" | custom-call | flops 14000000000 | bytes 29360128 | tf_op jit(solution)/shard_map/pallas_call | solution.py:628
  153.3 1.5 all-to-all-done.6.tiles
  154.8 1.4 shard_map.154
  (10 shorter events, 0.0 us)
Async XLA Ops:
  0.6 2.6 %copy-start = (bf16[1,1,8,128,320]{3,4,2,1,0:T(8,128)(2,1)S(1)}, bf16[1,1,8,128,320]{3,4,2,1,0:T(8,128)(2,1)}, u32[]{:S(2)}) copy-start(bf16[1,1,8,128,320]{3,4,2,1,0:T(8,128)(2,1)} %param.8) | copy-start | bytes 1966084
  1.4 1.0 copy-start.2
  3.2 21.4 %collective-permute-start = (bf16[1,320,128]{2,1,0:T(8,128)(2,1)S(1)}, bf16[1,320,128]{2,1,0:T(8,128)(2,1)S(1)}, u32[]{:S(2)}, u32[]{:S(2)}) collective-permute-start(bf16[1,320,128]{2,1,0:T(8,128)(2,1)S(1)} %get-tuple-element.31), channel_id=1, source_target_pairs={{0,16},{16,32},{32,48},{48,64},{64,80},{80,96},{96,112},{112,128},... | collective-permute-start | bytes 245768 | tf_op jit(solution)/shard_map/ppermute | solution.py:642
  7.7 16.9 %collective-permute-start.1 = (bf16[1,320,128]{2,1,0:T(8,128)(2,1)S(1)}, bf16[1,320,128]{2,1,0:T(8,128)(2,1)S(1)}, u32[]{:S(2)}, u32[]{:S(2)}) collective-permute-start(bf16[1,320,128]{2,1,0:T(8,128)(2,1)S(1)} %get-tuple-element.32), channel_id=1, source_target_pairs={{16,0},{32,16},{48,32},{64,48},{80,64},{96,80},{112,96},{128,112},... | collective-permute-start | bytes 245768 | tf_op jit(solution)/shard_map/ppermute | solution.py:643
  13.3 23.3 %all-to-all-start = ((bf16[16,16,128]{2,1,0:T(8,128)(2,1)}), bf16[16,16,128]{2,1,0:T(8,128)(2,1)S(1)}, u32[]{:S(2)}, u32[]{:S(2)}) async-start(bf16[16,16,128]{2,1,0:T(8,128)(2,1)} %shard_map.143.token), calls=%async_computation | async-start | bytes 131072 | tf_op jit(solution)/shard_map/all_to_all | solution.py:657
  26.5 2.6 %copy-start.6 = (bf16[3072,1024]{1,0:T(8,128)(2,1)}, bf16[3072,1024]{1,0:T(8,128)(2,1)S(1)}, u32[]{:S(2)}) copy-start(bf16[3072,1024]{1,0:T(8,128)(2,1)S(1)} %shard_map.145.patch) | copy-start | bytes 18874372
  55.6 25.1 %copy-start.9 = (f32[320]{0:T(512)S(1)}, f32[320]{0:T(512)}, u32[]{:S(2)}) copy-start(f32[320]{0:T(512)} %param.12) | copy-start | bytes 3844
  55.6 25.2 %copy-start.10 = (f32[320]{0:T(512)S(1)}, f32[320]{0:T(512)}, u32[]{:S(2)}) copy-start(f32[320]{0:T(512)} %param.13) | copy-start | bytes 3844
  55.6 25.3 %copy-start.1 = (bf16[1,1,8,128,320]{3,4,2,1,0:T(8,128)(2,1)S(1)}, bf16[1,1,8,128,320]{3,4,2,1,0:T(8,128)(2,1)}, u32[]{:S(2)}) copy-start(bf16[1,1,8,128,320]{3,4,2,1,0:T(8,128)(2,1)} %param.10) | copy-start | bytes 1966084
  55.6 8.6 %collective-permute-start.2 = (bf16[16,16,16,128]{3,2,1,0:T(8,128)(2,1)S(1)}, bf16[16,16,16,128]{3,2,1,0:T(8,128)(2,1)S(1)}, u32[]{:S(2)}, u32[]{:S(2)}) collective-permute-start(bf16[16,16,16,128]{3,2,1,0:T(8,128)(2,1)S(1)} %all_to_all.35.mine), channel_id=1, source_target_pairs={{0,16},{16,0},{1,17},{17,1},{2,18},{18,2},{3,19},{19,3},{4,20},{20... | collective-permute-start | bytes 3145736 | tf_op jit(solution)/shard_map/ppermute | solution.py:648
  99.2 22.7 %copy-start.7 = (bf16[8,320,128]{2,1,0:T(8,128)(2,1)}, bf16[8,320,128]{2,1,0:T(8,128)(2,1)S(1)}, u32[]{:S(2)}) copy-start(bf16[8,320,128]{2,1,0:T(8,128)(2,1)S(1)} %get-tuple-element.42.pre) | copy-start | bytes 1966084
  99.3 4.6 %collective-permute-start.5 = (bf16[16,16,16,128]{3,2,1,0:T(8,128)(2,1)S(1)}, bf16[16,16,16,128]{3,2,1,0:T(8,128)(2,1)S(1)}, u32[]{:S(2)}, u32[]{:S(2)}) collective-permute-start(bf16[16,16,16,128]{3,2,1,0:T(8,128)(2,1)S(1)} %get-tuple-element.46), channel_id=1, source_target_pairs={{0,16},{16,0},{1,17},{17,1},{2,18},{18,2},{3,19},{19,3},{4,20},{20... | collective-permute-start | bytes 3145736 | tf_op jit(solution)/shard_map/ppermute | solution.py:648
  122.8 16.0 %all-to-all-start.5 = ((bf16[16,16,128]{2,1,0:T(8,128)(2,1)}), bf16[16,16,128]{2,1,0:T(8,128)(2,1)S(1)}, u32[]{:S(2)}, u32[]{:S(2)}) async-start(bf16[16,16,128]{2,1,0:T(8,128)(2,1)} %shard_map.152), calls=%async_computation.5 | async-start | bytes 131072 | tf_op jit(solution)/shard_map/all_to_all | solution.py:675
  127.2 20.0 %collective-permute-start.3 = (bf16[1,320,128]{2,1,0:T(8,128)(2,1)S(1)}, bf16[1,320,128]{2,1,0:T(8,128)(2,1)S(1)}, u32[]{:S(2)}, u32[]{:S(2)}) collective-permute-start(bf16[1,320,128]{2,1,0:T(8,128)(2,1)S(1)} %get-tuple-element.43), channel_id=1, source_target_pairs={{0,16},{16,32},{32,48},{48,64},{64,80},{80,96},{96,112},{112,128},... | collective-permute-start | bytes 245768 | tf_op jit(solution)/shard_map/ppermute | solution.py:642
  131.8 15.4 %collective-permute-start.4 = (bf16[1,320,128]{2,1,0:T(8,128)(2,1)S(1)}, bf16[1,320,128]{2,1,0:T(8,128)(2,1)S(1)}, u32[]{:S(2)}, u32[]{:S(2)}) collective-permute-start(bf16[1,320,128]{2,1,0:T(8,128)(2,1)S(1)} %get-tuple-element.44), channel_id=1, source_target_pairs={{16,0},{32,16},{48,32},{64,48},{80,64},{96,80},{112,96},{128,112},... | collective-permute-start | bytes 245768 | tf_op jit(solution)/shard_map/ppermute | solution.py:643
  139.5 15.3 %all-to-all-start.6 = ((bf16[32,16,128]{2,1,0:T(8,128)(2,1)}), bf16[32,16,128]{2,1,0:T(8,128)(2,1)S(1)}, u32[]{:S(2)}, u32[]{:S(2)}) async-start(bf16[32,16,128]{2,1,0:T(8,128)(2,1)} %shard_map.153), calls=%async_computation.6 | async-start | bytes 262144 | tf_op jit(solution)/shard_map/all_to_all | solution.py:677
  147.2 1.1 copy-start.8
  148.3 6.5 %copy-start.3 = (f32[180,320]{1,0:T(8,128)S(1)}, f32[180,320]{1,0:T(8,128)}, u32[]{:S(2)}) copy-start(f32[180,320]{1,0:T(8,128)} %master.1) | copy-start | bytes 691204
  148.3 6.5 %copy-start.4 = (f32[180,320]{1,0:T(8,128)S(1)}, f32[180,320]{1,0:T(8,128)}, u32[]{:S(2)}) copy-start(f32[180,320]{1,0:T(8,128)} %first.1) | copy-start | bytes 691204
  148.3 6.5 %copy-start.5 = (f32[180,320]{1,0:T(8,128)S(1)}, f32[180,320]{1,0:T(8,128)}, u32[]{:S(2)}) copy-start(f32[180,320]{1,0:T(8,128)} %second.1) | copy-start | bytes 691204
